TPU v7x, 512 devices: a whole 4x8x8 slice. The times are simulated.
512 devices in a mesh: gx: 32 (over z_lo, y), gy: 16 (over x, z_hi, core).
Axes of the slice: x: 4, y: 8, z: 8 (z_hi: 2, z_lo: 4; z = z_hi * 4 + z_lo), core: 2. Of those that a mesh axis runs over, the one named last changes fastest.
Arguments:
- forward_pops: float32 [19, 256, 256, 128], P(None, 'gx', 'gy'), may hold values from 0.005 to 1, as said below
- later_adjoint: float32 [19, 256, 256, 128], P(None, 'gx', 'gy'), may hold values from -6 to 6
- design: float32 [256, 256, 128], P('gx', 'gy'), may hold values from 0 to 1
- node_type: int32 [256, 256, 128], P('gx', 'gy'), may hold values from 0 to 4, as said below
- region: int32 [256, 256, 128], P('gx', 'gy'), may hold values from 0 to 7
Outputs:
- adjoint: float32 [19, 256, 256, 128], P(None, 'gx', 'gy')
- sensitivity: float32 [256, 256, 128], P('gx', 'gy')
- objective: float32 [], replicated
- volumes: float32 [8], replicated
Inputs may be any that keep to these rules, and one draw needn't show every extreme that they name: `node_type`: 0 fluid, 1 design, 2 wall, 3 inlet, 4 outlet. `forward_pops`: positive populations.
All inputs are finite; a program needn't handle non-finite values.
Results may differ from a plain program's by a relative error of at most 0.00002.
Values sent between devices are 32-bit elements; how exact they have to be, the bound alone decides.
No kernel may reach another device: no remote copies, remote signals or barrier semaphores. Data moves between devices by JAX's collectives and lax.ppermute only.
A program may use at most 64 MiB of HBM per device.

v0:
```python
import math

import jax
import jax.numpy as jnp
from jax import lax
from jax.sharding import PartitionSpec as P

RAD = 3
REG = 8


VELOCITY = [
    (0, 0, 0),
    (1, 0, 0),
    (-1, 0, 0),
    (0, 1, 0),
    (0, -1, 0),
    (0, 0, 1),
    (0, 0, -1),
    (1, 1, 0),
    (-1, -1, 0),
    (1, -1, 0),
    (-1, 1, 0),
    (1, 0, 1),
    (-1, 0, -1),
    (1, 0, -1),
    (-1, 0, 1),
    (0, 1, 1),
    (0, -1, -1),
    (0, 1, -1),
    (0, -1, 1),
]
WEIGHTS = [1.0 / 3.0] + [1.0 / 18.0] * 6 + [1.0 / 36.0] * 12
OPPOSITE = [0, 2, 1, 4, 3, 6, 5, 8, 7, 10, 9, 12, 11, 14, 13, 16, 15, 18, 17]
RELAXATION = 1.0 / 0.6
BRINKMAN = 0.9


def padded_2(block, sides, width):
    for axis, dim in sides:
        count = lax.axis_size(axis)
        forward = [(i, i + 1) for i in range(count - 1)]
        forward.append((count - 1, 0))
        backward = [(target, source) for source, target in forward]
        low = lax.ppermute(
            lax.slice_in_dim(block, block.shape[dim] - width, None, axis=dim), axis, forward
        )
        high = lax.ppermute(lax.slice_in_dim(block, 0, width, axis=dim), axis, backward)
        block = jnp.concatenate([low, block, high], axis=dim)
    return block


def moments(populations):
    density = populations[0]
    for i in range(1, 19):
        density = density + populations[i]
    momenta = []
    for a in range(3):
        running = jnp.zeros_like(density)
        for i in range(19):
            if VELOCITY[i][a] == 1:
                running = running + populations[i]
            elif VELOCITY[i][a] == -1:
                running = running - populations[i]
        momenta.append(running)
    return (density, momenta)


def projections(velocity):
    result = []
    for i in range(19):
        running = jnp.zeros_like(velocity[0])
        for a in range(3):
            if VELOCITY[i][a] != 0:
                running = running + VELOCITY[i][a] * velocity[a]
        result.append(running)
    return result


def rates(kind):
    return jnp.where(kind <= 1, RELAXATION, 1.0)


def collide(populations, kind, factor):
    density, momenta = moments(populations)
    plain = [m / density for m in momenta]
    velocity = [factor * p for p in plain]
    speed_sq = velocity[0] * velocity[0] + velocity[1] * velocity[1] + velocity[2] * velocity[2]
    along = projections(velocity)
    omega_cell = rates(kind)
    wall = kind == 2
    output = []
    for i in range(19):
        balance = (
            WEIGHTS[i]
            * density
            * (1.0 + 3.0 * along[i] + 4.5 * along[i] * along[i] - 1.5 * speed_sq)
        )
        relaxed = (1.0 - omega_cell) * populations[i] + omega_cell * balance
        output.append(jnp.where(wall, populations[OPPOSITE[i]], relaxed))
    return jnp.stack(output)


def adjoint_collide(incoming, populations, kind, factor):
    density, momenta = moments(populations)
    plain = [m / density for m in momenta]
    velocity = [factor * p for p in plain]
    speed_sq = velocity[0] * velocity[0] + velocity[1] * velocity[1] + velocity[2] * velocity[2]
    along = projections(velocity)
    omega_cell = rates(kind)
    wall = kind == 2
    scalar_part = jnp.zeros_like(density)
    vector_part = [jnp.zeros_like(density), jnp.zeros_like(density), jnp.zeros_like(density)]
    for j in range(19):
        weighted = WEIGHTS[j] * incoming[j]
        scalar_part = scalar_part + weighted * (
            1.0 + 3.0 * along[j] + 4.5 * along[j] * along[j] - 1.5 * speed_sq
        )
        for a in range(3):
            vector_part[a] = vector_part[a] + weighted * (
                3.0 * VELOCITY[j][a] + 9.0 * along[j] * VELOCITY[j][a] - 3.0 * velocity[a]
            )
    output = []
    for i in range(19):
        coupling = scalar_part
        for a in range(3):
            coupling = coupling + vector_part[a] * (factor * VELOCITY[i][a] - velocity[a])
        relaxed = (1.0 - omega_cell) * incoming[i] + omega_cell * coupling
        output.append(jnp.where(wall, incoming[OPPOSITE[i]], relaxed))
    inner = vector_part[0] * plain[0] + vector_part[1] * plain[1] + vector_part[2] * plain[2]
    gradient = jnp.where(wall, 0.0, omega_cell * density * inner)
    return (jnp.stack(output), gradient)


def displace(extended, sign):
    padded = jnp.pad(extended, ((0, 0), (0, 0), (0, 0), (1, 1)))
    span_x = extended.shape[1] - 2
    span_y = extended.shape[2] - 2
    span_z = extended.shape[3]
    pieces = []
    for i in range(19):
        off_x = 1 + sign * VELOCITY[i][0]
        off_y = 1 + sign * VELOCITY[i][1]
        off_z = 1 + sign * VELOCITY[i][2]
        pieces.append(
            padded[i, off_x : off_x + span_x, off_y : off_y + span_y, off_z : off_z + span_z]
        )
    return jnp.stack(pieces)


def filter_taps(padded):
    span_x = padded.shape[0] - 2 * RAD
    span_y = padded.shape[1] - 2 * RAD
    span_z = padded.shape[2] - 2 * RAD
    running = jnp.zeros((span_x, span_y, span_z), jnp.float32)
    for a in range(-RAD, RAD + 1):
        for b in range(-RAD, RAD + 1):
            for c in range(-RAD, RAD + 1):
                weight = RAD + 1 - math.sqrt(a * a + b * b + c * c)
                if weight > 0:
                    running = (
                        running
                        + weight
                        * padded[
                            RAD + a : RAD + a + span_x,
                            RAD + b : RAD + b + span_y,
                            RAD + c : RAD + c + span_z,
                        ]
                    )
    return running


def filter_norm(depth):
    block = jnp.pad(
        jnp.ones((2 * RAD + 1, 2 * RAD + 1, depth), jnp.float32), ((0, 0), (0, 0), (RAD, RAD))
    )
    return filter_taps(block)


def filter_block(field):
    extended = padded_2(field, (("gx", 0), ("gy", 1)), RAD)
    return filter_taps(jnp.pad(extended, ((0, 0), (0, 0), (RAD, RAD))))


def lattice_rim(populations):
    return padded_2(populations, (("gx", 1), ("gy", 2)), 1)


def outlet_source(kind):
    source = jnp.where(kind == 4, 1.0, 0.0)
    return jnp.stack([VELOCITY[i][0] * source for i in range(19)])


def per_device(forward_pops, later_adjoint, design, node_type, region):
    norm_field = filter_norm(design.shape[2])
    filtered = filter_block(design) / norm_field
    factor = jnp.where(node_type == 1, 1.0 - BRINKMAN * (1.0 - filtered), 1.0)
    volume_local = jnp.stack(
        [jnp.sum(jnp.where((node_type == 1) & (region == r), filtered, 0.0)) for r in range(REG)]
    )
    post = collide(forward_pops, node_type, factor)
    both = lattice_rim(jnp.concatenate([post, later_adjoint], axis=0))
    next_pops = displace(both[:19], -1)
    incoming = displace(both[19:], 1)
    middle, first_grad = adjoint_collide(incoming, next_pops, node_type, factor)
    middle = middle + outlet_source(node_type)
    incoming = displace(lattice_rim(middle), 1)
    adjoint, second_grad = adjoint_collide(incoming, forward_pops, node_type, factor)
    density, momenta = moments(next_pops)
    objective_local = jnp.sum(jnp.where(node_type == 4, momenta[0], 0.0))
    objective, volumes = lax.psum((objective_local, volume_local), ("gx", "gy"))
    raw = jnp.where(node_type == 1, BRINKMAN * (first_grad + second_grad), 0.0) / norm_field
    sensitivity = filter_block(raw)
    return (adjoint, sensitivity, objective, volumes)


def solution(mesh):
    in_specs = (
        P(None, "gx", "gy", None),
        P(None, "gx", "gy", None),
        P("gx", "gy", None),
        P("gx", "gy", None),
        P("gx", "gy", None),
    )
    out_specs = (P(None, "gx", "gy", None), P("gx", "gy", None), P(), P())
    return jax.shard_map(
        per_device, mesh=mesh, in_specs=in_specs, out_specs=out_specs, check_vma=False
    )
```

profile of v0, /device:TPU:1, one launch (start us, length us, event | category | flops | bytes accessed | tf_op | source)
XLA Modules:
  0.0 247.7 jit_solution(16159938050270594559)
XLA Ops:
  1.4 4.0 %collective-permute-start = (f32[3,16,128]{2,1,0:T(8,128)S(1)}, f32[3,16,128]{2,1,0:T(8,128)S(1)}, u32[]{:S(2)}, u32[]{:S(2)}) collective-permute-start(f32[3,16,128]{2,1,0:T(8,128)S(1)} %get-tuple-element.162), channel_id=1, source_target_pairs={{0,16},{16,32},{32,48},{48,64},{64,80},{80,96},{96,112},{112,128},... | collective-permute-start | bytes 73736 | tf_op jit(solution)/shard_map/ppermute | solution.py:45
  5.4 9.2 %collective-permute-start.1 = (f32[3,16,128]{2,1,0:T(8,128)S(1)}, f32[3,16,128]{2,1,0:T(8,128)S(1)}, u32[]{:S(2)}, u32[]{:S(2)}) collective-permute-start(f32[3,16,128]{2,1,0:T(8,128)S(1)} %get-tuple-element.161), channel_id=1, source_target_pairs={{16,0},{32,16},{48,32},{64,48},{80,64},{96,80},{112,96},{128,112},... | collective-permute-start | bytes 73736 | tf_op jit(solution)/shard_map/ppermute | solution.py:48
  15.6 9.4 %collective-permute-start.2 = (f32[14,3,128]{2,1,0:T(4,128)S(1)}, f32[14,3,128]{2,1,0:T(4,128)S(1)}, u32[]{:S(2)}, u32[]{:S(2)}) collective-permute-start(f32[14,3,128]{2,1,0:T(4,128)S(1)} %get-tuple-element.153), channel_id=1, source_target_pairs={{0,1},{1,2},{2,3},{3,4},{4,5},{5,6},{6,7},{7,8},{8,9},{9,10},{10,1... | collective-permute-start | bytes 64520 | tf_op jit(solution)/shard_map/ppermute | solution.py:45
  25.0 1.9 collective-permute-start.3
  27.3 6.8 %collective-permute-done.3 = f32[14,3,128]{2,1,0:T(4,128)S(1)} collective-permute-done((f32[14,3,128]{2,1,0:T(4,128)S(1)}, f32[14,3,128]{2,1,0:T(4,128)S(1)}, u32[]{:S(2)}, u32[]{:S(2)}) %collective-permute-start.3) | collective-permute-done | bytes 21536 | tf_op jit(solution)/shard_map/ppermute | solution.py:48
  35.0 3.1 %fusion.254 = f32[8,16,128]{2,1,0:T(8,128)S(1)} fusion(f32[8,16,128]{2,1,0:T(8,128)S(1)} %div.35, f32[8,16,128]{2,1,0:T(8,128)S(1)} %broadcast.809, f32[14,16,128]{2,1,0:T(8,128)S(1)} %get-tuple-element.166, f32[14,3,128]{2,1,0:T(4,128)S(1)} %collective-permute-done.3, f32[8,16,128]{2,1,0:T(8,128)S(1)} %broadcast.806, ...), kind=kLoop, calls=%fused_computation.554 | loop fusion | flops 7995392 | bytes 15034368 | tf_op jit(solution)/shard_map/div | solution.py:196
  42.0 1.9 collective-permute-start.4
  43.9 7.8 %collective-permute-start.5 = (f32[38,1,16,128]{3,2,1,0:T(8,128)S(1)}, f32[38,1,16,128]{3,2,1,0:T(8,128)S(1)}, u32[]{:S(2)}, u32[]{:S(2)}) collective-permute-start(f32[38,1,16,128]{3,2,1,0:T(8,128)S(1)} %get-tuple-element.108), channel_id=1, source_target_pairs={{16,0},{32,16},{48,32},{64,48},{80,64},{96,80},{112,96},{128,112},... | collective-permute-start | bytes 933896 | tf_op jit(solution)/shard_map/ppermute | solution.py:48
  51.7 4.5 %collective-permute-done.4 = f32[38,1,16,128]{3,2,1,0:T(8,128)S(1)} collective-permute-done((f32[38,1,16,128]{3,2,1,0:T(8,128)S(1)}, f32[38,1,16,128]{3,2,1,0:T(8,128)S(1)}, u32[]{:S(2)}, u32[]{:S(2)}) %collective-permute-start.4) | collective-permute-done | bytes 311328 | tf_op jit(solution)/shard_map/ppermute | solution.py:45
  58.2 3.2 %collective-permute-start.6 = (f32[38,10,1,128]{3,2,1,0:T(1,128)S(1)}, f32[38,10,1,128]{3,2,1,0:T(1,128)S(1)}, u32[]{:S(2)}, u32[]{:S(2)}) collective-permute-start(f32[38,10,1,128]{3,2,1,0:T(1,128)S(1)} %get-tuple-element.105), channel_id=1, source_target_pairs={{0,1},{1,2},{2,3},{3,4},{4,5},{5,6},{6,7},{7,8},{8,9},{9,10},{10,1... | collective-permute-start | bytes 583688 | tf_op jit(solution)/shard_map/ppermute | solution.py:45
  61.4 1.9 collective-permute-start.7
  64.0 9.7 %collective-permute-done.7 = f32[38,10,1,128]{3,2,1,0:T(1,128)S(1)} collective-permute-done((f32[38,10,1,128]{3,2,1,0:T(1,128)S(1)}, f32[38,10,1,128]{3,2,1,0:T(1,128)S(1)}, u32[]{:S(2)}, u32[]{:S(2)}) %collective-permute-start.7) | collective-permute-done | bytes 194592 | tf_op jit(solution)/shard_map/ppermute | solution.py:48
  79.6 8.1 %collective-permute-start.8 = (f32[19,1,16,128]{3,2,1,0:T(8,128)S(1)}, f32[19,1,16,128]{3,2,1,0:T(8,128)S(1)}, u32[]{:S(2)}, u32[]{:S(2)}) collective-permute-start(f32[19,1,16,128]{3,2,1,0:T(8,128)S(1)} %get-tuple-element.112), channel_id=1, source_target_pairs={{16,0},{32,16},{48,32},{64,48},{80,64},{96,80},{112,96},{128,112},... | collective-permute-start | bytes 466952 | tf_op jit(solution)/shard_map/ppermute | solution.py:48
  87.7 1.9 collective-permute-start.9
  91.0 7.7 %collective-permute-done.9 = f32[19,1,16,128]{3,2,1,0:T(8,128)S(1)} collective-permute-done((f32[19,1,16,128]{3,2,1,0:T(8,128)S(1)}, f32[19,1,16,128]{3,2,1,0:T(8,128)S(1)}, u32[]{:S(2)}, u32[]{:S(2)}) %collective-permute-start.9) | collective-permute-done | bytes 155680 | tf_op jit(solution)/shard_map/ppermute | solution.py:45
  99.6 3.2 %collective-permute-start.10 = (f32[19,10,1,128]{3,2,1,0:T(1,128)}, f32[19,10,1,128]{3,2,1,0:T(1,128)S(1)}, u32[]{:S(2)}, u32[]{:S(2)}) collective-permute-start(f32[19,10,1,128]{3,2,1,0:T(1,128)} %get-tuple-element.110), channel_id=1, source_target_pairs={{1,0},{2,1},{3,2},{4,3},{5,4},{6,5},{7,6},{8,7},{9,8},{10,9},{11,1... | collective-permute-start | bytes 291848 | tf_op jit(solution)/shard_map/ppermute | solution.py:48
  102.8 6.3 %collective-permute-start.11 = (f32[19,10,1,128]{3,2,1,0:T(1,128)}, f32[19,10,1,128]{3,2,1,0:T(1,128)S(1)}, u32[]{:S(2)}, u32[]{:S(2)}) collective-permute-start(f32[19,10,1,128]{3,2,1,0:T(1,128)} %get-tuple-element.109), channel_id=1, source_target_pairs={{0,1},{1,2},{2,3},{3,4},{4,5},{5,6},{6,7},{7,8},{8,9},{9,10},{10,1... | collective-permute-start | bytes 291848 | tf_op jit(solution)/shard_map/ppermute | solution.py:45
  109.0 5.7 %stack.303 = f32[8]{0:T(128)} concatenate(f32[1]{0:T(128)} %bitcast.135, f32[1]{0:T(128)} %bitcast.136, f32[1]{0:T(128)} %bitcast.137, f32[1]{0:T(128)} %bitcast.138, f32[1]{0:T(128)} %bitcast.139, f32[1]{0:T(128)} %bitcast.140, f32[1]{0:T(128)} %bitcast.141, f32[1]{0:T(128)} %bitcast.142), dimensions={0} | concatenate | bytes 64 | tf_op jit(solution)/shard_map/stack | solution.py:198
  114.7 96.7 %all-reduce.6 = (f32[]{:T(128)}, f32[8]{0:T(128)}) all-reduce(f32[]{:T(128)} %get-tuple-element.15, f32[8]{0:T(128)} %stack.303), channel_id=1, replica_groups=mesh['gx'=32,'gy'=16] {'gx','gy'}, use_global_device_ids=true, to_apply=%region_1.2 | all-reduce | flops 9 | bytes 72 | tf_op jit(solution)/shard_map/psum | solution.py:211
  211.5 4.3 %select_maximum_fusion = f32[19,10,18,130]{3,2,1,0:T(8,128)S(1)} fusion(f32[19,10,1,128]{3,2,1,0:T(1,128)S(1)} %collective-permute-done.10, f32[19,10,1,128]{3,2,1,0:T(1,128)S(1)} %collective-permute-done.11, f32[19,1,16,128]{3,2,1,0:T(8,128)S(1)} %collective-permute-done.8, f32[19,8,16,128]{3,2,1,0:T(8,128)S(1)} %add.4920, ...), kind=kLoop, calls=%fused_computation.22 | loop fusion | flops 5335200 | bytes 3529440 | tf_op jit(solution)/shard_map/concatenate | solution.py:49
  218.8 7.3 %collective-permute-start.13 = (f32[3,16,128]{2,1,0:T(8,128)S(1)}, f32[3,16,128]{2,1,0:T(8,128)S(1)}, u32[]{:S(2)}, u32[]{:S(2)}) collective-permute-start(f32[3,16,128]{2,1,0:T(8,128)S(1)} %get-tuple-element.156), channel_id=1, source_target_pairs={{16,0},{32,16},{48,32},{64,48},{80,64},{96,80},{112,96},{128,112},... | collective-permute-start | bytes 73736 | tf_op jit(solution)/shard_map/ppermute | solution.py:48
  227.8 6.3 %collective-permute-start.14 = (f32[14,3,128]{2,1,0:T(4,128)S(1)}, f32[14,3,128]{2,1,0:T(4,128)S(1)}, u32[]{:S(2)}, u32[]{:S(2)}) collective-permute-start(f32[14,3,128]{2,1,0:T(4,128)S(1)} %get-tuple-element.151), channel_id=1, source_target_pairs={{0,1},{1,2},{2,3},{3,4},{4,5},{5,6},{6,7},{7,8},{8,9},{9,10},{10,1... | collective-permute-start | bytes 64520 | tf_op jit(solution)/shard_map/ppermute | solution.py:45
  236.2 7.0 %collective-permute-done.15 = f32[14,3,128]{2,1,0:T(4,128)S(1)} collective-permute-done((f32[14,3,128]{2,1,0:T(4,128)S(1)}, f32[14,3,128]{2,1,0:T(4,128)S(1)}, u32[]{:S(2)}, u32[]{:S(2)}) %collective-permute-start.15) | collective-permute-done | bytes 21536 | tf_op jit(solution)/shard_map/ppermute | solution.py:48
  244.4 3.3 %fusion.735 = f32[8,16,128]{2,1,0:T(8,128)} fusion(f32[8,16,128]{2,1,0:T(8,128)S(1)} %broadcast.806, f32[14,22,134]{2,1,0:T(8,128)S(1)} %select_maximum_fusion.4, f32[8,16,128]{2,1,0:T(8,128)S(1)} %broadcast.807, f32[14,19,128]{2,1,0:T(8,128)S(1)} %get-tuple-element.150, f32[8,16,128]{2,1,0:T(8,128)S(1)} %broadcast.808, f32[8,16,128]{2,1,0:T(8,128)S(1)} %broadcast.809, ...), kind=kLoop, calls=%fused_computation.1036 | loop fusion | flops 6438912 | bytes 14598144 | tf_op jit(solution)/shard_map/add | solution.py:162
  (151 shorter events, 24.8 us)
Async XLA Ops:
  1.4 13.3 %collective-permute-start = (f32[3,16,128]{2,1,0:T(8,128)S(1)}, f32[3,16,128]{2,1,0:T(8,128)S(1)}, u32[]{:S(2)}, u32[]{:S(2)}) collective-permute-start(f32[3,16,128]{2,1,0:T(8,128)S(1)} %get-tuple-element.162), channel_id=1, source_target_pairs={{0,16},{16,32},{32,48},{48,64},{64,80},{80,96},{96,112},{112,128},... | collective-permute-start | bytes 73736 | tf_op jit(solution)/shard_map/ppermute | solution.py:45
  5.4 10.2 %collective-permute-start.1 = (f32[3,16,128]{2,1,0:T(8,128)S(1)}, f32[3,16,128]{2,1,0:T(8,128)S(1)}, u32[]{:S(2)}, u32[]{:S(2)}) collective-permute-start(f32[3,16,128]{2,1,0:T(8,128)S(1)} %get-tuple-element.161), channel_id=1, source_target_pairs={{16,0},{32,16},{48,32},{64,48},{80,64},{96,80},{112,96},{128,112},... | collective-permute-start | bytes 73736 | tf_op jit(solution)/shard_map/ppermute | solution.py:48
  15.6 11.7 %collective-permute-start.2 = (f32[14,3,128]{2,1,0:T(4,128)S(1)}, f32[14,3,128]{2,1,0:T(4,128)S(1)}, u32[]{:S(2)}, u32[]{:S(2)}) collective-permute-start(f32[14,3,128]{2,1,0:T(4,128)S(1)} %get-tuple-element.153), channel_id=1, source_target_pairs={{0,1},{1,2},{2,3},{3,4},{4,5},{5,6},{6,7},{7,8},{8,9},{9,10},{10,1... | collective-permute-start | bytes 64520 | tf_op jit(solution)/shard_map/ppermute | solution.py:45
  25.0 9.1 %collective-permute-start.3 = (f32[14,3,128]{2,1,0:T(4,128)S(1)}, f32[14,3,128]{2,1,0:T(4,128)S(1)}, u32[]{:S(2)}, u32[]{:S(2)}) collective-permute-start(f32[14,3,128]{2,1,0:T(4,128)S(1)} %get-tuple-element.154), channel_id=1, source_target_pairs={{1,0},{2,1},{3,2},{4,3},{5,4},{6,5},{7,6},{8,7},{9,8},{10,9},{11,1... | collective-permute-start | bytes 64520 | tf_op jit(solution)/shard_map/ppermute | solution.py:48
  27.3 7.6 %copy-start.8 = (f32[128]{0:T(128)}, f32[128]{0:T(128)S(1)}, u32[]{:S(2)}) copy-start(f32[128]{0:T(128)S(1)} %add_add_fusion.1) | copy-start | bytes 1540
  35.0 3.1 %copy-start.2 = (s32[8,16,128]{2,1,0:T(8,128)S(1)}, s32[8,16,128]{2,1,0:T(8,128)}, u32[]{:S(2)}) copy-start(s32[8,16,128]{2,1,0:T(8,128)} %param.8) | copy-start | bytes 196612
  35.0 3.1 %copy-start.6 = (s32[8,16,128]{2,1,0:T(8,128)S(1)}, s32[8,16,128]{2,1,0:T(8,128)}, u32[]{:S(2)}) copy-start(s32[8,16,128]{2,1,0:T(8,128)} %param.9) | copy-start | bytes 196612
  35.0 3.9 %copy-start = (f32[19,8,16,128]{3,2,1,0:T(8,128)S(1)}, f32[19,8,16,128]{3,2,1,0:T(8,128)}, u32[]{:S(2)}) copy-start(f32[19,8,16,128]{3,2,1,0:T(8,128)} %param.5) | copy-start | bytes 3735556
  42.0 14.2 %collective-permute-start.4 = (f32[38,1,16,128]{3,2,1,0:T(8,128)S(1)}, f32[38,1,16,128]{3,2,1,0:T(8,128)S(1)}, u32[]{:S(2)}, u32[]{:S(2)}) collective-permute-start(f32[38,1,16,128]{3,2,1,0:T(8,128)S(1)} %get-tuple-element.107), channel_id=1, source_target_pairs={{0,16},{16,32},{32,48},{48,64},{64,80},{80,96},{96,112},{112,128},... | collective-permute-start | bytes 933896 | tf_op jit(solution)/shard_map/ppermute | solution.py:45
  43.9 14.1 %collective-permute-start.5 = (f32[38,1,16,128]{3,2,1,0:T(8,128)S(1)}, f32[38,1,16,128]{3,2,1,0:T(8,128)S(1)}, u32[]{:S(2)}, u32[]{:S(2)}) collective-permute-start(f32[38,1,16,128]{3,2,1,0:T(8,128)S(1)} %get-tuple-element.108), channel_id=1, source_target_pairs={{16,0},{32,16},{48,32},{64,48},{80,64},{96,80},{112,96},{128,112},... | collective-permute-start | bytes 933896 | tf_op jit(solution)/shard_map/ppermute | solution.py:48
  58.2 5.8 %collective-permute-start.6 = (f32[38,10,1,128]{3,2,1,0:T(1,128)S(1)}, f32[38,10,1,128]{3,2,1,0:T(1,128)S(1)}, u32[]{:S(2)}, u32[]{:S(2)}) collective-permute-start(f32[38,10,1,128]{3,2,1,0:T(1,128)S(1)} %get-tuple-element.105), channel_id=1, source_target_pairs={{0,1},{1,2},{2,3},{3,4},{4,5},{5,6},{6,7},{7,8},{8,9},{9,10},{10,1... | collective-permute-start | bytes 583688 | tf_op jit(solution)/shard_map/ppermute | solution.py:45
  61.4 12.3 %collective-permute-start.7 = (f32[38,10,1,128]{3,2,1,0:T(1,128)S(1)}, f32[38,10,1,128]{3,2,1,0:T(1,128)S(1)}, u32[]{:S(2)}, u32[]{:S(2)}) collective-permute-start(f32[38,10,1,128]{3,2,1,0:T(1,128)S(1)} %get-tuple-element.106), channel_id=1, source_target_pairs={{1,0},{2,1},{3,2},{4,3},{5,4},{6,5},{7,6},{8,7},{9,8},{10,9},{11,1... | collective-permute-start | bytes 583688 | tf_op jit(solution)/shard_map/ppermute | solution.py:48
  79.6 11.5 %collective-permute-start.8 = (f32[19,1,16,128]{3,2,1,0:T(8,128)S(1)}, f32[19,1,16,128]{3,2,1,0:T(8,128)S(1)}, u32[]{:S(2)}, u32[]{:S(2)}) collective-permute-start(f32[19,1,16,128]{3,2,1,0:T(8,128)S(1)} %get-tuple-element.112), channel_id=1, source_target_pairs={{16,0},{32,16},{48,32},{64,48},{80,64},{96,80},{112,96},{128,112},... | collective-permute-start | bytes 466952 | tf_op jit(solution)/shard_map/ppermute | solution.py:48
  87.7 11.1 %collective-permute-start.9 = (f32[19,1,16,128]{3,2,1,0:T(8,128)S(1)}, f32[19,1,16,128]{3,2,1,0:T(8,128)S(1)}, u32[]{:S(2)}, u32[]{:S(2)}) collective-permute-start(f32[19,1,16,128]{3,2,1,0:T(8,128)S(1)} %get-tuple-element.111), channel_id=1, source_target_pairs={{0,16},{16,32},{32,48},{48,64},{64,80},{80,96},{96,112},{112,128},... | collective-permute-start | bytes 466952 | tf_op jit(solution)/shard_map/ppermute | solution.py:45
  99.6 111.9 %collective-permute-start.10 = (f32[19,10,1,128]{3,2,1,0:T(1,128)}, f32[19,10,1,128]{3,2,1,0:T(1,128)S(1)}, u32[]{:S(2)}, u32[]{:S(2)}) collective-permute-start(f32[19,10,1,128]{3,2,1,0:T(1,128)} %get-tuple-element.110), channel_id=1, source_target_pairs={{1,0},{2,1},{3,2},{4,3},{5,4},{6,5},{7,6},{8,7},{9,8},{10,9},{11,1... | collective-permute-start | bytes 291848 | tf_op jit(solution)/shard_map/ppermute | solution.py:48
  102.8 108.7 %collective-permute-start.11 = (f32[19,10,1,128]{3,2,1,0:T(1,128)}, f32[19,10,1,128]{3,2,1,0:T(1,128)S(1)}, u32[]{:S(2)}, u32[]{:S(2)}) collective-permute-start(f32[19,10,1,128]{3,2,1,0:T(1,128)} %get-tuple-element.109), channel_id=1, source_target_pairs={{0,1},{1,2},{2,3},{3,4},{4,5},{5,6},{6,7},{7,8},{8,9},{9,10},{10,1... | collective-permute-start | bytes 291848 | tf_op jit(solution)/shard_map/ppermute | solution.py:45
  211.5 4.3 %copy-start.3 = (f32[8,16,128]{2,1,0:T(8,128)S(1)}, f32[8,16,128]{2,1,0:T(8,128)}, u32[]{:S(2)}) copy-start(f32[8,16,128]{2,1,0:T(8,128)} %get-tuple-element.96) | copy-start | bytes 196612
  211.5 4.3 %copy-start.5 = (pred[8,16,128]{2,1,0:T(8,128)(4,1)S(1)}, pred[8,16,128]{2,1,0:T(8,128)(4,1)}, u32[]{:S(2)}) copy-start(pred[8,16,128]{2,1,0:T(8,128)(4,1)} %copy-done.4) | copy-start | bytes 49156
  211.5 4.3 %copy-start.9 = (f32[128]{0:T(128)S(1)}, f32[128]{0:T(128)}, u32[]{:S(2)}) copy-start(f32[128]{0:T(128)} %copy-done.8) | copy-start | bytes 1540
  216.8 11.0 %collective-permute-start.12 = (f32[3,16,128]{2,1,0:T(8,128)S(1)}, f32[3,16,128]{2,1,0:T(8,128)S(1)}, u32[]{:S(2)}, u32[]{:S(2)}) collective-permute-start(f32[3,16,128]{2,1,0:T(8,128)S(1)} %get-tuple-element.155), channel_id=1, source_target_pairs={{0,16},{16,32},{32,48},{48,64},{64,80},{80,96},{96,112},{112,128},... | collective-permute-start | bytes 73736 | tf_op jit(solution)/shard_map/ppermute | solution.py:45
  218.8 9.0 %collective-permute-start.13 = (f32[3,16,128]{2,1,0:T(8,128)S(1)}, f32[3,16,128]{2,1,0:T(8,128)S(1)}, u32[]{:S(2)}, u32[]{:S(2)}) collective-permute-start(f32[3,16,128]{2,1,0:T(8,128)S(1)} %get-tuple-element.156), channel_id=1, source_target_pairs={{16,0},{32,16},{48,32},{64,48},{80,64},{96,80},{112,96},{128,112},... | collective-permute-start | bytes 73736 | tf_op jit(solution)/shard_map/ppermute | solution.py:48
  227.8 8.4 %collective-permute-start.14 = (f32[14,3,128]{2,1,0:T(4,128)S(1)}, f32[14,3,128]{2,1,0:T(4,128)S(1)}, u32[]{:S(2)}, u32[]{:S(2)}) collective-permute-start(f32[14,3,128]{2,1,0:T(4,128)S(1)} %get-tuple-element.151), channel_id=1, source_target_pairs={{0,1},{1,2},{2,3},{3,4},{4,5},{5,6},{6,7},{7,8},{8,9},{9,10},{10,1... | collective-permute-start | bytes 64520 | tf_op jit(solution)/shard_map/ppermute | solution.py:45
  234.2 9.1 %collective-permute-start.15 = (f32[14,3,128]{2,1,0:T(4,128)S(1)}, f32[14,3,128]{2,1,0:T(4,128)S(1)}, u32[]{:S(2)}, u32[]{:S(2)}) collective-permute-start(f32[14,3,128]{2,1,0:T(4,128)S(1)} %get-tuple-element.152), channel_id=1, source_target_pairs={{1,0},{2,1},{3,2},{4,3},{5,4},{6,5},{7,6},{8,7},{9,8},{10,9},{11,1... | collective-permute-start | bytes 64520 | tf_op jit(solution)/shard_map/ppermute | solution.py:48
  236.2 7.6 %copy-start.7 = (f32[19,8,16,128]{3,2,1,0:T(8,128)}, f32[19,8,16,128]{3,2,1,0:T(8,128)S(1)}, u32[]{:S(2)}) copy-start(f32[19,8,16,128]{3,2,1,0:T(8,128)S(1)} %constant_dynamic-update-slice_fusion.65) | copy-start | bytes 3735556
  (2 other events, 2.2 us)
where the time goes:
time: 248 us
  blocking collectives  96.7 us (39%)
  starting transfers between devices  76.4 us (31%)
  waiting for transfers between devices  39.6 us (16%)
  other arithmetic  25.4 us (10%)
  local copies, waits for them, and re-layouts  8.11 us (3%)
    psum x1, blocking collectives, per_device(): objective, volumes = lax.psum((objective_local, volume_local), ('gx', 'gy'))  96.7 us
    ppermute x8, starting transfers between devices, padded_2(): lax.ppermute(lax.slice_in_dim(block, 0, width, axis=dim), axis, backward)  41.4 us
    ppermute x8, starting transfers between devices, padded_2(): lax.ppermute(lax.slice_in_dim(block, block.shape[dim] - width, None, axis...  34.9 us
    ppermute x8, waiting for transfers between devices, padded_2(): lax.ppermute(lax.slice_in_dim(block, 0, width, axis=dim), axis, backward)  26.8 us
    ppermute x8, waiting for transfers between devices, padded_2(): lax.ppermute(lax.slice_in_dim(block, block.shape[dim] - width, None, axis...  12.8 us
    concatenate x7, other arithmetic, padded_2(): block = jnp.concatenate([low, block, high], axis=dim)  7.36 us
    unnamed x73, other arithmetic  6.69 us
    another operation x1, local copies, waits for them, and re-layouts, per_device(): jnp.stack([jnp.sum(jnp.where((node_type == 1) & (region == r), filtered,...  5.7 us
  transfers between devices with their start and end apart: 16, of which 8 were waited for; matrix products, arithmetic and copies ran while one was open for 4% of the time, Pallas kernels for 0%

commit v1 on v0

v1 whole, which is shorter than its diff:
```python
import math

import jax
import jax.numpy as jnp
from jax import lax
from jax.experimental import pallas as pl
from jax.experimental.pallas import tpu as pltpu
from jax.sharding import PartitionSpec as P

RAD = 3
REG = 8
VELOCITY = [
    (0, 0, 0),
    (1, 0, 0),
    (-1, 0, 0),
    (0, 1, 0),
    (0, -1, 0),
    (0, 0, 1),
    (0, 0, -1),
    (1, 1, 0),
    (-1, -1, 0),
    (1, -1, 0),
    (-1, 1, 0),
    (1, 0, 1),
    (-1, 0, -1),
    (1, 0, -1),
    (-1, 0, 1),
    (0, 1, 1),
    (0, -1, -1),
    (0, 1, -1),
    (0, -1, 1),
]
WEIGHTS = [1.0 / 3.0] + [1.0 / 18.0] * 6 + [1.0 / 36.0] * 12
OPPOSITE = [0, 2, 1, 4, 3, 6, 5, 8, 7, 10, 9, 12, 11, 14, 13, 16, 15, 18, 17]
RELAXATION = 1.0 / 0.6
BRINKMAN = 0.9
Q = 19
BX = 8
BY = 16
NZ = 128
F32 = jnp.float32

XP = tuple(i for i in range(Q) if VELOCITY[i][0] == 1)
XM = tuple(i for i in range(Q) if VELOCITY[i][0] == -1)
YP = tuple(i for i in range(Q) if VELOCITY[i][1] == 1)
YM = tuple(i for i in range(Q) if VELOCITY[i][1] == -1)

NODE, DENS, FWD, ADJ, MSG = 4, 5, 9, 14, 19

CLASSES = sorted(
    {a * a + b * b for a in range(RAD + 1) for b in range(RAD + 1) if a * a + b * b < (RAD + 1) ** 2}
)
TAPS = {
    s: [
        (a, b)
        for a in range(-RAD, RAD + 1)
        for b in range(-RAD, RAD + 1)
        if a * a + b * b == s
    ]
    for s in CLASSES
}


def tap_weight(s, c):
    return RAD + 1 - math.sqrt(s + c * c)


def lanes(shape):
    return lax.broadcasted_iota(jnp.int32, shape, len(shape) - 1)


def shift_z(value, c):
    if c == 0:
        return value
    z = lanes(value.shape)
    moved = pltpu.roll(value, (-c) % NZ, value.ndim - 1)
    return jnp.where((z + c >= 0) & (z + c < NZ), moved, 0.0)


def norm_row(shape):
    z = lanes(shape)
    result = None
    for c in range(RAD + 1):
        total = sum(len(TAPS[s]) * tap_weight(s, c) for s in CLASSES if tap_weight(s, c) > 0)
        if c == 0:
            result = jnp.full(shape, total, F32)
        else:
            result = result + jnp.where(z >= c, total, 0.0) + jnp.where(z < NZ - c, total, 0.0)
    return result


def filter_rows(load):
    sums = []
    for s in CLASSES:
        running = None
        for a, b in TAPS[s]:
            tile = load(a, b)
            running = tile if running is None else running + tile
        sums.append(running)
    result = None
    for c in range(RAD + 1):
        mixed = None
        for s, part in zip(CLASSES, sums):
            if tap_weight(s, c) > 0:
                term = tap_weight(s, c) * part
                mixed = term if mixed is None else mixed + term
        if c == 0:
            result = mixed
        else:
            result = result + shift_z(mixed, c) + shift_z(mixed, -c)
    return result


def add_all(values):
    values = list(values)
    while len(values) > 1:
        values = [
            values[k] + values[k + 1] if k + 1 < len(values) else values[k]
            for k in range(0, len(values), 2)
        ]
    return values[0]


def moments(p):
    momenta = []
    for a in range(3):
        up = add_all(p[i] for i in range(Q) if VELOCITY[i][a] == 1)
        down = add_all(p[i] for i in range(Q) if VELOCITY[i][a] == -1)
        momenta.append(up - down)
    return add_all(p), momenta


def along(i, vector):
    result = None
    for a in range(3):
        c = VELOCITY[i][a]
        if c == 0:
            continue
        if result is None:
            result = vector[a] if c == 1 else -vector[a]
        else:
            result = result + vector[a] if c == 1 else result - vector[a]
    return result


def post_tiles(which, straight, bounced, density, momenta, node, factor):
    inverse = 1.0 / density
    u = [factor * (m * inverse) for m in momenta]
    rest = 1.0 - 1.5 * (u[0] * u[0] + u[1] * u[1] + u[2] * u[2])
    rate = jnp.where(node <= 1.5, RELAXATION, 1.0)
    keep = 1.0 - rate
    wall = node == 2.0
    scale = rate * density
    result = {}
    for i in which:
        a = along(i, u)
        form = rest if a is None else rest + a * (3.0 + 4.5 * a)
        relaxed = keep * straight[i] + (WEIGHTS[i] * scale) * form
        result[i] = jnp.where(wall, bounced[i], relaxed)
    return result


def back_tiles(m, density, plain, node, factor):
    u = [factor * q for q in plain]
    rate = jnp.where(node <= 1.5, RELAXATION, 1.0)
    keep = 1.0 - rate
    wall = node == 2.0

    def weighted(select):
        total = None
        for w, group in ((1.0 / 18.0, range(1, 7)), (1.0 / 36.0, range(7, Q))):
            up = [m[i] for i in group if select(VELOCITY[i]) > 0]
            down = [m[i] for i in group if select(VELOCITY[i]) < 0]
            if not up and not down:
                continue
            value = add_all(up)
            if down:
                value = value - add_all(down)
            value = w * value
            total = value if total is None else total + value
        return total

    zero = (1.0 / 3.0) * m[0] + weighted(lambda c: 1)
    one = [weighted(lambda c, a=a: c[a]) for a in range(3)]
    two = {}
    for a in range(3):
        for b in range(a, 3):
            two[a, b] = two[b, a] = weighted(lambda c, a=a, b=b: c[a] * c[b])
    bent = [two[a, 0] * u[0] + two[a, 1] * u[1] + two[a, 2] * u[2] for a in range(3)]
    dot = lambda p, q: p[0] * q[0] + p[1] * q[1] + p[2] * q[2]
    scalar = zero * (1.0 - 1.5 * dot(u, u)) + 3.0 * dot(one, u) + 4.5 * dot(bent, u)
    vector = [3.0 * (one[a] + 3.0 * bent[a] - zero * u[a]) for a in range(3)]
    start = rate * (scalar - dot(vector, u))
    slope = [(rate * factor) * v for v in vector]
    result = []
    for i in range(Q):
        lean = along(i, slope)
        relaxed = keep * m[i] + (start if lean is None else start + lean)
        result.append(jnp.where(wall, m[OPPOSITE[i]], relaxed))
    gradient = jnp.where(wall, 0.0, rate * density * dot(vector, plain))
    return result, gradient


def whole(shape):
    return pl.BlockSpec(shape, lambda *_: (0,) * len(shape))


def anywhere():
    return pl.BlockSpec(memory_space=pl.ANY)


def call(body, outs, ins, specs, scratch=(), flops=1, name=None):
    size = sum(math.prod(o) for o in outs) * 4 + sum(math.prod(x.shape) for x in ins) * 4
    return pl.pallas_call(
        body,
        out_shape=[jax.ShapeDtypeStruct(o, F32) for o in outs],
        grid=(1,),
        in_specs=specs,
        out_specs=[whole(o) for o in outs],
        scratch_shapes=list(scratch),
        cost_estimate=pl.CostEstimate(flops=flops, bytes_accessed=size, transcendentals=0),
        compiler_params=pltpu.CompilerParams(vmem_limit_bytes=40 * 1024 * 1024),
        name=name,
    )(*ins)


def edge_message(out, fill, design, node, p, later, up, down):
    density, momenta = moments(p)
    wall = node == 2.0
    for j in range(RAD + 1):
        fill(out, j, design[j])
    fill(out, NODE, node)
    fill(out, DENS, density)
    for a in range(3):
        fill(out, DENS + 1 + a, momenta[a])
    for k, i in enumerate(up):
        fill(out, FWD + k, jnp.where(wall, p[OPPOSITE[i]], p[i]))
    for k, i in enumerate(down):
        fill(out, ADJ + k, later(i))


def first_x_body(fwd_lo, fwd_hi, later_lo, later_hi, des_lo, des_hi, node_lo, node_hi, up_out, down_out):
    for out, fwd, later, des, node, up, down in (
        (up_out, fwd_hi, later_hi, des_hi, node_hi, XP, XM),
        (down_out, fwd_lo, later_lo, des_lo, node_lo, XM, XP),
    ):
        for h in (0, 8):
            rows = slice(h, h + 8)

            def fill(out, k, value, rows=rows):
                out[k, rows, :] = value

            edge_message(
                out,
                fill,
                [des[j, rows, :] for j in range(RAD + 1)],
                node[0, rows, :].astype(F32),
                [fwd[i, 0, rows, :] for i in range(Q)],
                lambda i, later=later, rows=rows: later[i, 0, rows, :],
                up,
                down,
            )


def first_x(fwd, later, design, node):
    def plane(at):
        return pl.BlockSpec((Q, 1, BY, NZ), lambda g: (0, at, 0, 0))

    def slab(depth, at):
        return pl.BlockSpec((depth, BY, NZ), lambda g: (at, 0, 0))

    return call(
        first_x_body,
        [(MSG, BY, NZ)] * 2,
        (fwd, fwd, later, later, design, design, node, node),
        [plane(0), plane(BX - 1), plane(0), plane(BX - 1), slab(4, 0), slab(4, 1), slab(1, 0), slab(1, BX - 1)],
        flops=200000,
        name="first_x",
    )


def first_y_body(fwd, later, design, node, up_out, down_out):
    for out, row, rows, up, down in (
        (up_out, BY - 1, range(BY - 4, BY), YP, YM),
        (down_out, 0, range(4), YM, YP),
    ):

        def fill(out, k, value):
            out[k] = value

        edge_message(
            out,
            fill,
            [design[:, j, :] for j in rows],
            node[:, row, :].astype(F32),
            [fwd[i, :, row, :] for i in range(Q)],
            lambda i, row=row: later[i, :, row, :],
            up,
            down,
        )


def first_y(fwd, later, design, node):
    ins = (fwd, later, design, node)
    return call(
        first_y_body, [(MSG, BX, NZ)] * 2, ins, [whole(x.shape) for x in ins], flops=400000, name="first_y"
    )


def join_y_body(own_up, own_down, low, high, up_out, down_out):
    for out, own, row, rows, up, down in (
        (up_out, own_up, BY - 1, range(BY - 4, BY), YP, YM),
        (down_out, own_down, 0, range(4), YM, YP),
    ):
        out[...] = jnp.zeros_like(out)
        for k, j in enumerate(rows):
            out[k, 4:12, :] = own[k]
            for x in range(4):
                out[k, x : x + 1, :] = low[x, j : j + 1, :]
                out[k, 12 + x : 13 + x, :] = high[x, j : j + 1, :]
        for k in range(NODE, MSG):
            out[k, 1:9, :] = own[k]
        for k in range(NODE, FWD):
            out[k, 0:1, :] = low[k, row : row + 1, :]
            out[k, 9:10, :] = high[k, row : row + 1, :]
        for first, mine, from_low, from_high in ((FWD, up, XP, XM), (ADJ, down, XM, XP)):
            for k, i in enumerate(mine):
                if i in from_low:
                    out[first + k, 0:1, :] = low[first + from_low.index(i), row : row + 1, :]
                if i in from_high:
                    out[first + k, 9:10, :] = high[first + from_high.index(i), row : row + 1, :]


def join_y(own_up, own_down, low, high):
    ins = (own_up, own_down, low, high)
    return call(
        join_y_body, [(MSG, BY, NZ)] * 2, ins, [whole(x.shape) for x in ins], flops=40000, name="join_y"
    )


ROW = 8
PADY = 32


def main_body(
    fwd, later_any, design, node, region, xlow, xhigh, ylow, yhigh,
    mid, flow, first, factor_out, part, up_out, down_out,
    wide, kinds, fine, post, later, sem,
):
    copy = pltpu.make_async_copy(later_any, later.at[:, 1 : 1 + BX, ROW : ROW + BY, :], sem)
    copy.start()
    wide[...] = jnp.zeros_like(wide)
    wide[4:12, ROW : ROW + BY, :] = design[...]
    wide[0:4, ROW : ROW + BY, :] = xlow[0:4]
    wide[12:16, ROW : ROW + BY, :] = xhigh[0:4]
    kinds[...] = jnp.zeros_like(kinds)
    kinds[1:9, ROW : ROW + BY, :] = node[...].astype(F32)
    kinds[0, ROW : ROW + BY, :] = xlow[NODE]
    kinds[9, ROW : ROW + BY, :] = xhigh[NODE]
    for x in range(16):
        for j in range(4):
            wide[x, ROW - 4 + j : ROW - 3 + j, :] = ylow[j, x : x + 1, :]
            wide[x, ROW + BY + j : ROW + BY + 1 + j, :] = yhigh[j, x : x + 1, :]
    for x in range(10):
        kinds[x, ROW - 1 : ROW, :] = ylow[NODE, x : x + 1, :]
        kinds[x, ROW + BY : ROW + BY + 1, :] = yhigh[NODE, x : x + 1, :]
    norm = norm_row((8, NZ))
    inverse_norm = 1.0 / norm

    def filter_plane(x, carry):
        for r in (4, 12, 20):
            value = filter_rows(lambda a, b: wide[x + RAD + a, r + b : r + b + 8, :]) * inverse_norm
            fine[x, r : r + 8, :] = value
        return carry

    lax.fori_loop(0, 10, filter_plane, 0)

    def factor_of(kind, filtered):
        return jnp.where(kind == 1.0, 1.0 - BRINKMAN * (1.0 - filtered), 1.0)

    for x, message, comps in ((0, xlow, XP), (9, xhigh, XM)):
        for h in (0, 8):
            rows = slice(h, h + 8)
            padded = slice(ROW + h, ROW + h + 8)
            kind = kinds[x, padded, :]
            q = {i: message[FWD + k, rows, :] for k, i in enumerate(comps)}
            value = post_tiles(
                comps, q, q, message[DENS, rows, :], [message[DENS + 1 + a, rows, :] for a in range(3)],
                kind, factor_of(kind, fine[x, padded, :]),
            )
            for i in comps:
                post[i, x, padded, :] = value[i]
    for row, message, comps in ((ROW - 1, ylow, YP), (ROW + BY, yhigh, YM)):
        kind = kinds[:, row, :]
        q = {i: message[FWD + k, 0:10, :] for k, i in enumerate(comps)}
        value = post_tiles(
            comps, q, q, message[DENS, 0:10, :], [message[DENS + 1 + a, 0:10, :] for a in range(3)],
            kind, factor_of(kind, fine[:, row, :]),
        )
        for i in comps:
            for x in range(10):
                post[i, x, row : row + 1, :] = value[i][x : x + 1, :]

    def post_plane(x, carry):
        carry = list(carry)
        for h in (0, 8):
            rows = slice(h, h + 8)
            padded = slice(ROW + h, ROW + h + 8)
            p = [fwd[i, x, rows, :] for i in range(Q)]
            density, momenta = moments(p)
            kind = kinds[x + 1, padded, :]
            filtered = fine[x + 1, padded, :]
            factor = factor_of(kind, filtered)
            factor_out[x, rows, :] = factor
            inverse = 1.0 / density
            flow[0, x, rows, :] = density
            for a in range(3):
                flow[1 + a, x, rows, :] = momenta[a] * inverse
            bounced = [p[OPPOSITE[i]] for i in range(Q)]
            value = post_tiles(range(Q), p, bounced, density, momenta, kind, factor)
            for i in range(Q):
                post[i, x + 1, padded, :] = value[i]
            counted = jnp.where(kind == 1.0, filtered, 0.0)
            where_region = region[x, rows, :]
            for r in range(REG):
                carry[r] = carry[r] + jnp.where(where_region == r, counted, 0.0)
        return tuple(carry)

    empty = jnp.zeros((8, NZ), F32)
    totals = lax.fori_loop(0, BX, post_plane, (empty,) * REG)
    for r in range(REG):
        part[r] = totals[r]

    copy.wait()
    for x, message, comps in ((0, xlow, XM), (9, xhigh, XP)):
        for k, i in enumerate(comps):
            later[i, x, ROW : ROW + BY, :] = message[ADJ + k]
    for row, message, comps in ((ROW - 1, ylow, YM), (ROW + BY, yhigh, YP)):
        for k, i in enumerate(comps):
            for x in range(10):
                later[i, x, row : row + 1, :] = message[ADJ + k, x : x + 1, :]

    def mid_plane(x, carry):
        for h in (0, 8):
            rows = slice(h, h + 8)
            padded = slice(ROW + h, ROW + h + 8)
            density, mx, my, mz = 0.0, 0.0, 0.0, 0.0
            for cz in (0, 1, -1):
                p = {}
                for i in range(Q):
                    if VELOCITY[i][2] == cz:
                        at = ROW + h - VELOCITY[i][1]
                        p[i] = post[i, x + 1 - VELOCITY[i][0], at : at + 8, :]
                whole_sum = shift_z(add_all(p.values()), -cz)
                density = density + whole_sum
                if cz:
                    mz = mz + cz * whole_sum
                sides = []
                for a in range(2):
                    up = add_all(p[i] for i in p if VELOCITY[i][a] == 1)
                    down = add_all(p[i] for i in p if VELOCITY[i][a] == -1)
                    sides.append(shift_z(up - down, -cz))
                mx = mx + sides[0]
                my = my + sides[1]
            kind = kinds[x + 1, padded, :]
            outlet = kind == 4.0
            carry = carry + jnp.where(outlet, mx, 0.0)
            inverse = 1.0 / density
            m = []
            for i in range(Q):
                at = ROW + h + VELOCITY[i][1]
                m.append(shift_z(later[i, x + 1 + VELOCITY[i][0], at : at + 8, :], VELOCITY[i][2]))
            value, gradient = back_tiles(
                m, density, [mx * inverse, my * inverse, mz * inverse], kind, factor_out[x, rows, :]
            )
            source = jnp.where(outlet, 1.0, 0.0)
            for i in range(Q):
                c = VELOCITY[i][0]
                mid[i, x, rows, :] = value[i] + c * source if c else value[i]
            first[x, rows, :] = gradient
        return carry

    part[REG] = lax.fori_loop(0, BX, mid_plane, empty)
    for k, i in enumerate(XM):
        up_out[k] = mid[i, BX - 1]
    for k, i in enumerate(XP):
        down_out[k] = mid[i, 0]


def main(fwd, later, design, node, region, xlow, xhigh, ylow, yhigh):
    ins = (fwd, later, design, node, region, xlow, xhigh, ylow, yhigh)
    specs = [whole(x.shape) for x in ins]
    specs[1] = anywhere()
    return call(
        main_body,
        [(Q, BX, BY, NZ), (4, BX, BY, NZ), (BX, BY, NZ), (BX, BY, NZ), (REG + 1, 8, NZ), (5, BY, NZ), (5, BY, NZ)],
        ins,
        specs,
        scratch=(
            pltpu.VMEM((16, PADY, NZ), F32),
            pltpu.VMEM((10, PADY, NZ), F32),
            pltpu.VMEM((10, PADY, NZ), F32),
            pltpu.VMEM((Q, 10, PADY, NZ), F32),
            pltpu.VMEM((Q, 10, PADY, NZ), F32),
            pltpu.SemaphoreType.DMA,
        ),
        flops=20000000,
        name="main",
    )


def mid_y_body(mid, low, high, up_out, down_out):
    for out, row, comps in ((up_out, BY - 1, YM), (down_out, 0, YP)):
        for k, i in enumerate(comps):
            out[k] = jnp.zeros((BY, NZ), F32)
            out[k, 1:9, :] = mid[i, :, row, :]
            if i in XM:
                out[k, 0:1, :] = low[XM.index(i), row : row + 1, :]
            if i in XP:
                out[k, 9:10, :] = high[XP.index(i), row : row + 1, :]


def mid_y(mid, low, high):
    ins = (mid, low, high)
    return call(mid_y_body, [(5, BY, NZ)] * 2, ins, [whole(x.shape) for x in ins], flops=20000, name="mid_y")


def last_body(mid_any, flow, first, factor, node, xlow, xhigh, ylow, yhigh, adjoint, raw, up_out, down_out, mid, sem):
    copy = pltpu.make_async_copy(mid_any, mid.at[:, 1 : 1 + BX, ROW : ROW + BY, :], sem)
    copy.start()
    for x, message, comps in ((0, xlow, XM), (9, xhigh, XP)):
        for k, i in enumerate(comps):
            mid[i, x, ROW : ROW + BY, :] = message[k]
    for row, message, comps in ((ROW - 1, ylow, YM), (ROW + BY, yhigh, YP)):
        for k, i in enumerate(comps):
            for x in range(10):
                mid[i, x, row : row + 1, :] = message[k, x : x + 1, :]
    inverse_norm = BRINKMAN / norm_row((8, NZ))
    copy.wait()

    def plane(x, carry):
        for h in (0, 8):
            rows = slice(h, h + 8)
            kind = node[x, rows, :].astype(F32)
            m = []
            for i in range(Q):
                at = ROW + h + VELOCITY[i][1]
                m.append(shift_z(mid[i, x + 1 + VELOCITY[i][0], at : at + 8, :], VELOCITY[i][2]))
            value, gradient = back_tiles(
                m, flow[0, x, rows, :], [flow[1 + a, x, rows, :] for a in range(3)], kind, factor[x, rows, :]
            )
            for i in range(Q):
                adjoint[i, x, rows, :] = value[i]
            both = (first[x, rows, :] + gradient) * inverse_norm
            raw[x, rows, :] = jnp.where(kind == 1.0, both, 0.0)
        return carry

    lax.fori_loop(0, BX, plane, 0)
    up_out[...] = raw[BX - RAD :]
    down_out[...] = raw[:RAD]


def last(mid, flow, first, factor, node, xlow, xhigh, ylow, yhigh):
    ins = (mid, flow, first, factor, node, xlow, xhigh, ylow, yhigh)
    specs = [whole(x.shape) for x in ins]
    specs[0] = anywhere()
    return call(
        last_body,
        [(Q, BX, BY, NZ), (BX, BY, NZ), (RAD, BY, NZ), (RAD, BY, NZ)],
        ins,
        specs,
        scratch=(pltpu.VMEM((Q, 10, PADY, NZ), F32), pltpu.SemaphoreType.DMA),
        flops=8000000,
        name="last",
    )


def raw_y_body(raw, low, high, up_out, down_out):
    for out, begin in ((up_out, BY - RAD), (down_out, 0)):
        out[...] = jnp.zeros_like(out)
        for j in range(RAD):
            out[j, RAD : RAD + BX, :] = raw[:, begin + j, :]
            for x in range(RAD):
                out[j, x : x + 1, :] = low[x, begin + j : begin + j + 1, :]
                out[j, RAD + BX + x : RAD + BX + x + 1, :] = high[x, begin + j : begin + j + 1, :]


def raw_y(raw, low, high):
    ins = (raw, low, high)
    return call(raw_y_body, [(RAD, BY, NZ)] * 2, ins, [whole(x.shape) for x in ins], flops=20000, name="raw_y")


def spread_body(raw, xlow, xhigh, ylow, yhigh, out, wide):
    wide[RAD : RAD + BX, ROW : ROW + BY, :] = raw[...]
    wide[0:RAD, ROW : ROW + BY, :] = xlow[...]
    wide[RAD + BX :, ROW : ROW + BY, :] = xhigh[...]
    for x in range(BX + 2 * RAD):
        for j in range(RAD):
            wide[x, ROW - RAD + j : ROW - RAD + j + 1, :] = ylow[j, x : x + 1, :]
            wide[x, ROW + BY + j : ROW + BY + j + 1, :] = yhigh[j, x : x + 1, :]

    def plane(x, carry):
        for h in (0, 8):
            at = ROW + h
            out[x, h : h + 8, :] = filter_rows(lambda a, b: wide[x + RAD + a, at + b : at + b + 8, :])
        return carry

    lax.fori_loop(0, BX, plane, 0)


def spread(raw, xlow, xhigh, ylow, yhigh):
    ins = (raw, xlow, xhigh, ylow, yhigh)
    return call(
        spread_body,
        [(BX, BY, NZ)],
        ins,
        [whole(x.shape) for x in ins],
        scratch=(pltpu.VMEM((BX + 2 * RAD, PADY, NZ), F32),),
        flops=2000000,
        name="spread",
    )[0]


def exchange(up, down, axis):
    count = lax.axis_size(axis)
    forward = [(i, (i + 1) % count) for i in range(count)]
    backward = [(j, i) for i, j in forward]
    return lax.ppermute(up, axis, forward), lax.ppermute(down, axis, backward)


def total(row):
    for axis in ("gy", "gx"):
        count = lax.axis_size(axis)
        rows = jnp.broadcast_to(row[None], (count,) + row.shape)
        row = jnp.sum(lax.all_to_all(rows, axis, 0, 0, tiled=True), axis=0)
    return row


def per_device(forward_pops, later_adjoint, design, node_type, region):
    up, down = first_x(forward_pops, later_adjoint, design, node_type)
    own_up, own_down = first_y(forward_pops, later_adjoint, design, node_type)
    xlow, xhigh = exchange(up, down, "gx")
    up, down = join_y(own_up, own_down, xlow, xhigh)
    ylow, yhigh = exchange(up, down, "gy")
    mid, flow, first, factor, part, up, down = main(
        forward_pops, later_adjoint, design, node_type, region, xlow, xhigh, ylow, yhigh
    )
    sums = total(jnp.pad(jnp.sum(part, axis=(1, 2)), (0, NZ - REG - 1)))
    xlow, xhigh = exchange(up, down, "gx")
    up, down = mid_y(mid, xlow, xhigh)
    ylow, yhigh = exchange(up, down, "gy")
    adjoint, raw, up, down = last(mid, flow, first, factor, node_type, xlow, xhigh, ylow, yhigh)
    xlow, xhigh = exchange(up, down, "gx")
    up, down = raw_y(raw, xlow, xhigh)
    ylow, yhigh = exchange(up, down, "gy")
    sensitivity = spread(raw, xlow, xhigh, ylow, yhigh)
    return adjoint, sensitivity, sums[REG], sums[:REG]


def solution(mesh):
    cells = P("gx", "gy", None)
    pops = P(None, "gx", "gy", None)
    return jax.shard_map(
        per_device,
        mesh=mesh,
        in_specs=(pops, pops, cells, cells, cells),
        out_specs=(pops, cells, P(), P()),
        check_vma=False,
    )
```

time: 248 us -> 119 us (0.48)
  blocking collectives: 96.7 us -> 19.3 us
  other arithmetic: 25.4 us -> 0.19 us
  starting transfers between devices: 76.4 us -> 57.8 us
  waiting for transfers between devices: 39.6 us -> 26 us
  Pallas kernels: 0 us -> 8.06 us
  local copies, waits for them, and re-layouts: 8.11 us -> 5.49 us
    psum x1 -> x0, blocking collectives: 96.7 us -> none  [per_device(): objective, volumes = lax.psum((objective_local, volume_local), ('gx', 'gy'))]
    ppermute x16 -> x12, starting transfers between devices: 76.4 us -> 54 us  [exchange(): return (lax.ppermute(up, axis, forward), lax.ppermute(down, axis, backward))]
    all_to_all x0 -> x1, blocking collectives: none -> 19.3 us  [total(): row = jnp.sum(lax.all_to_all(rows, axis, 0, 0, tiled=True), axis=0)]
    ppermute x16 -> x12, waiting for transfers between devices: 39.6 us -> 21.8 us  [exchange(): return (lax.ppermute(up, axis, forward), lax.ppermute(down, axis, backward))]
    pallas_call x0 -> x8, Pallas kernels: none -> 8.06 us  [call(): pl.pallas_call(body, out_shape=[jax.ShapeDtypeStruct(o, F32) for o in out...]
    concatenate x7 -> x0, other arithmetic: 7.36 us -> none  [padded_2(): block = jnp.concatenate([low, block, high], axis=dim)]
    unnamed x73 -> x0, other arithmetic: 6.69 us -> none
    another operation x13 -> x0, local copies, waits for them, and re-layouts: 5.78 us -> none  [the longest x1 5.7 us: per_device(): jnp.stack([jnp.sum(jnp.where((node_type == 1) & (region == r), filtered,...]
  transfers between devices with their start and end apart: 16 -> 13, of which waited for: 8 -> 8; matrix products, arithmetic and copies ran while one was open for 4% -> 1% of each run, Pallas kernels for 0% -> 0%
where the time goes in v1:
time: 119 us; the launch traced here: 118 us
  starting transfers between devices  57.8 us (49%)
  waiting for transfers between devices  26 us (22%)
  blocking collectives  19.3 us (16%)
  Pallas kernels  8.06 us (7%)
  local copies, waits for them, and re-layouts  5.49 us (5%)
    ppermute x12, starting transfers between devices, exchange(): return (lax.ppermute(up, axis, forward), lax.ppermute(down, axis, backward))  54 us
    ppermute x12, waiting for transfers between devices, exchange(): return (lax.ppermute(up, axis, forward), lax.ppermute(down, axis, backward))  21.8 us
    all_to_all x1, blocking collectives, total(): row = jnp.sum(lax.all_to_all(rows, axis, 0, 0, tiled=True), axis=0)  19.3 us
    pallas_call x8, Pallas kernels, call(): pl.pallas_call(body, out_shape=[jax.ShapeDtypeStruct(o, F32) for o in out...  8.06 us
    unnamed x14, local copies, waits for them, and re-layouts  4.28 us
    all_to_all x1, waiting for transfers between devices, total(): row = jnp.sum(lax.all_to_all(rows, axis, 0, 0, tiled=True), axis=0)  4.13 us
    all_to_all x1, starting transfers between devices, total(): row = jnp.sum(lax.all_to_all(rows, axis, 0, 0, tiled=True), axis=0)  3.83 us
  transfers between devices with their start and end apart: 13, of which 8 were waited for; matrix products, arithmetic and copies ran while one was open for 1% of the time, Pallas kernels for 0%

profile of v1, /device:TPU:1, one launch (start us, length us, event | category | flops | bytes accessed | tf_op | source)
XLA Modules:
  0.0 117.7 jit_solution(1981441116387547426)
XLA Ops:
  0.6 1.3 %copy-done = f32[19,8,16,128]{3,2,1,0:T(8,128)S(1)} copy-done((f32[19,8,16,128]{3,2,1,0:T(8,128)S(1)}, f32[19,8,16,128]{3,2,1,0:T(8,128)}, u32[]{:S(2)}) %copy-start) | copy-done | bytes 1245208
  1.9 1.3 %copy-done.2 = f32[19,8,16,128]{3,2,1,0:T(8,128)S(1)} copy-done((f32[19,8,16,128]{3,2,1,0:T(8,128)S(1)}, f32[19,8,16,128]{3,2,1,0:T(8,128)}, u32[]{:S(2)}) %copy-start.2) | copy-done | bytes 1245208
  4.9 4.0 %collective-permute-start = (f32[19,16,128]{2,1,0:T(8,128)S(1)}, f32[19,16,128]{2,1,0:T(8,128)S(1)}, u32[]{:S(2)}, u32[]{:S(2)}) collective-permute-start(f32[19,16,128]{2,1,0:T(8,128)S(1)} %get-tuple-element.25), channel_id=1, source_target_pairs={{0,16},{16,32},{32,48},{48,64},{64,80},{80,96},{96,112},{112,128},... | collective-permute-start | bytes 466952 | tf_op jit(solution)/shard_map/ppermute | solution.py:628
  9.0 9.4 %collective-permute-start.1 = (f32[19,16,128]{2,1,0:T(8,128)S(1)}, f32[19,16,128]{2,1,0:T(8,128)S(1)}, u32[]{:S(2)}, u32[]{:S(2)}) collective-permute-start(f32[19,16,128]{2,1,0:T(8,128)S(1)} %get-tuple-element.26), channel_id=1, source_target_pairs={{16,0},{32,16},{48,32},{64,48},{80,64},{96,80},{112,96},{128,112},... | collective-permute-start | bytes 466952 | tf_op jit(solution)/shard_map/ppermute | solution.py:628
  18.9 1.6 %collective-permute-done.1.high.xhigh = f32[19,16,128]{2,1,0:T(8,128)S(1)} collective-permute-done((f32[19,16,128]{2,1,0:T(8,128)S(1)}, f32[19,16,128]{2,1,0:T(8,128)S(1)}, u32[]{:S(2)}, u32[]{:S(2)}) %collective-permute-start.1) | collective-permute-done | bytes 155680 | tf_op jit(solution)/shard_map/ppermute | solution.py:628
  20.6 9.9 %collective-permute-start.2 = (f32[19,16,128]{2,1,0:T(8,128)S(1)}, f32[19,16,128]{2,1,0:T(8,128)S(1)}, u32[]{:S(2)}, u32[]{:S(2)}) collective-permute-start(f32[19,16,128]{2,1,0:T(8,128)S(1)} %get-tuple-element.29), channel_id=1, source_target_pairs={{0,1},{1,2},{2,3},{3,4},{4,5},{5,6},{6,7},{7,8},{8,9},{9,10},{10,1... | collective-permute-start | bytes 466952 | tf_op jit(solution)/shard_map/ppermute | solution.py:628
  30.5 1.9 %collective-permute-start.3 = (f32[19,16,128]{2,1,0:T(8,128)S(1)}, f32[19,16,128]{2,1,0:T(8,128)S(1)}, u32[]{:S(2)}, u32[]{:S(2)}) collective-permute-start(f32[19,16,128]{2,1,0:T(8,128)S(1)} %get-tuple-element.30), channel_id=1, source_target_pairs={{1,0},{2,1},{3,2},{4,3},{5,4},{6,5},{7,6},{8,7},{9,8},{10,9},{11,1... | collective-permute-start | bytes 466952 | tf_op jit(solution)/shard_map/ppermute | solution.py:628
  32.7 8.9 %collective-permute-done.3.yhigh = f32[19,16,128]{2,1,0:T(8,128)S(1)} collective-permute-done((f32[19,16,128]{2,1,0:T(8,128)S(1)}, f32[19,16,128]{2,1,0:T(8,128)S(1)}, u32[]{:S(2)}, u32[]{:S(2)}) %collective-permute-start.3) | collective-permute-done | bytes 155680 | tf_op jit(solution)/shard_map/ppermute | solution.py:628
  41.5 3.7 %main.1 = (f32[19,8,16,128]{3,2,1,0:T(8,128)S(1)}, f32[4,8,16,128]{3,2,1,0:T(8,128)S(1)}, f32[8,16,128]{2,1,0:T(8,128)S(1)}, f32[8,16,128]{2,1,0:T(8,128)S(1)}, ...) custom-call(f32[19,8,16,128]{3,2,1,0:T(8,128)S(1)} %copy-done.1, ...), custom_call_target="tpu_custom_call" | custom-call | flops 20000000 | bytes 5066752 | tf_op jit(solution)/shard_map/main/pallas_call | solution.py:214
  45.3 1.9 %collective-permute-start.4 = (f32[5,16,128]{2,1,0:T(8,128)S(1)}, f32[5,16,128]{2,1,0:T(8,128)S(1)}, u32[]{:S(2)}, u32[]{:S(2)}) collective-permute-start(f32[5,16,128]{2,1,0:T(8,128)S(1)} %get-tuple-element.35), channel_id=1, source_target_pairs={{0,16},{16,32},{32,48},{48,64},{64,80},{80,96},{96,112},{112,128},... | collective-permute-start | bytes 122888 | tf_op jit(solution)/shard_map/ppermute | solution.py:628
  47.2 7.8 %collective-permute-start.5 = (f32[5,16,128]{2,1,0:T(8,128)S(1)}, f32[5,16,128]{2,1,0:T(8,128)S(1)}, u32[]{:S(2)}, u32[]{:S(2)}) collective-permute-start(f32[5,16,128]{2,1,0:T(8,128)S(1)} %get-tuple-element.36), channel_id=1, source_target_pairs={{16,0},{32,16},{48,32},{64,48},{80,64},{96,80},{112,96},{128,112},... | collective-permute-start | bytes 122888 | tf_op jit(solution)/shard_map/ppermute | solution.py:628
  56.1 2.6 %collective-permute-start.6 = (f32[5,16,128]{2,1,0:T(8,128)S(1)}, f32[5,16,128]{2,1,0:T(8,128)S(1)}, u32[]{:S(2)}, u32[]{:S(2)}) collective-permute-start(f32[5,16,128]{2,1,0:T(8,128)S(1)} %get-tuple-element.37), channel_id=1, source_target_pairs={{0,1},{1,2},{2,3},{3,4},{4,5},{5,6},{6,7},{7,8},{8,9},{9,10},{10,1... | collective-permute-start | bytes 122888 | tf_op jit(solution)/shard_map/ppermute | solution.py:628
  58.7 1.9 %collective-permute-start.7 = (f32[5,16,128]{2,1,0:T(8,128)S(1)}, f32[5,16,128]{2,1,0:T(8,128)S(1)}, u32[]{:S(2)}, u32[]{:S(2)}) collective-permute-start(f32[5,16,128]{2,1,0:T(8,128)S(1)} %get-tuple-element.38), channel_id=1, source_target_pairs={{1,0},{2,1},{3,2},{4,3},{5,4},{6,5},{7,6},{8,7},{9,8},{10,9},{11,1... | collective-permute-start | bytes 122888 | tf_op jit(solution)/shard_map/ppermute | solution.py:628
  60.7 7.4 %collective-permute-done.7.yhigh = f32[5,16,128]{2,1,0:T(8,128)S(1)} collective-permute-done((f32[5,16,128]{2,1,0:T(8,128)S(1)}, f32[5,16,128]{2,1,0:T(8,128)S(1)}, u32[]{:S(2)}, u32[]{:S(2)}) %collective-permute-start.7) | collective-permute-done | bytes 40992 | tf_op jit(solution)/shard_map/ppermute | solution.py:628
  68.1 2.4 %last.1 = (f32[19,8,16,128]{3,2,1,0:T(8,128)}, f32[8,16,128]{2,1,0:T(8,128)S(1)}, f32[3,16,128]{2,1,0:T(8,128)S(1)}, f32[3,16,128]{2,1,0:T(8,128)S(1)}) custom-call(f32[19,8,16,128]{3,2,1,0:T(8,128)S(1)} %get-tuple-element.31.mid.mid_any, f32[4,8,16,128]{3,2,1,0:T(8,128)S(1)} %get-tuple-element.32.flow, f32[8,16,128]{2,1,0:T(8,128)S(1)} %get-tuple-element.33.first, ...), custom_call_target="tpu_custom_call" | custom-call | flops 8000000 | bytes 3227648 | tf_op jit(solution)/shard_map/last/pallas_call | solution.py:214
  70.5 1.9 %collective-permute-start.8 = (f32[3,16,128]{2,1,0:T(8,128)S(1)}, f32[3,16,128]{2,1,0:T(8,128)S(1)}, u32[]{:S(2)}, u32[]{:S(2)}) collective-permute-start(f32[3,16,128]{2,1,0:T(8,128)S(1)} %get-tuple-element.41), channel_id=1, source_target_pairs={{0,16},{16,32},{32,48},{48,64},{64,80},{80,96},{96,112},{112,128},... | collective-permute-start | bytes 73736 | tf_op jit(solution)/shard_map/ppermute | solution.py:628
  72.4 7.9 %collective-permute-start.9 = (f32[3,16,128]{2,1,0:T(8,128)S(1)}, f32[3,16,128]{2,1,0:T(8,128)S(1)}, u32[]{:S(2)}, u32[]{:S(2)}) collective-permute-start(f32[3,16,128]{2,1,0:T(8,128)S(1)} %get-tuple-element.42), channel_id=1, source_target_pairs={{16,0},{32,16},{48,32},{64,48},{80,64},{96,80},{112,96},{128,112},... | collective-permute-start | bytes 73736 | tf_op jit(solution)/shard_map/ppermute | solution.py:628
  80.5 19.3 %all_to_all.12 = f32[16,1,128]{2,1,0:T(1,128)S(1)} all-to-all(f32[16,1,128]{2,1,0:T(1,128)S(1)} %broadcast_in_dim.4), channel_id=1, replica_groups=mesh['gx'=32,'gy'=16] {'gy'}, dimensions={0} | all-to-all | bytes 16384 | tf_op jit(solution)/shard_map/all_to_all | solution.py:635
  100.4 3.8 %all-to-all-start.1 = ((f32[32,1,128]{2,1,0:T(1,128)}), f32[32,1,128]{2,1,0:T(1,128)S(1)}, u32[]{:S(2)}, u32[]{:S(2)}) async-start(f32[32,1,128]{2,1,0:T(1,128)} %broadcast_in_dim.5), calls=%async_computation.1 | async-start | bytes 32768 | tf_op jit(solution)/shard_map/all_to_all | solution.py:635
  104.3 2.8 %collective-permute-start.10 = (f32[3,16,128]{2,1,0:T(8,128)S(1)}, f32[3,16,128]{2,1,0:T(8,128)S(1)}, u32[]{:S(2)}, u32[]{:S(2)}) collective-permute-start(f32[3,16,128]{2,1,0:T(8,128)S(1)} %get-tuple-element.43), channel_id=1, source_target_pairs={{0,1},{1,2},{2,3},{3,4},{4,5},{5,6},{6,7},{7,8},{8,9},{9,10},{10,1... | collective-permute-start | bytes 73736 | tf_op jit(solution)/shard_map/ppermute | solution.py:628
  107.1 1.9 %collective-permute-start.11 = (f32[3,16,128]{2,1,0:T(8,128)S(1)}, f32[3,16,128]{2,1,0:T(8,128)S(1)}, u32[]{:S(2)}, u32[]{:S(2)}) collective-permute-start(f32[3,16,128]{2,1,0:T(8,128)S(1)} %get-tuple-element.44), channel_id=1, source_target_pairs={{1,0},{2,1},{3,2},{4,3},{5,4},{6,5},{7,6},{8,7},{9,8},{10,9},{11,1... | collective-permute-start | bytes 73736 | tf_op jit(solution)/shard_map/ppermute | solution.py:628
  109.0 4.1 %all-to-all-done.1 = f32[32,1,128]{2,1,0:T(1,128)S(1)} async-done(((f32[32,1,128]{2,1,0:T(1,128)}), f32[32,1,128]{2,1,0:T(1,128)S(1)}, u32[]{:S(2)}, u32[]{:S(2)}) %all-to-all-start.1) | async-done | bytes 16416 | tf_op jit(solution)/shard_map/all_to_all | solution.py:635
  113.8 2.4 %collective-permute-done.11.yhigh = f32[3,16,128]{2,1,0:T(8,128)S(1)} collective-permute-done((f32[3,16,128]{2,1,0:T(8,128)S(1)}, f32[3,16,128]{2,1,0:T(8,128)S(1)}, u32[]{:S(2)}, u32[]{:S(2)}) %collective-permute-start.11) | collective-permute-done | bytes 24608 | tf_op jit(solution)/shard_map/ppermute | solution.py:628
  116.1 1.6 %spread.1 = f32[8,16,128]{2,1,0:T(8,128)} custom-call(f32[8,16,128]{2,1,0:T(8,128)S(1)} %get-tuple-element.40.raw, f32[3,16,128]{2,1,0:T(8,128)S(1)} %collective-permute-done.8.low.xlow, f32[3,16,128]{2,1,0:T(8,128)S(1)} %collective-permute-done.9.high.xhigh, f32[3,16,128]{2,1,0:T(8,128)S(1)} %collective-permute-done.10.ylow, ...), custom_call_target="tpu_custom_call" | custom-call | flops 2000000 | bytes 229376 | tf_op jit(solution)/shard_map/spread/pallas_call | solution.py:214
  (32 shorter events, 5.1 us)
Async XLA Ops:
  0.6 1.3 %copy-start = (f32[19,8,16,128]{3,2,1,0:T(8,128)S(1)}, f32[19,8,16,128]{3,2,1,0:T(8,128)}, u32[]{:S(2)}) copy-start(f32[19,8,16,128]{3,2,1,0:T(8,128)} %fwd.3) | copy-start | bytes 3735556
  1.9 1.3 %copy-start.2 = (f32[19,8,16,128]{3,2,1,0:T(8,128)S(1)}, f32[19,8,16,128]{3,2,1,0:T(8,128)}, u32[]{:S(2)}) copy-start(f32[19,8,16,128]{3,2,1,0:T(8,128)} %later_any.1) | copy-start | bytes 3735556
  3.2 0.8 copy-start.3
  4.1 0.8 copy-start.4
  4.9 14.0 %collective-permute-start = (f32[19,16,128]{2,1,0:T(8,128)S(1)}, f32[19,16,128]{2,1,0:T(8,128)S(1)}, u32[]{:S(2)}, u32[]{:S(2)}) collective-permute-start(f32[19,16,128]{2,1,0:T(8,128)S(1)} %get-tuple-element.25), channel_id=1, source_target_pairs={{0,16},{16,32},{32,48},{48,64},{64,80},{80,96},{96,112},{112,128},... | collective-permute-start | bytes 466952 | tf_op jit(solution)/shard_map/ppermute | solution.py:628
  9.0 32.5 %copy-start.1 = (f32[19,8,16,128]{3,2,1,0:T(8,128)S(1)}, f32[19,8,16,128]{3,2,1,0:T(8,128)}, u32[]{:S(2)}) copy-start(f32[19,8,16,128]{3,2,1,0:T(8,128)} %fwd.3) | copy-start | bytes 3735556
  9.0 32.5 %copy-start.5 = (s32[8,16,128]{2,1,0:T(8,128)S(1)}, s32[8,16,128]{2,1,0:T(8,128)}, u32[]{:S(2)}) copy-start(s32[8,16,128]{2,1,0:T(8,128)} %region.1) | copy-start | bytes 196612
  9.0 11.5 %collective-permute-start.1 = (f32[19,16,128]{2,1,0:T(8,128)S(1)}, f32[19,16,128]{2,1,0:T(8,128)S(1)}, u32[]{:S(2)}, u32[]{:S(2)}) collective-permute-start(f32[19,16,128]{2,1,0:T(8,128)S(1)} %get-tuple-element.26), channel_id=1, source_target_pairs={{16,0},{32,16},{48,32},{64,48},{80,64},{96,80},{112,96},{128,112},... | collective-permute-start | bytes 466952 | tf_op jit(solution)/shard_map/ppermute | solution.py:628
  20.6 12.0 %collective-permute-start.2 = (f32[19,16,128]{2,1,0:T(8,128)S(1)}, f32[19,16,128]{2,1,0:T(8,128)S(1)}, u32[]{:S(2)}, u32[]{:S(2)}) collective-permute-start(f32[19,16,128]{2,1,0:T(8,128)S(1)} %get-tuple-element.29), channel_id=1, source_target_pairs={{0,1},{1,2},{2,3},{3,4},{4,5},{5,6},{6,7},{7,8},{8,9},{9,10},{10,1... | collective-permute-start | bytes 466952 | tf_op jit(solution)/shard_map/ppermute | solution.py:628
  30.5 11.0 %collective-permute-start.3 = (f32[19,16,128]{2,1,0:T(8,128)S(1)}, f32[19,16,128]{2,1,0:T(8,128)S(1)}, u32[]{:S(2)}, u32[]{:S(2)}) collective-permute-start(f32[19,16,128]{2,1,0:T(8,128)S(1)} %get-tuple-element.30), channel_id=1, source_target_pairs={{1,0},{2,1},{3,2},{4,3},{5,4},{6,5},{7,6},{8,7},{9,8},{10,9},{11,1... | collective-permute-start | bytes 466952 | tf_op jit(solution)/shard_map/ppermute | solution.py:628
  45.3 9.8 %collective-permute-start.4 = (f32[5,16,128]{2,1,0:T(8,128)S(1)}, f32[5,16,128]{2,1,0:T(8,128)S(1)}, u32[]{:S(2)}, u32[]{:S(2)}) collective-permute-start(f32[5,16,128]{2,1,0:T(8,128)S(1)} %get-tuple-element.35), channel_id=1, source_target_pairs={{0,16},{16,32},{32,48},{48,64},{64,80},{80,96},{96,112},{112,128},... | collective-permute-start | bytes 122888 | tf_op jit(solution)/shard_map/ppermute | solution.py:628
  47.2 8.9 %collective-permute-start.5 = (f32[5,16,128]{2,1,0:T(8,128)S(1)}, f32[5,16,128]{2,1,0:T(8,128)S(1)}, u32[]{:S(2)}, u32[]{:S(2)}) collective-permute-start(f32[5,16,128]{2,1,0:T(8,128)S(1)} %get-tuple-element.36), channel_id=1, source_target_pairs={{16,0},{32,16},{48,32},{64,48},{80,64},{96,80},{112,96},{128,112},... | collective-permute-start | bytes 122888 | tf_op jit(solution)/shard_map/ppermute | solution.py:628
  56.1 4.5 %collective-permute-start.6 = (f32[5,16,128]{2,1,0:T(8,128)S(1)}, f32[5,16,128]{2,1,0:T(8,128)S(1)}, u32[]{:S(2)}, u32[]{:S(2)}) collective-permute-start(f32[5,16,128]{2,1,0:T(8,128)S(1)} %get-tuple-element.37), channel_id=1, source_target_pairs={{0,1},{1,2},{2,3},{3,4},{4,5},{5,6},{6,7},{7,8},{8,9},{9,10},{10,1... | collective-permute-start | bytes 122888 | tf_op jit(solution)/shard_map/ppermute | solution.py:628
  58.7 9.3 %collective-permute-start.7 = (f32[5,16,128]{2,1,0:T(8,128)S(1)}, f32[5,16,128]{2,1,0:T(8,128)S(1)}, u32[]{:S(2)}, u32[]{:S(2)}) collective-permute-start(f32[5,16,128]{2,1,0:T(8,128)S(1)} %get-tuple-element.38), channel_id=1, source_target_pairs={{1,0},{2,1},{3,2},{4,3},{5,4},{6,5},{7,6},{8,7},{9,8},{10,9},{11,1... | collective-permute-start | bytes 122888 | tf_op jit(solution)/shard_map/ppermute | solution.py:628
  70.5 33.8 %collective-permute-start.8 = (f32[3,16,128]{2,1,0:T(8,128)S(1)}, f32[3,16,128]{2,1,0:T(8,128)S(1)}, u32[]{:S(2)}, u32[]{:S(2)}) collective-permute-start(f32[3,16,128]{2,1,0:T(8,128)S(1)} %get-tuple-element.41), channel_id=1, source_target_pairs={{0,16},{16,32},{32,48},{48,64},{64,80},{80,96},{96,112},{112,128},... | collective-permute-start | bytes 73736 | tf_op jit(solution)/shard_map/ppermute | solution.py:628
  72.4 31.9 %collective-permute-start.9 = (f32[3,16,128]{2,1,0:T(8,128)S(1)}, f32[3,16,128]{2,1,0:T(8,128)S(1)}, u32[]{:S(2)}, u32[]{:S(2)}) collective-permute-start(f32[3,16,128]{2,1,0:T(8,128)S(1)} %get-tuple-element.42), channel_id=1, source_target_pairs={{16,0},{32,16},{48,32},{64,48},{80,64},{96,80},{112,96},{128,112},... | collective-permute-start | bytes 73736 | tf_op jit(solution)/shard_map/ppermute | solution.py:628
  100.4 12.7 %all-to-all-start.1 = ((f32[32,1,128]{2,1,0:T(1,128)}), f32[32,1,128]{2,1,0:T(1,128)S(1)}, u32[]{:S(2)}, u32[]{:S(2)}) async-start(f32[32,1,128]{2,1,0:T(1,128)} %broadcast_in_dim.5), calls=%async_computation.1 | async-start | bytes 32768 | tf_op jit(solution)/shard_map/all_to_all | solution.py:635
  104.3 9.4 %collective-permute-start.10 = (f32[3,16,128]{2,1,0:T(8,128)S(1)}, f32[3,16,128]{2,1,0:T(8,128)S(1)}, u32[]{:S(2)}, u32[]{:S(2)}) collective-permute-start(f32[3,16,128]{2,1,0:T(8,128)S(1)} %get-tuple-element.43), channel_id=1, source_target_pairs={{0,1},{1,2},{2,3},{3,4},{4,5},{5,6},{6,7},{7,8},{8,9},{9,10},{10,1... | collective-permute-start | bytes 73736 | tf_op jit(solution)/shard_map/ppermute | solution.py:628
  107.1 9.1 %collective-permute-start.11 = (f32[3,16,128]{2,1,0:T(8,128)S(1)}, f32[3,16,128]{2,1,0:T(8,128)S(1)}, u32[]{:S(2)}, u32[]{:S(2)}) collective-permute-start(f32[3,16,128]{2,1,0:T(8,128)S(1)} %get-tuple-element.44), channel_id=1, source_target_pairs={{1,0},{2,1},{3,2},{4,3},{5,4},{6,5},{7,6},{8,7},{9,8},{10,9},{11,1... | collective-permute-start | bytes 73736 | tf_op jit(solution)/shard_map/ppermute | solution.py:628
  113.2 4.5 %copy-start.6 = (f32[128]{0:T(128)}, f32[128]{0:T(128)S(1)}, u32[]{:S(2)}) copy-start(f32[128]{0:T(128)S(1)} %reduce_sum.29) | copy-start | bytes 1540

commit v2 on v1

v2 whole, which is shorter than its diff:
```python
import math

import jax
import jax.numpy as jnp
from jax import lax
from jax.experimental import pallas as pl
from jax.experimental.pallas import tpu as pltpu
from jax.sharding import PartitionSpec as P

RAD = 3
REG = 8
VELOCITY = [
    (0, 0, 0),
    (1, 0, 0),
    (-1, 0, 0),
    (0, 1, 0),
    (0, -1, 0),
    (0, 0, 1),
    (0, 0, -1),
    (1, 1, 0),
    (-1, -1, 0),
    (1, -1, 0),
    (-1, 1, 0),
    (1, 0, 1),
    (-1, 0, -1),
    (1, 0, -1),
    (-1, 0, 1),
    (0, 1, 1),
    (0, -1, -1),
    (0, 1, -1),
    (0, -1, 1),
]
WEIGHTS = [1.0 / 3.0] + [1.0 / 18.0] * 6 + [1.0 / 36.0] * 12
OPPOSITE = [0, 2, 1, 4, 3, 6, 5, 8, 7, 10, 9, 12, 11, 14, 13, 16, 15, 18, 17]
RELAXATION = 1.0 / 0.6
BRINKMAN = 0.9
Q = 19
BX = 8
BY = 16
NZ = 128
F32 = jnp.float32

XP = tuple(i for i in range(Q) if VELOCITY[i][0] == 1)
XM = tuple(i for i in range(Q) if VELOCITY[i][0] == -1)
YP = tuple(i for i in range(Q) if VELOCITY[i][1] == 1)
YM = tuple(i for i in range(Q) if VELOCITY[i][1] == -1)

KIND, DENS, MOVING = 0, 1, 5
DEEP = RAD + 2


def sided(axis, sign, ring):
    keep = (lambda c: c >= 0) if ring == 0 else (lambda c: c > 0)
    go = [i for i in range(Q) if keep(sign * VELOCITY[i][axis])]
    come = [i for i in range(Q) if keep(-sign * VELOCITY[i][axis])]
    return go, come


SIZES = [MOVING + sum(map(len, sided(0, 1, ring))) for ring in (0, 1)]
BASES = (0, SIZES[0])
DESIGN = sum(SIZES)
MSG = DESIGN + DEEP
WIDE_ROWS = 24
FLAT = DESIGN * BY + DEEP * WIDE_ROWS


def slot(axis, sign, ring, field, which=None):
    base = BASES[ring]
    if field in ("go", "come"):
        go, come = sided(axis, sign, ring)
        listed = go if field == "go" else come
        if which not in listed:
            return None
        return base + MOVING + (0 if field == "go" else len(go)) + listed.index(which)
    return base + field


CLASSES = sorted(
    {a * a + b * b for a in range(RAD + 1) for b in range(RAD + 1) if a * a + b * b < (RAD + 1) ** 2}
)
TAPS = {
    s: [
        (a, b)
        for a in range(-RAD, RAD + 1)
        for b in range(-RAD, RAD + 1)
        if a * a + b * b == s
    ]
    for s in CLASSES
}


def tap_weight(s, c):
    return RAD + 1 - math.sqrt(s + c * c)


def lanes(shape):
    return lax.broadcasted_iota(jnp.int32, shape, len(shape) - 1)


def shift_z(value, c):
    if c == 0:
        return value
    z = lanes(value.shape)
    moved = pltpu.roll(value, (-c) % NZ, value.ndim - 1)
    return jnp.where((z + c >= 0) & (z + c < NZ), moved, 0.0)


def norm_row(shape):
    z = lanes(shape)
    result = None
    for c in range(RAD + 1):
        total = sum(len(TAPS[s]) * tap_weight(s, c) for s in CLASSES if tap_weight(s, c) > 0)
        if c == 0:
            result = jnp.full(shape, total, F32)
        else:
            result = result + jnp.where(z >= c, total, 0.0) + jnp.where(z < NZ - c, total, 0.0)
    return result


def filter_rows(load):
    sums = []
    for s in CLASSES:
        running = None
        for a, b in TAPS[s]:
            tile = load(a, b)
            running = tile if running is None else running + tile
        sums.append(running)
    result = None
    for c in range(RAD + 1):
        mixed = None
        for s, part in zip(CLASSES, sums):
            if tap_weight(s, c) > 0:
                term = tap_weight(s, c) * part
                mixed = term if mixed is None else mixed + term
        if c == 0:
            result = mixed
        else:
            result = result + shift_z(mixed, c) + shift_z(mixed, -c)
    return result


def add_all(values):
    values = list(values)
    while len(values) > 1:
        values = [
            values[k] + values[k + 1] if k + 1 < len(values) else values[k]
            for k in range(0, len(values), 2)
        ]
    return values[0]


def moments(p):
    momenta = []
    for a in range(3):
        up = add_all(p[i] for i in range(Q) if VELOCITY[i][a] == 1)
        down = add_all(p[i] for i in range(Q) if VELOCITY[i][a] == -1)
        momenta.append(up - down)
    return add_all(p), momenta


def along(i, vector):
    result = None
    for a in range(3):
        c = VELOCITY[i][a]
        if c == 0:
            continue
        if result is None:
            result = vector[a] if c == 1 else -vector[a]
        else:
            result = result + vector[a] if c == 1 else result - vector[a]
    return result


def post_tiles(which, straight, bounced, density, momenta, node, factor):
    inverse = 1.0 / density
    u = [factor * (m * inverse) for m in momenta]
    rest = 1.0 - 1.5 * (u[0] * u[0] + u[1] * u[1] + u[2] * u[2])
    rate = jnp.where(node <= 1.5, RELAXATION, 1.0)
    keep = 1.0 - rate
    wall = node == 2.0
    scale = rate * density
    result = {}
    for i in which:
        a = along(i, u)
        form = rest if a is None else rest + a * (3.0 + 4.5 * a)
        relaxed = keep * straight[i] + (WEIGHTS[i] * scale) * form
        result[i] = jnp.where(wall, bounced[i], relaxed)
    return result


def back_tiles(m, density, plain, node, factor):
    u = [factor * q for q in plain]
    rate = jnp.where(node <= 1.5, RELAXATION, 1.0)
    keep = 1.0 - rate
    wall = node == 2.0

    def weighted(select):
        total = None
        for w, group in ((1.0 / 18.0, range(1, 7)), (1.0 / 36.0, range(7, Q))):
            up = [m[i] for i in group if select(VELOCITY[i]) > 0]
            down = [m[i] for i in group if select(VELOCITY[i]) < 0]
            if not up and not down:
                continue
            value = add_all(up)
            if down:
                value = value - add_all(down)
            value = w * value
            total = value if total is None else total + value
        return total

    zero = (1.0 / 3.0) * m[0] + weighted(lambda c: 1)
    one = [weighted(lambda c, a=a: c[a]) for a in range(3)]
    two = {}
    for a in range(3):
        for b in range(a, 3):
            two[a, b] = two[b, a] = weighted(lambda c, a=a, b=b: c[a] * c[b])
    bent = [two[a, 0] * u[0] + two[a, 1] * u[1] + two[a, 2] * u[2] for a in range(3)]
    dot = lambda p, q: p[0] * q[0] + p[1] * q[1] + p[2] * q[2]
    scalar = zero * (1.0 - 1.5 * dot(u, u)) + 3.0 * dot(one, u) + 4.5 * dot(bent, u)
    vector = [3.0 * (one[a] + 3.0 * bent[a] - zero * u[a]) for a in range(3)]
    start = rate * (scalar - dot(vector, u))
    slope = [(rate * factor) * v for v in vector]
    result = []
    for i in range(Q):
        lean = along(i, slope)
        relaxed = keep * m[i] + (start if lean is None else start + lean)
        result.append(jnp.where(wall, m[OPPOSITE[i]], relaxed))
    gradient = jnp.where(wall, 0.0, rate * density * dot(vector, plain))
    return result, gradient


def whole(shape):
    return pl.BlockSpec(shape, lambda *_: (0,) * len(shape))


def scalar():
    return pl.BlockSpec(memory_space=pltpu.SMEM)


def anywhere():
    return pl.BlockSpec(memory_space=pl.ANY)


def call(body, outs, ins, specs, scratch=(), flops=1, name=None):
    size = sum(math.prod(o) for o in outs) * 4 + sum(math.prod(x.shape) for x in ins) * 4
    return pl.pallas_call(
        body,
        out_shape=[jax.ShapeDtypeStruct(o, F32) for o in outs],
        grid=(1,),
        in_specs=specs,
        out_specs=[whole(o) for o in outs],
        scratch_shapes=list(scratch),
        cost_estimate=pl.CostEstimate(flops=flops, bytes_accessed=size, transcendentals=0),
        compiler_params=pltpu.CompilerParams(vmem_limit_bytes=40 * 1024 * 1024),
        name=name,
    )(*ins)


def ring_fields(axis, sign, ring, p, node, later):
    density, momenta = moments(p)
    wall = node == 2.0
    go, come = sided(axis, sign, ring)
    fields = [node, density, *momenta]
    fields += [jnp.where(wall, p[OPPOSITE[i]], p[i]) for i in go]
    return fields + [later(i) for i in come]


def first_x_body(fwd_any, later_any, des, node, up_out, down_out, fwd, later, sems):
    copies = []
    for k, (source, target) in enumerate(((fwd_any, fwd), (later_any, later))):
        for e in (0, 1):
            copies.append(
                pltpu.make_async_copy(
                    source.at[:, e * (BX - 2) : e * (BX - 2) + 2], target.at[:, 2 * e : 2 * e + 2], sems.at[k, e]
                )
            )
    for copy in copies:
        copy.start()
    up_out[DESIGN:] = des[BX - DEEP :]
    down_out[DESIGN:] = des[:DEEP]
    for copy in copies:
        copy.wait()
    for out, sign, planes in ((up_out, 1, (BX - 1, BX - 2)), (down_out, -1, (0, 1))):
        for ring, x in enumerate(planes):
            at = x if x < 2 else x - (BX - 4)
            for h in (0, 8):
                rows = slice(h, h + 8)
                fields = ring_fields(
                    0,
                    sign,
                    ring,
                    [fwd[i, at, rows, :] for i in range(Q)],
                    node[x, rows, :].astype(F32),
                    lambda i, at=at, rows=rows: later[i, at, rows, :],
                )
                for k, value in enumerate(fields):
                    out[BASES[ring] + k, rows, :] = value


def first_x(fwd, later, design, node):
    return call(
        first_x_body,
        [(MSG, BY, NZ)] * 2,
        (fwd, later, design, node),
        [pl.BlockSpec(memory_space=pltpu.HBM)] * 2 + [whole(design.shape), whole(node.shape)],
        scratch=(
            pltpu.VMEM((Q, 4, BY, NZ), F32),
            pltpu.VMEM((Q, 4, BY, NZ), F32),
            pltpu.SemaphoreType.DMA((2, 2)),
        ),
        flops=400000,
        name="first_x",
    )


def first_y_body(fwd, later, design, node, up_out, down_out):
    for out, sign, lines, deep in (
        (up_out, 1, (BY - 1, BY - 2), range(BY - DEEP, BY)),
        (down_out, -1, (0, 1), range(DEEP)),
    ):
        for k, y in enumerate(deep):
            out[DESIGN + k] = design[:, y, :]
        for ring, y in enumerate(lines):
            fields = ring_fields(
                1,
                sign,
                ring,
                [fwd[i, :, y, :] for i in range(Q)],
                node[:, y, :].astype(F32),
                lambda i, y=y: later[i, :, y, :],
            )
            for k, value in enumerate(fields):
                out[BASES[ring] + k] = value


def first_y(fwd, later, design, node):
    ins = (fwd, later, design, node)
    return call(
        first_y_body, [(MSG, BX, NZ)] * 2, ins, [whole(x.shape) for x in ins], flops=800000, name="first_y"
    )


def by_parity(odd, up, down, near_out, far_out):
    @pl.when(odd[0] == 0)
    def _():
        near_out[...] = up[...]
        far_out[...] = down[...]

    @pl.when(odd[0] == 1)
    def _():
        near_out[...] = down[...]
        far_out[...] = up[...]


def to_sides(odd, near, far, low, high):
    @pl.when(odd[0] == 0)
    def _():
        high[...] = near[...]
        low[...] = far[...]

    @pl.when(odd[0] == 1)
    def _():
        low[...] = near[...]
        high[...] = far[...]


def join_y_body(odd, own_up, own_down, low, high, near_out, far_out, up_out, down_out):
    for out, own, sign, lines, deep in (
        (up_out, own_up, 1, (BY - 1, BY - 2), range(BY - DEEP, BY)),
        (down_out, own_down, -1, (0, 1), range(DEEP)),
    ):
        out[...] = jnp.zeros_like(out)
        for k, y in enumerate(deep):
            base = DESIGN * BY + k * WIDE_ROWS
            out[base + DEEP : base + DEEP + BX, :] = own[DESIGN + k]
            for x in range(DEEP):
                out[base + x : base + x + 1, :] = low[DESIGN + x, y : y + 1, :]
                at = base + DEEP + BX + x
                out[at : at + 1, :] = high[DESIGN + x, y : y + 1, :]
        for ring, y in enumerate(lines):
            go, come = sided(1, sign, ring)
            fields = [(f, None) for f in range(MOVING)] + [("go", i) for i in go] + [("come", i) for i in come]
            for k, (field, i) in enumerate(fields):
                base = (BASES[ring] + k) * BY
                out[base + 2 : base + 2 + BX, :] = own[BASES[ring] + k]
                for source, side, places in ((low, 1, (1, 0)), (high, -1, (2 + BX, 3 + BX))):
                    for other in (0, 1):
                        found = slot(0, side, other, field, i)
                        if found is not None:
                            at = base + places[other]
                            out[at : at + 1, :] = source[found, y : y + 1, :]
    by_parity(odd, up_out, down_out, near_out, far_out)


def join_y(odd, own_up, own_down, low, high):
    ins = (odd, own_up, own_down, low, high)
    return call(
        join_y_body,
        [(FLAT, NZ)] * 2,
        ins,
        [scalar()] + [whole(x.shape) for x in ins[1:]],
        scratch=(pltpu.VMEM((FLAT, NZ), F32),) * 2,
        flops=80000,
        name="join_y",
    )


EX = BX + 4
ROW = 8
PADY = 32


def main_body(
    odd, fwd, later_any, design, node, region, xlow, xhigh, near, far,
    adjoint, raw, part, up_out, down_out,
    ylow, yhigh, wide, kinds, fine, post, later, mid, flow, flux, first, sem,
):
    copy = pltpu.make_async_copy(later_any, later.at[:, 2 : 2 + BX, ROW : ROW + BY, :], sem)
    copy.start()
    to_sides(odd, near, far, ylow, yhigh)
    wide[...] = jnp.zeros_like(wide)
    wide[DEEP : DEEP + BX, ROW : ROW + BY, :] = design[...]
    wide[0:DEEP, ROW : ROW + BY, :] = xlow[DESIGN:]
    wide[DEEP + BX :, ROW : ROW + BY, :] = xhigh[DESIGN:]
    for j in range(DEEP):
        for x in range(BX + 2 * DEEP):
            at = DESIGN * BY + j * WIDE_ROWS + x
            wide[x, ROW - DEEP + j : ROW - DEEP + j + 1, :] = ylow[at : at + 1, :]
            wide[x, ROW + BY + j : ROW + BY + j + 1, :] = yhigh[at : at + 1, :]
    xrings = ((1, xlow, 1, 0), (0, xlow, 1, 1), (2 + BX, xhigh, -1, 0), (3 + BX, xhigh, -1, 1))
    yrings = ((ROW - 1, ylow, 1, 0), (ROW - 2, ylow, 1, 1), (ROW + BY, yhigh, -1, 0), (ROW + BY + 1, yhigh, -1, 1))
    kinds[...] = jnp.zeros_like(kinds)
    kinds[2 : 2 + BX, ROW : ROW + BY, :] = node[...].astype(F32)
    for x, message, sign, ring in xrings:
        kinds[x, ROW : ROW + BY, :] = message[slot(0, sign, ring, KIND)]
    for row, message, sign, ring in yrings:
        base = slot(1, sign, ring, KIND) * BY
        for x in range(EX):
            kinds[x, row : row + 1, :] = message[base + x : base + x + 1, :]
    inverse_norm = 1.0 / norm_row((8, NZ))

    def filter_plane(x, carry):
        for r in (4, 12, 20):
            value = filter_rows(lambda a, b: wide[x + RAD + a, r + b : r + b + 8, :]) * inverse_norm
            fine[x, r : r + 8, :] = value
        return carry

    lax.fori_loop(0, EX, filter_plane, 0)

    def factor_of(kind, filtered):
        return jnp.where(kind == 1.0, 1.0 - BRINKMAN * (1.0 - filtered), 1.0)

    for x, message, sign, ring in xrings:
        comps = sided(0, sign, ring)[0]
        for h in (0, 8):
            rows = slice(h, h + 8)
            padded = slice(ROW + h, ROW + h + 8)
            kind = kinds[x, padded, :]
            q = {i: message[slot(0, sign, ring, "go", i), rows, :] for i in comps}
            base = slot(0, sign, ring, DENS)
            value = post_tiles(
                comps, q, q, message[base, rows, :], [message[base + 1 + a, rows, :] for a in range(3)],
                kind, factor_of(kind, fine[x, padded, :]),
            )
            for i in comps:
                post[i, x, padded, :] = value[i]
    for row, message, sign, ring in yrings:
        comps = sided(1, sign, ring)[0]
        kind = kinds[:, row, :]

        def line(k, message=message):
            return message[k * BY : k * BY + EX, :]

        q = {i: line(slot(1, sign, ring, "go", i)) for i in comps}
        base = slot(1, sign, ring, DENS)
        value = post_tiles(
            comps, q, q, line(base), [line(base + 1 + a) for a in range(3)],
            kind, factor_of(kind, fine[:, row, :]),
        )
        for i in comps:
            for x in range(EX):
                post[i, x, row : row + 1, :] = value[i][x : x + 1, :]

    def post_plane(x, carry):
        carry = list(carry)
        for h in (0, 8):
            rows = slice(h, h + 8)
            padded = slice(ROW + h, ROW + h + 8)
            p = [fwd[i, x, rows, :] for i in range(Q)]
            density, momenta = moments(p)
            kind = kinds[x + 2, padded, :]
            filtered = fine[x + 2, padded, :]
            inverse = 1.0 / density
            flow[0, x, rows, :] = density
            for a in range(3):
                flow[1 + a, x, rows, :] = momenta[a] * inverse
            bounced = [p[OPPOSITE[i]] for i in range(Q)]
            value = post_tiles(range(Q), p, bounced, density, momenta, kind, factor_of(kind, filtered))
            for i in range(Q):
                post[i, x + 2, padded, :] = value[i]
            counted = jnp.where(kind == 1.0, filtered, 0.0)
            where_region = region[x, rows, :]
            for r in range(REG):
                carry[r] = carry[r] + jnp.where(where_region == r, counted, 0.0)
        return tuple(carry)

    empty = jnp.zeros((8, NZ), F32)
    totals = lax.fori_loop(0, BX, post_plane, (empty,) * REG)
    for r in range(REG):
        part[r] = totals[r]

    copy.wait()
    for x, message, sign, ring in xrings:
        for i in sided(0, sign, ring)[1]:
            later[i, x, ROW : ROW + BY, :] = message[slot(0, sign, ring, "come", i)]
    for row, message, sign, ring in yrings:
        for i in sided(1, sign, ring)[1]:
            base = slot(1, sign, ring, "come", i) * BY
            for x in range(EX):
                later[i, x, row : row + 1, :] = message[base + x : base + x + 1, :]

    def mid_plane(x, carry):
        for start in (ROW - 1, ROW + 7, ROW + 15):
            rows = slice(start, start + 8)
            density, mx, my, mz = 0.0, 0.0, 0.0, 0.0
            for cz in (0, 1, -1):
                p = {}
                for i in range(Q):
                    if VELOCITY[i][2] == cz:
                        at = start - VELOCITY[i][1]
                        p[i] = post[i, x + 1 - VELOCITY[i][0], at : at + 8, :]
                whole_sum = shift_z(add_all(p.values()), -cz)
                density = density + whole_sum
                if cz:
                    mz = mz + cz * whole_sum
                sides = []
                for a in range(2):
                    up = add_all(p[i] for i in p if VELOCITY[i][a] == 1)
                    down = add_all(p[i] for i in p if VELOCITY[i][a] == -1)
                    sides.append(shift_z(up - down, -cz))
                mx = mx + sides[0]
                my = my + sides[1]
            kind = kinds[x + 1, rows, :]
            outlet = kind == 4.0
            flux[x, rows, :] = jnp.where(outlet, mx, 0.0)
            inverse = 1.0 / density
            m = []
            for i in range(Q):
                at = start + VELOCITY[i][1]
                m.append(shift_z(later[i, x + 1 + VELOCITY[i][0], at : at + 8, :], VELOCITY[i][2]))
            value, gradient = back_tiles(
                m, density, [mx * inverse, my * inverse, mz * inverse], kind,
                factor_of(kind, fine[x + 1, rows, :]),
            )
            source = jnp.where(outlet, 1.0, 0.0)
            for i in range(Q):
                c = VELOCITY[i][0]
                mid[i, x, rows, :] = value[i] + c * source if c else value[i]
            first[x, rows, :] = gradient
        return carry

    lax.fori_loop(0, BX + 2, mid_plane, 0)
    raw_scale = BRINKMAN * inverse_norm

    def last_plane(x, carry):
        for h in (0, 8):
            rows = slice(h, h + 8)
            padded = slice(ROW + h, ROW + h + 8)
            kind = kinds[x + 2, padded, :]
            carry = carry + flux[x + 1, padded, :]
            m = []
            for i in range(Q):
                at = ROW + h + VELOCITY[i][1]
                m.append(shift_z(mid[i, x + 1 + VELOCITY[i][0], at : at + 8, :], VELOCITY[i][2]))
            value, gradient = back_tiles(
                m, flow[0, x, rows, :], [flow[1 + a, x, rows, :] for a in range(3)], kind,
                factor_of(kind, fine[x + 2, padded, :]),
            )
            for i in range(Q):
                adjoint[i, x, rows, :] = value[i]
            both = (first[x + 1, padded, :] + gradient) * raw_scale
            raw[x, rows, :] = jnp.where(kind == 1.0, both, 0.0)
        return carry

    part[REG] = lax.fori_loop(0, BX, last_plane, empty)
    up_out[...] = raw[BX - RAD :]
    down_out[...] = raw[:RAD]


def main(odd, fwd, later, design, node, region, xlow, xhigh, near, far):
    ins = (odd, fwd, later, design, node, region, xlow, xhigh, near, far)
    specs = [scalar()] + [whole(x.shape) for x in ins[1:]]
    specs[2] = anywhere()
    return call(
        main_body,
        [(Q, BX, BY, NZ), (BX, BY, NZ), (REG + 1, 8, NZ), (RAD, BY, NZ), (RAD, BY, NZ)],
        ins,
        specs,
        scratch=(
            pltpu.VMEM((FLAT, NZ), F32),
            pltpu.VMEM((FLAT, NZ), F32),
            pltpu.VMEM((BX + 2 * DEEP, PADY, NZ), F32),
            pltpu.VMEM((EX, PADY, NZ), F32),
            pltpu.VMEM((EX, PADY, NZ), F32),
            pltpu.VMEM((Q, EX, PADY, NZ), F32),
            pltpu.VMEM((Q, EX, PADY, NZ), F32),
            pltpu.VMEM((Q, BX + 2, PADY, NZ), F32),
            pltpu.VMEM((4, BX, BY, NZ), F32),
            pltpu.VMEM((BX + 2, PADY, NZ), F32),
            pltpu.VMEM((BX + 2, PADY, NZ), F32),
            pltpu.SemaphoreType.DMA,
        ),
        flops=30000000,
        name="main",
    )


def raw_y_body(odd, raw, low, high, near_out, far_out, up_out, down_out):
    for out, begin in ((up_out, BY - RAD), (down_out, 0)):
        out[...] = jnp.zeros_like(out)
        for j in range(RAD):
            out[j, RAD : RAD + BX, :] = raw[:, begin + j, :]
            for x in range(RAD):
                out[j, x : x + 1, :] = low[x, begin + j : begin + j + 1, :]
                out[j, RAD + BX + x : RAD + BX + x + 1, :] = high[x, begin + j : begin + j + 1, :]
    by_parity(odd, up_out, down_out, near_out, far_out)


def raw_y(odd, raw, low, high):
    ins = (odd, raw, low, high)
    return call(
        raw_y_body,
        [(RAD, BY, NZ)] * 2,
        ins,
        [scalar()] + [whole(x.shape) for x in ins[1:]],
        scratch=(pltpu.VMEM((RAD, BY, NZ), F32),) * 2,
        flops=20000,
        name="raw_y",
    )


def spread_body(odd, raw, xlow, xhigh, near, far, out, ylow, yhigh, wide):
    to_sides(odd, near, far, ylow, yhigh)
    wide[RAD : RAD + BX, ROW : ROW + BY, :] = raw[...]
    wide[0:RAD, ROW : ROW + BY, :] = xlow[...]
    wide[RAD + BX :, ROW : ROW + BY, :] = xhigh[...]
    for x in range(BX + 2 * RAD):
        for j in range(RAD):
            wide[x, ROW - RAD + j : ROW - RAD + j + 1, :] = ylow[j, x : x + 1, :]
            wide[x, ROW + BY + j : ROW + BY + j + 1, :] = yhigh[j, x : x + 1, :]

    def plane(x, carry):
        for h in (0, 8):
            at = ROW + h
            out[x, h : h + 8, :] = filter_rows(lambda a, b: wide[x + RAD + a, at + b : at + b + 8, :])
        return carry

    lax.fori_loop(0, BX, plane, 0)


def spread(odd, raw, xlow, xhigh, near, far):
    ins = (odd, raw, xlow, xhigh, near, far)
    return call(
        spread_body,
        [(BX, BY, NZ)],
        ins,
        [scalar()] + [whole(x.shape) for x in ins[1:]],
        scratch=(pltpu.VMEM((RAD, BY, NZ), F32),) * 2 + (pltpu.VMEM((BX + 2 * RAD, PADY, NZ), F32),),
        flops=2000000,
        name="spread",
    )[0]


def exchange(up, down, axis):
    count = lax.axis_size(axis)
    forward = [(i, (i + 1) % count) for i in range(count)]
    backward = [(j, i) for i, j in forward]
    return lax.ppermute(up, axis, forward), lax.ppermute(down, axis, backward)


def swap(near, far, axis):
    count = lax.axis_size(axis)
    inner = [(i, i ^ 1) for i in range(count)]
    outer = [(i, (i + 1 if i % 2 else i - 1) % count) for i in range(count)]
    return lax.ppermute(near, axis, inner), lax.ppermute(far, axis, outer)


def total(row):
    axes = ("gx", "gy")
    count = lax.axis_size(axes)
    rows = jnp.broadcast_to(row[None], (count,) + row.shape)
    return jnp.sum(lax.all_to_all(rows, axes, 0, 0, tiled=True), axis=0)


def per_device(forward_pops, later_adjoint, design, node_type, region):
    odd = jnp.reshape(lax.axis_index("gy") % 2, (1,)).astype(jnp.int32)
    up, down = first_x(forward_pops, later_adjoint, design, node_type)
    own_up, own_down = first_y(forward_pops, later_adjoint, design, node_type)
    xlow, xhigh = exchange(up, down, "gx")
    near, far = swap(*join_y(odd, own_up, own_down, xlow, xhigh), "gy")
    adjoint, raw, part, up, down = main(
        odd, forward_pops, later_adjoint, design, node_type, region, xlow, xhigh, near, far
    )
    sums = total(jnp.pad(jnp.sum(part, axis=(1, 2)), (0, NZ - REG - 1)))
    xlow, xhigh = exchange(up, down, "gx")
    near, far = swap(*raw_y(odd, raw, xlow, xhigh), "gy")
    sensitivity = spread(odd, raw, xlow, xhigh, near, far)
    return adjoint, sensitivity, sums[REG], sums[:REG]


def solution(mesh):
    cells = P("gx", "gy", None)
    pops = P(None, "gx", "gy", None)
    return jax.shard_map(
        per_device,
        mesh=mesh,
        in_specs=(pops, pops, cells, cells, cells),
        out_specs=(pops, cells, P(), P()),
        check_vma=False,
    )
```

time: 119 us -> 117 us (0.983)
  blocking collectives: 19.3 us -> 0 us
  starting transfers between devices: 57.8 us -> 65.6 us
  waiting for transfers between devices: 26 us -> 30.2 us
  Pallas kernels: 8.06 us -> 11 us
  local copies, waits for them, and re-layouts: 5.49 us -> 7.51 us
    ppermute x12 -> x4, starting transfers between devices: 54 us -> 24.3 us  [exchange(): return (lax.ppermute(up, axis, forward), lax.ppermute(down, axis, backward))]
    ppermute x0 -> x4, starting transfers between devices: none -> 24.4 us  [swap(): return (lax.ppermute(near, axis, inner), lax.ppermute(far, axis, outer))]
    ppermute x0 -> x4, waiting for transfers between devices: none -> 23.2 us  [swap(): return (lax.ppermute(near, axis, inner), lax.ppermute(far, axis, outer))]
    all_to_all x1 -> x0, blocking collectives: 19.3 us -> none  [total(): row = jnp.sum(lax.all_to_all(rows, axis, 0, 0, tiled=True), axis=0)]
    ppermute x12 -> x4, waiting for transfers between devices: 21.8 us -> 7 us  [exchange(): return (lax.ppermute(up, axis, forward), lax.ppermute(down, axis, backward))]
    all_to_all x1, starting transfers between devices: 3.83 us -> 16.9 us  [total(): return jnp.sum(lax.all_to_all(rows, axes, 0, 0, tiled=True), axis=0)]
    all_to_all x1, waiting for transfers between devices: 4.13 us -> 0.01 us  [total(): return jnp.sum(lax.all_to_all(rows, axes, 0, 0, tiled=True), axis=0)]
    pallas_call x8 -> x6, Pallas kernels: 8.06 us -> 11 us  [call(): pl.pallas_call(body, out_shape=[jax.ShapeDtypeStruct(o, F32) for o in out...]
  transfers between devices with their start and end apart: 13 -> 9, of which waited for: 8 -> 6; matrix products, arithmetic and copies ran while one was open for 1% -> 0% of each run, Pallas kernels for 0% -> 2%
where the time goes in v2:
time: 117 us; the launch traced here: 116 us
  starting transfers between devices  65.6 us (56%)
  waiting for transfers between devices  30.2 us (26%)
  Pallas kernels  11 us (9%)
  local copies, waits for them, and re-layouts  7.51 us (6%)
    ppermute x4, starting transfers between devices, swap(): return (lax.ppermute(near, axis, inner), lax.ppermute(far, axis, outer))  24.4 us
    ppermute x4, starting transfers between devices, exchange(): return (lax.ppermute(up, axis, forward), lax.ppermute(down, axis, backward))  24.3 us
    ppermute x4, waiting for transfers between devices, swap(): return (lax.ppermute(near, axis, inner), lax.ppermute(far, axis, outer))  23.2 us
    all_to_all x1, starting transfers between devices, total(): return jnp.sum(lax.all_to_all(rows, axes, 0, 0, tiled=True), axis=0)  16.9 us
    pallas_call x6, Pallas kernels, call(): pl.pallas_call(body, out_shape=[jax.ShapeDtypeStruct(o, F32) for o in out...  11 us
    ppermute x4, waiting for transfers between devices, exchange(): return (lax.ppermute(up, axis, forward), lax.ppermute(down, axis, backward))  7 us
    unnamed x26, local copies, waits for them, and re-layouts  6.08 us
  transfers between devices with their start and end apart: 9, of which 6 were waited for; matrix products, arithmetic and copies ran while one was open for 0% of the time, Pallas kernels for 2%

profile of v2, /device:TPU:1, one launch (start us, length us, event | category | flops | bytes accessed | tf_op | source)
XLA Modules:
  0.0 116.2 jit_solution(8682267140379238233)
XLA Ops:
  0.6 1.3 %copy-done = f32[19,8,16,128]{3,2,1,0:T(8,128)S(1)} copy-done((f32[19,8,16,128]{3,2,1,0:T(8,128)S(1)}, f32[19,8,16,128]{3,2,1,0:T(8,128)}, u32[]{:S(2)}) %copy-start) | copy-done | bytes 1245208
  1.9 1.3 %copy-done.2 = f32[19,8,16,128]{3,2,1,0:T(8,128)S(1)} copy-done((f32[19,8,16,128]{3,2,1,0:T(8,128)S(1)}, f32[19,8,16,128]{3,2,1,0:T(8,128)}, u32[]{:S(2)}) %copy-start.2) | copy-done | bytes 1245208
  3.2 0.8 copy-done.4
  4.1 0.8 copy-done.6
  4.9 1.1 first_x.1
  6.0 4.0 %collective-permute-start = (f32[53,16,128]{2,1,0:T(8,128)}, f32[53,16,128]{2,1,0:T(8,128)S(1)}, u32[]{:S(2)}, u32[]{:S(2)}) collective-permute-start(f32[53,16,128]{2,1,0:T(8,128)} %get-tuple-element.17), channel_id=1, source_target_pairs={{0,16},{16,32},{32,48},{48,64},{64,80},{80,96},{96,112},{112,128},... | collective-permute-start | bytes 1302536 | tf_op jit(solution)/shard_map/ppermute | solution.py:678
  10.0 9.2 %collective-permute-start.1 = (f32[53,16,128]{2,1,0:T(8,128)}, f32[53,16,128]{2,1,0:T(8,128)S(1)}, u32[]{:S(2)}, u32[]{:S(2)}) collective-permute-start(f32[53,16,128]{2,1,0:T(8,128)} %get-tuple-element.18), channel_id=1, source_target_pairs={{16,0},{32,16},{48,32},{64,48},{80,64},{96,80},{112,96},{128,112},... | collective-permute-start | bytes 1302536 | tf_op jit(solution)/shard_map/ppermute | solution.py:678
  19.9 4.9 %collective-permute-done.low.xlow = f32[53,16,128]{2,1,0:T(8,128)S(1)} collective-permute-done((f32[53,16,128]{2,1,0:T(8,128)}, f32[53,16,128]{2,1,0:T(8,128)S(1)}, u32[]{:S(2)}, u32[]{:S(2)}) %collective-permute-start) | collective-permute-done | bytes 434208 | tf_op jit(solution)/shard_map/ppermute | solution.py:678
  24.8 1.0 collective-permute-done.1.high.xhigh
  26.1 5.9 %collective-permute-start.2 = (f32[888,128]{1,0:T(8,128)S(1)}, f32[888,128]{1,0:T(8,128)S(1)}, u32[]{:S(2)}, u32[]{:S(2)}) collective-permute-start(f32[888,128]{1,0:T(8,128)S(1)} %get-tuple-element.21), channel_id=1, source_target_pairs={{0,1},{1,0},{2,3},{3,2},{4,5},{5,4},{6,7},{7,6},{8,9},{9,8},{10,11... | collective-permute-start | bytes 1363976 | tf_op jit(solution)/shard_map/ppermute | solution.py:685
  32.0 7.8 %collective-permute-start.3 = (f32[888,128]{1,0:T(8,128)S(1)}, f32[888,128]{1,0:T(8,128)S(1)}, u32[]{:S(2)}, u32[]{:S(2)}) collective-permute-start(f32[888,128]{1,0:T(8,128)S(1)} %get-tuple-element.22), channel_id=1, source_target_pairs={{0,15},{1,2},{2,1},{3,4},{4,3},{5,6},{6,5},{7,8},{8,7},{9,10},{10,... | collective-permute-start | bytes 1363976 | tf_op jit(solution)/shard_map/ppermute | solution.py:685
  39.8 19.2 %collective-permute-done.3.far = f32[888,128]{1,0:T(8,128)S(1)} collective-permute-done((f32[888,128]{1,0:T(8,128)S(1)}, f32[888,128]{1,0:T(8,128)S(1)}, u32[]{:S(2)}, u32[]{:S(2)}) %collective-permute-start.3) | collective-permute-done | bytes 454688 | tf_op jit(solution)/shard_map/ppermute | solution.py:685
  59.0 7.5 %main.1 = (f32[19,8,16,128]{3,2,1,0:T(8,128)}, f32[8,16,128]{2,1,0:T(8,128)S(1)}, f32[9,8,128]{2,1,0:T(8,128)S(1)}, f32[3,16,128]{2,1,0:T(8,128)S(1)}, f32[3,16,128]{2,1,0:T(8,128)S(1)}) custom-call(s32[1]{0:T(128)} %bitcast.odd, f32[19,8,16,128]{3,2,1,0:T(8,128)S(1)} %copy-done.1, f32[19,8,16,128]{3,2,1,0:T(8,128)S(1)} %copy-done.3, ...), custom_call_target="tpu_custom_call" | custom-call | flops 30000000 | bytes 5861380 | tf_op jit(solution)/shard_map/main/pallas_call | solution.py:246
  66.6 0.6 copy-done.9
  68.4 0.9 reduce_sum.18
  69.3 0.8 broadcast_in_dim.2
  70.1 16.9 %all-to-all-start = ((f32[512,1,128]{2,1,0:T(1,128)}), f32[512,1,128]{2,1,0:T(1,128)S(1)}, u32[]{:S(2)}, u32[]{:S(2)}) async-start(f32[512,1,128]{2,1,0:T(1,128)} %broadcast_in_dim.2), calls=%async_computation | async-start | bytes 524288 | tf_op jit(solution)/shard_map/all_to_all | solution.py:692
  87.0 3.3 %collective-permute-start.4 = (f32[3,16,128]{2,1,0:T(8,128)}, f32[3,16,128]{2,1,0:T(8,128)S(1)}, u32[]{:S(2)}, u32[]{:S(2)}) collective-permute-start(f32[3,16,128]{2,1,0:T(8,128)} %copy-done.11), channel_id=1, source_target_pairs={{0,16},{16,32},{32,48},{48,64},{64,80},{80,96},{96,112},{112,128},... | collective-permute-start | bytes 73736 | tf_op jit(solution)/shard_map/ppermute | solution.py:678
  90.3 7.8 %collective-permute-start.5 = (f32[3,16,128]{2,1,0:T(8,128)}, f32[3,16,128]{2,1,0:T(8,128)S(1)}, u32[]{:S(2)}, u32[]{:S(2)}) collective-permute-start(f32[3,16,128]{2,1,0:T(8,128)} %copy-done.10), channel_id=1, source_target_pairs={{16,0},{32,16},{48,32},{64,48},{80,64},{96,80},{112,96},{128,112},... | collective-permute-start | bytes 73736 | tf_op jit(solution)/shard_map/ppermute | solution.py:678
  98.2 1.1 collective-permute-done.5.high.xhigh
  99.3 5.5 %collective-permute-start.6 = (f32[3,16,128]{2,1,0:T(8,128)S(1)}, f32[3,16,128]{2,1,0:T(8,128)S(1)}, u32[]{:S(2)}, u32[]{:S(2)}) collective-permute-start(f32[3,16,128]{2,1,0:T(8,128)S(1)} %get-tuple-element.27), channel_id=1, source_target_pairs={{0,1},{1,0},{2,3},{3,2},{4,5},{5,4},{6,7},{7,6},{8,9},{9,8},{10,11... | collective-permute-start | bytes 73736 | tf_op jit(solution)/shard_map/ppermute | solution.py:685
  104.8 5.2 %collective-permute-start.7 = (f32[3,16,128]{2,1,0:T(8,128)S(1)}, f32[3,16,128]{2,1,0:T(8,128)S(1)}, u32[]{:S(2)}, u32[]{:S(2)}) collective-permute-start(f32[3,16,128]{2,1,0:T(8,128)S(1)} %get-tuple-element.28), channel_id=1, source_target_pairs={{0,15},{1,2},{2,1},{3,4},{4,3},{5,6},{6,5},{7,8},{8,7},{9,10},{10,... | collective-permute-start | bytes 73736 | tf_op jit(solution)/shard_map/ppermute | solution.py:685
  110.0 4.0 %collective-permute-done.7.far = f32[3,16,128]{2,1,0:T(8,128)S(1)} collective-permute-done((f32[3,16,128]{2,1,0:T(8,128)S(1)}, f32[3,16,128]{2,1,0:T(8,128)S(1)}, u32[]{:S(2)}, u32[]{:S(2)}) %collective-permute-start.7) | collective-permute-done | bytes 24608 | tf_op jit(solution)/shard_map/ppermute | solution.py:685
  114.0 1.6 %spread.1 = f32[8,16,128]{2,1,0:T(8,128)} custom-call(s32[1]{0:T(128)} %bitcast.odd, f32[8,16,128]{2,1,0:T(8,128)S(1)} %get-tuple-element.24.raw, f32[3,16,128]{2,1,0:T(8,128)S(1)} %collective-permute-done.4.low.xlow, f32[3,16,128]{2,1,0:T(8,128)S(1)} %collective-permute-done.5.high.xhigh, f32[3,16,128]{2,1,0:T(8,128)S(1)} %collective-permute-done.6.near, ...), custom_call_target="tpu_custom_call" | custom-call | flops 2000000 | bytes 229380 | tf_op jit(solution)/shard_map/spread/pallas_call | solution.py:246
  (31 shorter events, 2.8 us)
Async XLA Ops:
  0.6 1.3 %copy-start = (f32[19,8,16,128]{3,2,1,0:T(8,128)S(1)}, f32[19,8,16,128]{3,2,1,0:T(8,128)}, u32[]{:S(2)}) copy-start(f32[19,8,16,128]{3,2,1,0:T(8,128)} %fwd.3) | copy-start | bytes 3735556
  1.9 1.3 %copy-start.2 = (f32[19,8,16,128]{3,2,1,0:T(8,128)S(1)}, f32[19,8,16,128]{3,2,1,0:T(8,128)}, u32[]{:S(2)}) copy-start(f32[19,8,16,128]{3,2,1,0:T(8,128)} %later_any.3) | copy-start | bytes 3735556
  3.2 0.8 copy-start.4
  4.1 0.8 copy-start.6
  4.9 14.4 %copy-start.1 = (f32[19,8,16,128]{3,2,1,0:T(8,128)S(1)}, f32[19,8,16,128]{3,2,1,0:T(8,128)}, u32[]{:S(2)}) copy-start(f32[19,8,16,128]{3,2,1,0:T(8,128)} %fwd.3) | copy-start | bytes 3735556
  4.9 14.4 %copy-start.3 = (f32[19,8,16,128]{3,2,1,0:T(8,128)S(1)}, f32[19,8,16,128]{3,2,1,0:T(8,128)}, u32[]{:S(2)}) copy-start(f32[19,8,16,128]{3,2,1,0:T(8,128)} %later_any.3) | copy-start | bytes 3735556
  4.9 14.4 %copy-start.5 = (f32[8,16,128]{2,1,0:T(8,128)S(1)}, f32[8,16,128]{2,1,0:T(8,128)}, u32[]{:S(2)}) copy-start(f32[8,16,128]{2,1,0:T(8,128)} %design.3) | copy-start | bytes 196612
  4.9 14.4 %copy-start.7 = (s32[8,16,128]{2,1,0:T(8,128)S(1)}, s32[8,16,128]{2,1,0:T(8,128)}, u32[]{:S(2)}) copy-start(s32[8,16,128]{2,1,0:T(8,128)} %node.5) | copy-start | bytes 196612
  6.0 18.8 %collective-permute-start = (f32[53,16,128]{2,1,0:T(8,128)}, f32[53,16,128]{2,1,0:T(8,128)S(1)}, u32[]{:S(2)}, u32[]{:S(2)}) collective-permute-start(f32[53,16,128]{2,1,0:T(8,128)} %get-tuple-element.17), channel_id=1, source_target_pairs={{0,16},{16,32},{32,48},{48,64},{64,80},{80,96},{96,112},{112,128},... | collective-permute-start | bytes 1302536 | tf_op jit(solution)/shard_map/ppermute | solution.py:678
  10.0 15.7 %collective-permute-start.1 = (f32[53,16,128]{2,1,0:T(8,128)}, f32[53,16,128]{2,1,0:T(8,128)S(1)}, u32[]{:S(2)}, u32[]{:S(2)}) collective-permute-start(f32[53,16,128]{2,1,0:T(8,128)} %get-tuple-element.18), channel_id=1, source_target_pairs={{16,0},{32,16},{48,32},{64,48},{80,64},{96,80},{112,96},{128,112},... | collective-permute-start | bytes 1302536 | tf_op jit(solution)/shard_map/ppermute | solution.py:678
  19.9 39.1 %copy-start.8 = (s32[8,16,128]{2,1,0:T(8,128)S(1)}, s32[8,16,128]{2,1,0:T(8,128)}, u32[]{:S(2)}) copy-start(s32[8,16,128]{2,1,0:T(8,128)} %region.1) | copy-start | bytes 196612
  26.1 13.8 %collective-permute-start.2 = (f32[888,128]{1,0:T(8,128)S(1)}, f32[888,128]{1,0:T(8,128)S(1)}, u32[]{:S(2)}, u32[]{:S(2)}) collective-permute-start(f32[888,128]{1,0:T(8,128)S(1)} %get-tuple-element.21), channel_id=1, source_target_pairs={{0,1},{1,0},{2,3},{3,2},{4,5},{5,4},{6,7},{7,6},{8,9},{9,8},{10,11... | collective-permute-start | bytes 1363976 | tf_op jit(solution)/shard_map/ppermute | solution.py:685
  32.0 27.1 %collective-permute-start.3 = (f32[888,128]{1,0:T(8,128)S(1)}, f32[888,128]{1,0:T(8,128)S(1)}, u32[]{:S(2)}, u32[]{:S(2)}) collective-permute-start(f32[888,128]{1,0:T(8,128)S(1)} %get-tuple-element.22), channel_id=1, source_target_pairs={{0,15},{1,2},{2,1},{3,4},{4,3},{5,6},{6,5},{7,8},{8,7},{9,10},{10,... | collective-permute-start | bytes 1363976 | tf_op jit(solution)/shard_map/ppermute | solution.py:685
  66.6 0.6 copy-start.9
  67.2 0.6 copy-start.10
  67.8 0.6 copy-start.11
  70.1 45.4 %all-to-all-start = ((f32[512,1,128]{2,1,0:T(1,128)}), f32[512,1,128]{2,1,0:T(1,128)S(1)}, u32[]{:S(2)}, u32[]{:S(2)}) async-start(f32[512,1,128]{2,1,0:T(1,128)} %broadcast_in_dim.2), calls=%async_computation | async-start | bytes 524288 | tf_op jit(solution)/shard_map/all_to_all | solution.py:692
  87.0 11.1 %collective-permute-start.4 = (f32[3,16,128]{2,1,0:T(8,128)}, f32[3,16,128]{2,1,0:T(8,128)S(1)}, u32[]{:S(2)}, u32[]{:S(2)}) collective-permute-start(f32[3,16,128]{2,1,0:T(8,128)} %copy-done.11), channel_id=1, source_target_pairs={{0,16},{16,32},{32,48},{48,64},{64,80},{80,96},{96,112},{112,128},... | collective-permute-start | bytes 73736 | tf_op jit(solution)/shard_map/ppermute | solution.py:678
  90.3 8.9 %collective-permute-start.5 = (f32[3,16,128]{2,1,0:T(8,128)}, f32[3,16,128]{2,1,0:T(8,128)S(1)}, u32[]{:S(2)}, u32[]{:S(2)}) collective-permute-start(f32[3,16,128]{2,1,0:T(8,128)} %copy-done.10), channel_id=1, source_target_pairs={{16,0},{32,16},{48,32},{64,48},{80,64},{96,80},{112,96},{128,112},... | collective-permute-start | bytes 73736 | tf_op jit(solution)/shard_map/ppermute | solution.py:678
  99.3 10.7 %collective-permute-start.6 = (f32[3,16,128]{2,1,0:T(8,128)S(1)}, f32[3,16,128]{2,1,0:T(8,128)S(1)}, u32[]{:S(2)}, u32[]{:S(2)}) collective-permute-start(f32[3,16,128]{2,1,0:T(8,128)S(1)} %get-tuple-element.27), channel_id=1, source_target_pairs={{0,1},{1,0},{2,3},{3,2},{4,5},{5,4},{6,7},{7,6},{8,9},{9,8},{10,11... | collective-permute-start | bytes 73736 | tf_op jit(solution)/shard_map/ppermute | solution.py:685
  104.8 9.2 %collective-permute-start.7 = (f32[3,16,128]{2,1,0:T(8,128)S(1)}, f32[3,16,128]{2,1,0:T(8,128)S(1)}, u32[]{:S(2)}, u32[]{:S(2)}) collective-permute-start(f32[3,16,128]{2,1,0:T(8,128)S(1)} %get-tuple-element.28), channel_id=1, source_target_pairs={{0,15},{1,2},{2,1},{3,4},{4,3},{5,6},{6,5},{7,8},{8,7},{9,10},{10,... | collective-permute-start | bytes 73736 | tf_op jit(solution)/shard_map/ppermute | solution.py:685
  115.6 0.6 copy-start.12

commit v3 on v2

--- a/solution.py
+++ b/solution.py
@@ -40,10 +40,6 @@
 NZ = 128
 F32 = jnp.float32
 
-XP = tuple(i for i in range(Q) if VELOCITY[i][0] == 1)
-XM = tuple(i for i in range(Q) if VELOCITY[i][0] == -1)
-YP = tuple(i for i in range(Q) if VELOCITY[i][1] == 1)
-YM = tuple(i for i in range(Q) if VELOCITY[i][1] == -1)
 
 KIND, DENS, MOVING = 0, 1, 5
 DEEP = RAD + 2
@@ -60,8 +56,14 @@
 BASES = (0, SIZES[0])
 DESIGN = sum(SIZES)
 MSG = DESIGN + DEEP
-WIDE_ROWS = 24
-FLAT = DESIGN * BY + DEEP * WIDE_ROWS
+LINE = BY + 4
+WIDE_LINE = BY + 2 * DEEP
+FLAT = (DESIGN * LINE + DEEP * WIDE_LINE + 7) // 8 * 8
+RAW_ROWS = RAD * BY
+
+
+def design_row(j):
+    return DESIGN * LINE + j * WIDE_LINE
 
 
 def slot(axis, sign, ring, field, which=None):
@@ -241,17 +243,17 @@
     return pl.BlockSpec(memory_space=pl.ANY)
 
 
-def call(body, outs, ins, specs, scratch=(), flops=1, name=None):
+def call(body, outs, ins, specs, scratch=(), flops=1, name=None, out_specs=None, vmem=40):
     size = sum(math.prod(o) for o in outs) * 4 + sum(math.prod(x.shape) for x in ins) * 4
     return pl.pallas_call(
         body,
         out_shape=[jax.ShapeDtypeStruct(o, F32) for o in outs],
         grid=(1,),
         in_specs=specs,
-        out_specs=[whole(o) for o in outs],
+        out_specs=out_specs or [whole(o) for o in outs],
         scratch_shapes=list(scratch),
         cost_estimate=pl.CostEstimate(flops=flops, bytes_accessed=size, transcendentals=0),
-        compiler_params=pltpu.CompilerParams(vmem_limit_bytes=40 * 1024 * 1024),
+        compiler_params=pltpu.CompilerParams(vmem_limit_bytes=vmem * 1024 * 1024),
         name=name,
     )(*ins)
 
@@ -265,55 +267,47 @@
     return fields + [later(i) for i in come]
 
 
-def first_x_body(fwd_any, later_any, des, node, up_out, down_out, fwd, later, sems):
-    copies = []
-    for k, (source, target) in enumerate(((fwd_any, fwd), (later_any, later))):
-        for e in (0, 1):
-            copies.append(
-                pltpu.make_async_copy(
-                    source.at[:, e * (BX - 2) : e * (BX - 2) + 2], target.at[:, 2 * e : 2 * e + 2], sems.at[k, e]
-                )
-            )
-    for copy in copies:
-        copy.start()
-    up_out[DESIGN:] = des[BX - DEEP :]
-    down_out[DESIGN:] = des[:DEEP]
-    for copy in copies:
-        copy.wait()
-    for out, sign, planes in ((up_out, 1, (BX - 1, BX - 2)), (down_out, -1, (0, 1))):
+def first_x_body(fwd, later, des, node, up_out, down_out):
+    for out, sign, planes, deep in (
+        (up_out, 1, (BX - 1, BX - 2), slice(BX - DEEP, BX)),
+        (down_out, -1, (0, 1), slice(0, DEEP)),
+    ):
+        out[DESIGN:] = des[deep]
         for ring, x in enumerate(planes):
-            at = x if x < 2 else x - (BX - 4)
             for h in (0, 8):
                 rows = slice(h, h + 8)
                 fields = ring_fields(
                     0,
                     sign,
                     ring,
-                    [fwd[i, at, rows, :] for i in range(Q)],
+                    [fwd[i, x, rows, :] for i in range(Q)],
                     node[x, rows, :].astype(F32),
-                    lambda i, at=at, rows=rows: later[i, at, rows, :],
+                    lambda i, x=x, rows=rows: later[i, x, rows, :],
                 )
                 for k, value in enumerate(fields):
                     out[BASES[ring] + k, rows, :] = value
 
 
 def first_x(fwd, later, design, node):
+    ins = (fwd, later, design, node)
     return call(
-        first_x_body,
-        [(MSG, BY, NZ)] * 2,
-        (fwd, later, design, node),
-        [pl.BlockSpec(memory_space=pltpu.HBM)] * 2 + [whole(design.shape), whole(node.shape)],
-        scratch=(
-            pltpu.VMEM((Q, 4, BY, NZ), F32),
-            pltpu.VMEM((Q, 4, BY, NZ), F32),
-            pltpu.SemaphoreType.DMA((2, 2)),
-        ),
-        flops=400000,
-        name="first_x",
+        first_x_body, [(MSG, BY, NZ)] * 2, ins, [whole(x.shape) for x in ins], flops=800000, name="first_x"
     )
 
 
-def first_y_body(fwd, later, design, node, up_out, down_out):
+CHUNKS = ((0, 5), (5, 10), (10, 15), (15, 19))
+
+
+def first_y_body(odd, fwd_any, later_any, design, node, near_out, far_out, fwd, later, up_out, down_out, sems):
+    copies = [
+        pltpu.make_async_copy(source.at[lo:hi], target.at[lo:hi], sems.at[k, c])
+        for c, (lo, hi) in enumerate(CHUNKS)
+        for k, (source, target) in enumerate(((fwd_any, fwd), (later_any, later)))
+    ]
+    for copy in copies:
+        copy.start()
+    for copy in copies:
+        copy.wait()
     for out, sign, lines, deep in (
         (up_out, 1, (BY - 1, BY - 2), range(BY - DEEP, BY)),
         (down_out, -1, (0, 1), range(DEEP)),
@@ -331,12 +325,26 @@
             )
             for k, value in enumerate(fields):
                 out[BASES[ring] + k] = value
-
-
-def first_y(fwd, later, design, node):
-    ins = (fwd, later, design, node)
+    by_parity(odd, up_out, down_out, near_out, far_out)
+
+
+def first_y(odd, fwd, later, design, node):
+    block = pltpu.VMEM(fwd.shape, F32)
     return call(
-        first_y_body, [(MSG, BX, NZ)] * 2, ins, [whole(x.shape) for x in ins], flops=800000, name="first_y"
+        first_y_body,
+        [(MSG, BX, NZ)] * 2,
+        (odd, fwd, later, design, node),
+        [scalar(), anywhere(), anywhere(), whole(design.shape), whole(node.shape)],
+        scratch=(
+            block,
+            block,
+            pltpu.VMEM((MSG, BX, NZ), F32),
+            pltpu.VMEM((MSG, BX, NZ), F32),
+            pltpu.SemaphoreType.DMA((2, len(CHUNKS))),
+        ),
+        flops=800000,
+        name="first_y",
+        vmem=60,
     )
 
 
@@ -364,44 +372,44 @@
         high[...] = far[...]
 
 
-def join_y_body(odd, own_up, own_down, low, high, near_out, far_out, up_out, down_out):
-    for out, own, sign, lines, deep in (
-        (up_out, own_up, 1, (BY - 1, BY - 2), range(BY - DEEP, BY)),
+def join_x_body(odd, own_up, own_down, near, far, up_out, down_out, low, high):
+    to_sides(odd, near, far, low, high)
+    for out, own, sign, planes, deep in (
+        (up_out, own_up, 1, (BX - 1, BX - 2), range(BX - DEEP, BX)),
         (down_out, own_down, -1, (0, 1), range(DEEP)),
     ):
         out[...] = jnp.zeros_like(out)
-        for k, y in enumerate(deep):
-            base = DESIGN * BY + k * WIDE_ROWS
-            out[base + DEEP : base + DEEP + BX, :] = own[DESIGN + k]
-            for x in range(DEEP):
-                out[base + x : base + x + 1, :] = low[DESIGN + x, y : y + 1, :]
-                at = base + DEEP + BX + x
-                out[at : at + 1, :] = high[DESIGN + x, y : y + 1, :]
-        for ring, y in enumerate(lines):
-            go, come = sided(1, sign, ring)
+        for k, x in enumerate(deep):
+            base = design_row(k)
+            out[base + DEEP : base + DEEP + BY, :] = own[DESIGN + k]
+            for t in range(DEEP):
+                out[base + t : base + t + 1, :] = low[DESIGN + t, x : x + 1, :]
+                at = base + DEEP + BY + t
+                out[at : at + 1, :] = high[DESIGN + t, x : x + 1, :]
+        for ring, x in enumerate(planes):
+            go, come = sided(0, sign, ring)
             fields = [(f, None) for f in range(MOVING)] + [("go", i) for i in go] + [("come", i) for i in come]
             for k, (field, i) in enumerate(fields):
-                base = (BASES[ring] + k) * BY
-                out[base + 2 : base + 2 + BX, :] = own[BASES[ring] + k]
-                for source, side, places in ((low, 1, (1, 0)), (high, -1, (2 + BX, 3 + BX))):
+                base = (BASES[ring] + k) * LINE
+                out[base + 2 : base + 2 + BY, :] = own[BASES[ring] + k]
+                for source, side, places in ((low, 1, (1, 0)), (high, -1, (2 + BY, 3 + BY))):
                     for other in (0, 1):
-                        found = slot(0, side, other, field, i)
+                        found = slot(1, side, other, field, i)
                         if found is not None:
                             at = base + places[other]
-                            out[at : at + 1, :] = source[found, y : y + 1, :]
-    by_parity(odd, up_out, down_out, near_out, far_out)
-
-
-def join_y(odd, own_up, own_down, low, high):
-    ins = (odd, own_up, own_down, low, high)
+                            out[at : at + 1, :] = source[found, x : x + 1, :]
+
+
+def join_x(odd, own_up, own_down, near, far):
+    ins = (odd, own_up, own_down, near, far)
     return call(
-        join_y_body,
+        join_x_body,
         [(FLAT, NZ)] * 2,
         ins,
         [scalar()] + [whole(x.shape) for x in ins[1:]],
-        scratch=(pltpu.VMEM((FLAT, NZ), F32),) * 2,
+        scratch=(pltpu.VMEM((MSG, BX, NZ), F32),) * 2,
         flops=80000,
-        name="join_y",
+        name="join_x",
     )
 
 
@@ -412,31 +420,35 @@
 
 def main_body(
     odd, fwd, later_any, design, node, region, xlow, xhigh, near, far,
-    adjoint, raw, part, up_out, down_out,
-    ylow, yhigh, wide, kinds, fine, post, later, mid, flow, flux, first, sem,
+    adjoint_any, raw, part, up_out, down_out,
+    ylow, yhigh, wide, kinds, fine, post, later, mid, flow, flux, first, adjoint, sem, sems,
 ):
     copy = pltpu.make_async_copy(later_any, later.at[:, 2 : 2 + BX, ROW : ROW + BY, :], sem)
     copy.start()
     to_sides(odd, near, far, ylow, yhigh)
     wide[...] = jnp.zeros_like(wide)
     wide[DEEP : DEEP + BX, ROW : ROW + BY, :] = design[...]
-    wide[0:DEEP, ROW : ROW + BY, :] = xlow[DESIGN:]
-    wide[DEEP + BX :, ROW : ROW + BY, :] = xhigh[DESIGN:]
     for j in range(DEEP):
-        for x in range(BX + 2 * DEEP):
-            at = DESIGN * BY + j * WIDE_ROWS + x
-            wide[x, ROW - DEEP + j : ROW - DEEP + j + 1, :] = ylow[at : at + 1, :]
-            wide[x, ROW + BY + j : ROW + BY + j + 1, :] = yhigh[at : at + 1, :]
+        at = design_row(j)
+        wide[j, ROW - DEEP : ROW + BY + DEEP, :] = xlow[at : at + WIDE_LINE, :]
+        wide[DEEP + BX + j, ROW - DEEP : ROW + BY + DEEP, :] = xhigh[at : at + WIDE_LINE, :]
+        for x in range(BX):
+            wide[DEEP + x, ROW - DEEP + j : ROW - DEEP + j + 1, :] = ylow[DESIGN + j, x : x + 1, :]
+            wide[DEEP + x, ROW + BY + j : ROW + BY + j + 1, :] = yhigh[DESIGN + j, x : x + 1, :]
+    long = slice(ROW - 2, ROW + BY + 2)
     xrings = ((1, xlow, 1, 0), (0, xlow, 1, 1), (2 + BX, xhigh, -1, 0), (3 + BX, xhigh, -1, 1))
     yrings = ((ROW - 1, ylow, 1, 0), (ROW - 2, ylow, 1, 1), (ROW + BY, yhigh, -1, 0), (ROW + BY + 1, yhigh, -1, 1))
     kinds[...] = jnp.zeros_like(kinds)
     kinds[2 : 2 + BX, ROW : ROW + BY, :] = node[...].astype(F32)
+
+    def line(message, k):
+        return message[k * LINE : (k + 1) * LINE, :]
+
     for x, message, sign, ring in xrings:
-        kinds[x, ROW : ROW + BY, :] = message[slot(0, sign, ring, KIND)]
+        kinds[x, long, :] = line(message, slot(0, sign, ring, KIND))
     for row, message, sign, ring in yrings:
-        base = slot(1, sign, ring, KIND) * BY
-        for x in range(EX):
-            kinds[x, row : row + 1, :] = message[base + x : base + x + 1, :]
+        for x in range(BX):
+            kinds[2 + x, row : row + 1, :] = message[slot(1, sign, ring, KIND), x : x + 1, :]
     inverse_norm = 1.0 / norm_row((8, NZ))
 
     def filter_plane(x, carry):
@@ -452,34 +464,27 @@
 
     for x, message, sign, ring in xrings:
         comps = sided(0, sign, ring)[0]
-        for h in (0, 8):
-            rows = slice(h, h + 8)
-            padded = slice(ROW + h, ROW + h + 8)
-            kind = kinds[x, padded, :]
-            q = {i: message[slot(0, sign, ring, "go", i), rows, :] for i in comps}
-            base = slot(0, sign, ring, DENS)
-            value = post_tiles(
-                comps, q, q, message[base, rows, :], [message[base + 1 + a, rows, :] for a in range(3)],
-                kind, factor_of(kind, fine[x, padded, :]),
-            )
-            for i in comps:
-                post[i, x, padded, :] = value[i]
+        kind = kinds[x, long, :]
+        q = {i: line(message, slot(0, sign, ring, "go", i)) for i in comps}
+        base = slot(0, sign, ring, DENS)
+        value = post_tiles(
+            comps, q, q, line(message, base), [line(message, base + 1 + a) for a in range(3)],
+            kind, factor_of(kind, fine[x, long, :]),
+        )
+        for i in comps:
+            post[i, x, long, :] = value[i]
     for row, message, sign, ring in yrings:
         comps = sided(1, sign, ring)[0]
-        kind = kinds[:, row, :]
-
-        def line(k, message=message):
-            return message[k * BY : k * BY + EX, :]
-
-        q = {i: line(slot(1, sign, ring, "go", i)) for i in comps}
+        kind = kinds[2 : 2 + BX, row, :]
+        q = {i: message[slot(1, sign, ring, "go", i)] for i in comps}
         base = slot(1, sign, ring, DENS)
         value = post_tiles(
-            comps, q, q, line(base), [line(base + 1 + a) for a in range(3)],
-            kind, factor_of(kind, fine[:, row, :]),
+            comps, q, q, message[base], [message[base + 1 + a] for a in range(3)],
+            kind, factor_of(kind, fine[2 : 2 + BX, row, :]),
         )
         for i in comps:
-            for x in range(EX):
-                post[i, x, row : row + 1, :] = value[i][x : x + 1, :]
+            for x in range(BX):
+                post[i, 2 + x, row : row + 1, :] = value[i][x : x + 1, :]
 
     def post_plane(x, carry):
         carry = list(carry)
@@ -506,18 +511,15 @@
 
     empty = jnp.zeros((8, NZ), F32)
     totals = lax.fori_loop(0, BX, post_plane, (empty,) * REG)
-    for r in range(REG):
-        part[r] = totals[r]
-
     copy.wait()
     for x, message, sign, ring in xrings:
         for i in sided(0, sign, ring)[1]:
-            later[i, x, ROW : ROW + BY, :] = message[slot(0, sign, ring, "come", i)]
+            later[i, x, long, :] = line(message, slot(0, sign, ring, "come", i))
     for row, message, sign, ring in yrings:
         for i in sided(1, sign, ring)[1]:
-            base = slot(1, sign, ring, "come", i) * BY
-            for x in range(EX):
-                later[i, x, row : row + 1, :] = message[base + x : base + x + 1, :]
+            found = slot(1, sign, ring, "come", i)
+            for x in range(BX):
+                later[i, 2 + x, row : row + 1, :] = message[found, x : x + 1, :]
 
     def mid_plane(x, carry):
         for start in (ROW - 1, ROW + 7, ROW + 15):
@@ -562,6 +564,10 @@
     lax.fori_loop(0, BX + 2, mid_plane, 0)
     raw_scale = BRINKMAN * inverse_norm
 
+    def send(x):
+        at = pl.ds(x, 1)
+        return pltpu.make_async_copy(adjoint.at[:, at], adjoint_any.at[:, at], sems.at[x])
+
     def last_plane(x, carry):
         for h in (0, 8):
             rows = slice(h, h + 8)
@@ -580,25 +586,35 @@
                 adjoint[i, x, rows, :] = value[i]
             both = (first[x + 1, padded, :] + gradient) * raw_scale
             raw[x, rows, :] = jnp.where(kind == 1.0, both, 0.0)
+        send(x).start()
         return carry
 
-    part[REG] = lax.fori_loop(0, BX, last_plane, empty)
-    up_out[...] = raw[BX - RAD :]
-    down_out[...] = raw[:RAD]
+    totals = (*totals, lax.fori_loop(0, BX, last_plane, empty))
+    row = jnp.zeros((8, NZ), F32)
+    for r, value in enumerate(totals):
+        row = jnp.where(lanes((8, NZ)) == r, jnp.sum(value, axis=(0, 1), keepdims=True), row)
+    part[...] = row
+    for out, begin in ((up_out, BX - RAD), (down_out, 0)):
+        for j in range(RAD):
+            out[j * BY : (j + 1) * BY, :] = raw[begin + j]
+        out[RAW_ROWS:, :] = row
+    for x in range(BX):
+        send(x).wait()
 
 
 def main(odd, fwd, later, design, node, region, xlow, xhigh, near, far):
     ins = (odd, fwd, later, design, node, region, xlow, xhigh, near, far)
     specs = [scalar()] + [whole(x.shape) for x in ins[1:]]
     specs[2] = anywhere()
+    outs = [(Q, BX, BY, NZ), (BX, BY, NZ), (8, NZ), (RAW_ROWS + 8, NZ), (RAW_ROWS + 8, NZ)]
     return call(
         main_body,
-        [(Q, BX, BY, NZ), (BX, BY, NZ), (REG + 1, 8, NZ), (RAD, BY, NZ), (RAD, BY, NZ)],
+        outs,
         ins,
         specs,
         scratch=(
-            pltpu.VMEM((FLAT, NZ), F32),
-            pltpu.VMEM((FLAT, NZ), F32),
+            pltpu.VMEM((MSG, BX, NZ), F32),
+            pltpu.VMEM((MSG, BX, NZ), F32),
             pltpu.VMEM((BX + 2 * DEEP, PADY, NZ), F32),
             pltpu.VMEM((EX, PADY, NZ), F32),
             pltpu.VMEM((EX, PADY, NZ), F32),
@@ -608,29 +624,37 @@
             pltpu.VMEM((4, BX, BY, NZ), F32),
             pltpu.VMEM((BX + 2, PADY, NZ), F32),
             pltpu.VMEM((BX + 2, PADY, NZ), F32),
+            pltpu.VMEM((Q, BX, BY, NZ), F32),
             pltpu.SemaphoreType.DMA,
+            pltpu.SemaphoreType.DMA((BX,)),
         ),
         flops=30000000,
         name="main",
+        out_specs=[anywhere()] + [whole(o) for o in outs[1:]],
     )
 
 
-def raw_y_body(odd, raw, low, high, near_out, far_out, up_out, down_out):
+def raw_y_body(odd, raw, part, low, high, near_out, far_out, rows_out, up_out, down_out):
     for out, begin in ((up_out, BY - RAD), (down_out, 0)):
         out[...] = jnp.zeros_like(out)
         for j in range(RAD):
-            out[j, RAD : RAD + BX, :] = raw[:, begin + j, :]
+            y = begin + j
+            out[j, RAD : RAD + BX, :] = raw[:, y, :]
             for x in range(RAD):
-                out[j, x : x + 1, :] = low[x, begin + j : begin + j + 1, :]
-                out[j, RAD + BX + x : RAD + BX + x + 1, :] = high[x, begin + j : begin + j + 1, :]
+                out[j, x : x + 1, :] = low[x * BY + y : x * BY + y + 1, :]
+                out[j, RAD + BX + x : RAD + BX + x + 1, :] = high[x * BY + y : x * BY + y + 1, :]
     by_parity(odd, up_out, down_out, near_out, far_out)
-
-
-def raw_y(odd, raw, low, high):
-    ins = (odd, raw, low, high)
+    other = jnp.where(odd[1] == 1, low[RAW_ROWS : RAW_ROWS + 8, :], high[RAW_ROWS : RAW_ROWS + 8, :])
+    row = part[...] + other
+    for k in range(0, rows_out.shape[0], 8):
+        rows_out[k : k + 8, :] = row
+
+
+def raw_y(odd, raw, part, low, high, count):
+    ins = (odd, raw, part, low, high)
     return call(
         raw_y_body,
-        [(RAD, BY, NZ)] * 2,
+        [(RAD, BY, NZ), (RAD, BY, NZ), (count, NZ)],
         ins,
         [scalar()] + [whole(x.shape) for x in ins[1:]],
         scratch=(pltpu.VMEM((RAD, BY, NZ), F32),) * 2,
@@ -639,11 +663,12 @@
     )
 
 
-def spread_body(odd, raw, xlow, xhigh, near, far, out, ylow, yhigh, wide):
+def spread_body(odd, raw, xlow, xhigh, near, far, rows, out, objective, volumes, ylow, yhigh, wide):
     to_sides(odd, near, far, ylow, yhigh)
     wide[RAD : RAD + BX, ROW : ROW + BY, :] = raw[...]
-    wide[0:RAD, ROW : ROW + BY, :] = xlow[...]
-    wide[RAD + BX :, ROW : ROW + BY, :] = xhigh[...]
+    for j in range(RAD):
+        wide[j, ROW : ROW + BY, :] = xlow[j * BY : (j + 1) * BY, :]
+        wide[RAD + BX + j, ROW : ROW + BY, :] = xhigh[j * BY : (j + 1) * BY, :]
     for x in range(BX + 2 * RAD):
         for j in range(RAD):
             wide[x, ROW - RAD + j : ROW - RAD + j + 1, :] = ylow[j, x : x + 1, :]
@@ -656,19 +681,28 @@
         return carry
 
     lax.fori_loop(0, BX, plane, 0)
-
-
-def spread(odd, raw, xlow, xhigh, near, far):
-    ins = (odd, raw, xlow, xhigh, near, far)
+    total = add_all(rows[k : k + 8, :] for k in range(0, rows.shape[0], 8))
+    lane = lanes((8, NZ))
+    for r in range(REG + 1):
+        value = jnp.sum(jnp.where(lane == r, total, 0.0))
+        if r < REG:
+            volumes[r] = value
+        else:
+            objective[0] = value
+
+
+def spread(odd, raw, xlow, xhigh, near, far, rows):
+    ins = (odd, raw, xlow, xhigh, near, far, rows)
     return call(
         spread_body,
-        [(BX, BY, NZ)],
+        [(BX, BY, NZ), (1,), (REG,)],
         ins,
         [scalar()] + [whole(x.shape) for x in ins[1:]],
         scratch=(pltpu.VMEM((RAD, BY, NZ), F32),) * 2 + (pltpu.VMEM((BX + 2 * RAD, PADY, NZ), F32),),
         flops=2000000,
         name="spread",
-    )[0]
+        out_specs=[whole((BX, BY, NZ)), scalar(), scalar()],
+    )
 
 
 def exchange(up, down, axis):
@@ -685,27 +719,27 @@
     return lax.ppermute(near, axis, inner), lax.ppermute(far, axis, outer)
 
 
-def total(row):
-    axes = ("gx", "gy")
-    count = lax.axis_size(axes)
-    rows = jnp.broadcast_to(row[None], (count,) + row.shape)
-    return jnp.sum(lax.all_to_all(rows, axes, 0, 0, tiled=True), axis=0)
+def share(rows):
+    nx, ny = lax.axis_size("gx"), lax.axis_size("gy")
+    groups = [[x * ny + y for x in range(p, nx, 2) for y in range(ny)] for p in (0, 1)]
+    return lax.all_to_all(rows, ("gx", "gy"), 0, 0, tiled=True, axis_index_groups=groups)
 
 
 def per_device(forward_pops, later_adjoint, design, node_type, region):
-    odd = jnp.reshape(lax.axis_index("gy") % 2, (1,)).astype(jnp.int32)
-    up, down = first_x(forward_pops, later_adjoint, design, node_type)
-    own_up, own_down = first_y(forward_pops, later_adjoint, design, node_type)
-    xlow, xhigh = exchange(up, down, "gx")
-    near, far = swap(*join_y(odd, own_up, own_down, xlow, xhigh), "gy")
+    odd = jnp.stack([lax.axis_index("gy") % 2, lax.axis_index("gx") % 2]).astype(jnp.int32)
+    near, far = swap(*first_y(odd, forward_pops, later_adjoint, design, node_type), "gy")
+    own_up, own_down = first_x(forward_pops, later_adjoint, design, node_type)
+    xlow, xhigh = exchange(*join_x(odd, own_up, own_down, near, far), "gx")
     adjoint, raw, part, up, down = main(
         odd, forward_pops, later_adjoint, design, node_type, region, xlow, xhigh, near, far
     )
-    sums = total(jnp.pad(jnp.sum(part, axis=(1, 2)), (0, NZ - REG - 1)))
     xlow, xhigh = exchange(up, down, "gx")
-    near, far = swap(*raw_y(odd, raw, xlow, xhigh), "gy")
-    sensitivity = spread(odd, raw, xlow, xhigh, near, far)
-    return adjoint, sensitivity, sums[REG], sums[:REG]
+    pairs = lax.axis_size("gx") * lax.axis_size("gy") // 2
+    near, far, rows = raw_y(odd, raw, part, xlow, xhigh, pairs)
+    rows = share(rows)
+    near, far = swap(near, far, "gy")
+    sensitivity, objective, volumes = spread(odd, raw, xlow, xhigh, near, far, rows)
+    return adjoint, sensitivity, objective[0], volumes
 
 
 def solution(mesh):

time: 117 us -> 103 us (0.88)
  waiting for transfers between devices: 30.2 us -> 22 us
  local copies, waits for them, and re-layouts: 7.51 us -> 0.03 us
  Pallas kernels: 11 us -> 16 us
  starting transfers between devices: 65.6 us -> 63.6 us
    ppermute x4, waiting for transfers between devices: 23.2 us -> 9.83 us  [swap(): return (lax.ppermute(near, axis, inner), lax.ppermute(far, axis, outer))]
    unnamed x26 -> x12, local copies, waits for them, and re-layouts: 6.08 us -> 0.03 us
    pallas_call x6, Pallas kernels: 11 us -> 16 us  [call(): pl.pallas_call(body, out_shape=[jax.ShapeDtypeStruct(o, F32) for o in out...]
    ppermute x4, waiting for transfers between devices: 7 us -> 10.7 us  [exchange(): return (lax.ppermute(up, axis, forward), lax.ppermute(down, axis, backward))]
    ppermute x4, starting transfers between devices: 24.3 us -> 21.6 us  [exchange(): return (lax.ppermute(up, axis, forward), lax.ppermute(down, axis, backward))]
    all_to_all x1, starting transfers between devices: 16.9 us -> 18.5 us  [share(): lax.all_to_all(rows, ('gx', 'gy'), 0, 0, tiled=True, axis_index_groups=gr...]
    all_to_all x1, waiting for transfers between devices: 0.01 us -> 1.46 us  [share(): lax.all_to_all(rows, ('gx', 'gy'), 0, 0, tiled=True, axis_index_groups=gr...]
  transfers between devices with their start and end apart: 9 -> 9, of which waited for: 6 -> 6; matrix products, arithmetic and copies ran while one was open for 0% -> 0% of each run, Pallas kernels for 2% -> 0%
where the time goes in v3:
time: 103 us
  starting transfers between devices  63.6 us (62%)
  waiting for transfers between devices  22 us (21%)
  Pallas kernels  16 us (16%)
    ppermute x4, starting transfers between devices, swap(): return (lax.ppermute(near, axis, inner), lax.ppermute(far, axis, outer))  23.5 us
    ppermute x4, starting transfers between devices, exchange(): return (lax.ppermute(up, axis, forward), lax.ppermute(down, axis, backward))  21.6 us
    all_to_all x1, starting transfers between devices, share(): lax.all_to_all(rows, ('gx', 'gy'), 0, 0, tiled=True, axis_index_groups=gr...  18.5 us
    pallas_call x6, Pallas kernels, call(): pl.pallas_call(body, out_shape=[jax.ShapeDtypeStruct(o, F32) for o in out...  16 us
    ppermute x4, waiting for transfers between devices, exchange(): return (lax.ppermute(up, axis, forward), lax.ppermute(down, axis, backward))  10.7 us
    ppermute x4, waiting for transfers between devices, swap(): return (lax.ppermute(near, axis, inner), lax.ppermute(far, axis, outer))  9.83 us
  transfers between devices with their start and end apart: 9, of which 6 were waited for; matrix products, arithmetic and copies ran while one was open for 0% of the time, Pallas kernels for 0%

profile of v3, /device:TPU:1, one launch (start us, length us, event | category | flops | bytes accessed | tf_op | source)
XLA Modules:
  0.0 102.9 jit_solution(14135517772294699416)
XLA Ops:
  0.6 0.6 pad_add_fusion.odd
  1.2 4.1 %first_y.1 = (f32[53,8,128]{2,1,0:T(8,128)}, f32[53,8,128]{2,1,0:T(8,128)}) custom-call(s32[2]{0:T(128)} %pad_add_fusion.odd, f32[19,8,16,128]{3,2,1,0:T(8,128)} %fwd.3, f32[19,8,16,128]{3,2,1,0:T(8,128)} %later_any.3, f32[8,16,128]{2,1,0:T(8,128)} %design.3, s32[8,16,128]{2,1,0:T(8,128)} %node.5), custom_call_target="tpu_custom_call" | custom-call | flops 800000 | bytes 3055624 | tf_op jit(solution)/shard_map/first_y/pallas_call | solution.py:248
  5.4 8.8 %collective-permute-start = (f32[53,8,128]{2,1,0:T(8,128)}, f32[53,8,128]{2,1,0:T(8,128)S(1)}, u32[]{:S(2)}, u32[]{:S(2)}) collective-permute-start(f32[53,8,128]{2,1,0:T(8,128)} %get-tuple-element.23), channel_id=1, source_target_pairs={{0,1},{1,0},{2,3},{3,2},{4,5},{5,4},{6,7},{7,6},{8,9},{9,8},{10,11... | collective-permute-start | bytes 651272 | tf_op jit(solution)/shard_map/ppermute | solution.py:719
  14.2 0.0 copy-start.5
  14.2 5.2 %collective-permute-start.1 = (f32[53,8,128]{2,1,0:T(8,128)}, f32[53,8,128]{2,1,0:T(8,128)S(1)}, u32[]{:S(2)}, u32[]{:S(2)}) collective-permute-start(f32[53,8,128]{2,1,0:T(8,128)} %get-tuple-element.24), channel_id=1, source_target_pairs={{0,15},{1,2},{2,1},{3,4},{4,3},{5,6},{6,5},{7,8},{8,7},{9,10},{10,... | collective-permute-start | bytes 651272 | tf_op jit(solution)/shard_map/ppermute | solution.py:719
  19.4 0.1 first_x.1
  19.5 0.0 copy-start.4
  19.5 6.3 %collective-permute-done.1.far = f32[53,8,128]{2,1,0:T(8,128)S(1)} collective-permute-done((f32[53,8,128]{2,1,0:T(8,128)}, f32[53,8,128]{2,1,0:T(8,128)S(1)}, u32[]{:S(2)}, u32[]{:S(2)}) %collective-permute-start.1) | collective-permute-done | bytes 217120 | tf_op jit(solution)/shard_map/ppermute | solution.py:719
  25.8 0.8 join_x.1
  26.6 2.9 %collective-permute-start.2 = (f32[1096,128]{1,0:T(8,128)S(1)}, f32[1096,128]{1,0:T(8,128)S(1)}, u32[]{:S(2)}, u32[]{:S(2)}) collective-permute-start(f32[1096,128]{1,0:T(8,128)S(1)} %get-tuple-element.25), channel_id=1, source_target_pairs={{0,16},{16,32},{32,48},{48,64},{64,80},{80,96},{96,112},{112,128},... | collective-permute-start | bytes 1683464 | tf_op jit(solution)/shard_map/ppermute | solution.py:712
  29.6 8.7 %collective-permute-start.3 = (f32[1096,128]{1,0:T(8,128)S(1)}, f32[1096,128]{1,0:T(8,128)S(1)}, u32[]{:S(2)}, u32[]{:S(2)}) collective-permute-start(f32[1096,128]{1,0:T(8,128)S(1)} %get-tuple-element.26), channel_id=1, source_target_pairs={{16,0},{32,16},{48,32},{64,48},{80,64},{96,80},{112,96},{128,112},... | collective-permute-start | bytes 1683464 | tf_op jit(solution)/shard_map/ppermute | solution.py:712
  38.3 8.8 %collective-permute-done.2.xlow = f32[1096,128]{1,0:T(8,128)S(1)} collective-permute-done((f32[1096,128]{1,0:T(8,128)S(1)}, f32[1096,128]{1,0:T(8,128)S(1)}, u32[]{:S(2)}, u32[]{:S(2)}) %collective-permute-start.2) | collective-permute-done | bytes 561184 | tf_op jit(solution)/shard_map/ppermute | solution.py:712
  47.1 0.9 collective-permute-done.3.xhigh
  48.0 7.5 %main.1 = (f32[19,8,16,128]{3,2,1,0:T(8,128)}, f32[8,16,128]{2,1,0:T(8,128)S(1)}, f32[8,128]{1,0:T(8,128)S(1)}, f32[56,128]{1,0:T(8,128)S(1)}, f32[56,128]{1,0:T(8,128)S(1)}) custom-call(s32[2]{0:T(128)S(1)} %copy-done.5, f32[19,8,16,128]{3,2,1,0:T(8,128)S(1)} %copy-done, f32[19,8,16,128]{3,2,1,0:T(8,128)S(1)} %copy-done.1, f32[8,16,128]{2,1,0:T(8,128)S(1)} %copy-done.2, ...), custom_call_target="tpu_custom_call" | custom-call | flops 30000000 | bytes 5615624 | tf_op jit(solution)/shard_map/main/pallas_call | solution.py:248
  55.6 1.9 %collective-permute-start.4 = (f32[56,128]{1,0:T(8,128)S(1)}, f32[56,128]{1,0:T(8,128)S(1)}, u32[]{:S(2)}, u32[]{:S(2)}) collective-permute-start(f32[56,128]{1,0:T(8,128)S(1)} %get-tuple-element.29), channel_id=1, source_target_pairs={{0,16},{16,32},{32,48},{48,64},{64,80},{80,96},{96,112},{112,128},... | collective-permute-start | bytes 86024 | tf_op jit(solution)/shard_map/ppermute | solution.py:712
  57.5 8.0 %collective-permute-start.5 = (f32[56,128]{1,0:T(8,128)S(1)}, f32[56,128]{1,0:T(8,128)S(1)}, u32[]{:S(2)}, u32[]{:S(2)}) collective-permute-start(f32[56,128]{1,0:T(8,128)S(1)} %get-tuple-element.30), channel_id=1, source_target_pairs={{16,0},{32,16},{48,32},{64,48},{80,64},{96,80},{112,96},{128,112},... | collective-permute-start | bytes 86024 | tf_op jit(solution)/shard_map/ppermute | solution.py:712
  65.5 1.0 collective-permute-done.5.high.xhigh
  66.5 1.2 %raw_y.1 = (f32[3,16,128]{2,1,0:T(8,128)S(1)}, f32[3,16,128]{2,1,0:T(8,128)S(1)}, f32[256,128]{1,0:T(8,128)}) custom-call(s32[2]{0:T(128)S(1)} %copy-done.5, f32[8,16,128]{2,1,0:T(8,128)S(1)} %get-tuple-element.28.raw, f32[8,128]{1,0:T(8,128)S(1)} %get-tuple-element.31.part, f32[56,128]{1,0:T(8,128)S(1)} %collective-permute-done.4.low.xlow, ...), custom_call_target="tpu_custom_call" | custom-call | flops 20000 | bytes 307208 | tf_op jit(solution)/shard_map/raw_y/pallas_call | solution.py:248
  67.7 18.5 %all-to-all-start = ((f32[256,1,128]{2,1,0:T(1,128)}), f32[256,1,128]{2,1,0:T(1,128)S(1)}, u32[]{:S(2)}, u32[]{:S(2)}) async-start(f32[256,1,128]{2,1,0:T(1,128)} %bitcast.3), calls=%async_computation | async-start | bytes 262144 | tf_op jit(solution)/shard_map/all_to_all | solution.py:725
  86.3 3.7 %collective-permute-start.6 = (f32[3,16,128]{2,1,0:T(8,128)S(1)}, f32[3,16,128]{2,1,0:T(8,128)S(1)}, u32[]{:S(2)}, u32[]{:S(2)}) collective-permute-start(f32[3,16,128]{2,1,0:T(8,128)S(1)} %get-tuple-element.32), channel_id=1, source_target_pairs={{0,1},{1,0},{2,3},{3,2},{4,5},{5,4},{6,7},{7,6},{8,9},{9,8},{10,11... | collective-permute-start | bytes 73736 | tf_op jit(solution)/shard_map/ppermute | solution.py:719
  89.9 5.8 %collective-permute-start.7 = (f32[3,16,128]{2,1,0:T(8,128)S(1)}, f32[3,16,128]{2,1,0:T(8,128)S(1)}, u32[]{:S(2)}, u32[]{:S(2)}) collective-permute-start(f32[3,16,128]{2,1,0:T(8,128)S(1)} %get-tuple-element.33), channel_id=1, source_target_pairs={{0,15},{1,2},{2,1},{3,4},{4,3},{5,6},{6,5},{7,8},{8,7},{9,10},{10,... | collective-permute-start | bytes 73736 | tf_op jit(solution)/shard_map/ppermute | solution.py:719
  95.8 3.5 %collective-permute-done.7.far = f32[3,16,128]{2,1,0:T(8,128)S(1)} collective-permute-done((f32[3,16,128]{2,1,0:T(8,128)S(1)}, f32[3,16,128]{2,1,0:T(8,128)S(1)}, u32[]{:S(2)}, u32[]{:S(2)}) %collective-permute-start.7) | collective-permute-done | bytes 24608 | tf_op jit(solution)/shard_map/ppermute | solution.py:719
  99.3 1.5 %all-to-all-done = f32[256,1,128]{2,1,0:T(1,128)S(1)} async-done(((f32[256,1,128]{2,1,0:T(1,128)}), f32[256,1,128]{2,1,0:T(1,128)S(1)}, u32[]{:S(2)}, u32[]{:S(2)}) %all-to-all-start) | async-done | bytes 131104 | tf_op jit(solution)/shard_map/all_to_all | solution.py:725
  100.8 2.1 %spread.1 = (f32[8,16,128]{2,1,0:T(8,128)}, f32[1]{0:T(128)}, f32[8]{0:T(128)}) custom-call(s32[2]{0:T(128)S(1)} %copy-done.5, f32[8,16,128]{2,1,0:T(8,128)S(1)} %get-tuple-element.28.raw, f32[56,128]{1,0:T(8,128)S(1)} %collective-permute-done.4.low.xlow, f32[56,128]{1,0:T(8,128)S(1)} %collective-permute-done.5.high.xhigh, ...), custom_call_target="tpu_custom_call" | custom-call | flops 2000000 | bytes 368684 | tf_op jit(solution)/shard_map/spread/pallas_call | solution.py:248
  (13 shorter events, 0.0 us)
Async XLA Ops:
  1.2 18.1 %copy-start = (f32[19,8,16,128]{3,2,1,0:T(8,128)S(1)}, f32[19,8,16,128]{3,2,1,0:T(8,128)}, u32[]{:S(2)}) copy-start(f32[19,8,16,128]{3,2,1,0:T(8,128)} %fwd.3) | copy-start | bytes 3735556
  1.2 18.2 %copy-start.1 = (f32[19,8,16,128]{3,2,1,0:T(8,128)S(1)}, f32[19,8,16,128]{3,2,1,0:T(8,128)}, u32[]{:S(2)}) copy-start(f32[19,8,16,128]{3,2,1,0:T(8,128)} %later_any.3) | copy-start | bytes 3735556
  1.2 18.2 %copy-start.2 = (f32[8,16,128]{2,1,0:T(8,128)S(1)}, f32[8,16,128]{2,1,0:T(8,128)}, u32[]{:S(2)}) copy-start(f32[8,16,128]{2,1,0:T(8,128)} %design.3) | copy-start | bytes 196612
  1.2 18.2 %copy-start.3 = (s32[8,16,128]{2,1,0:T(8,128)S(1)}, s32[8,16,128]{2,1,0:T(8,128)}, u32[]{:S(2)}) copy-start(s32[8,16,128]{2,1,0:T(8,128)} %node.5) | copy-start | bytes 196612
  5.4 14.1 %collective-permute-start = (f32[53,8,128]{2,1,0:T(8,128)}, f32[53,8,128]{2,1,0:T(8,128)S(1)}, u32[]{:S(2)}, u32[]{:S(2)}) collective-permute-start(f32[53,8,128]{2,1,0:T(8,128)} %get-tuple-element.23), channel_id=1, source_target_pairs={{0,1},{1,0},{2,3},{3,2},{4,5},{5,4},{6,7},{7,6},{8,9},{9,8},{10,11... | collective-permute-start | bytes 651272 | tf_op jit(solution)/shard_map/ppermute | solution.py:719
  14.2 11.6 %copy-start.5 = (s32[2]{0:T(128)S(1)}, s32[2]{0:T(128)}, u32[]{:S(2)}) copy-start(s32[2]{0:T(128)} %pad_add_fusion.odd) | copy-start | bytes 28
  14.2 11.6 %collective-permute-start.1 = (f32[53,8,128]{2,1,0:T(8,128)}, f32[53,8,128]{2,1,0:T(8,128)S(1)}, u32[]{:S(2)}, u32[]{:S(2)}) collective-permute-start(f32[53,8,128]{2,1,0:T(8,128)} %get-tuple-element.24), channel_id=1, source_target_pairs={{0,15},{1,2},{2,1},{3,4},{4,3},{5,6},{6,5},{7,8},{8,7},{9,10},{10,... | collective-permute-start | bytes 651272 | tf_op jit(solution)/shard_map/ppermute | solution.py:719
  19.5 28.5 %copy-start.4 = (s32[8,16,128]{2,1,0:T(8,128)S(1)}, s32[8,16,128]{2,1,0:T(8,128)}, u32[]{:S(2)}) copy-start(s32[8,16,128]{2,1,0:T(8,128)} %region.1) | copy-start | bytes 196612
  26.6 20.5 %collective-permute-start.2 = (f32[1096,128]{1,0:T(8,128)S(1)}, f32[1096,128]{1,0:T(8,128)S(1)}, u32[]{:S(2)}, u32[]{:S(2)}) collective-permute-start(f32[1096,128]{1,0:T(8,128)S(1)} %get-tuple-element.25), channel_id=1, source_target_pairs={{0,16},{16,32},{32,48},{48,64},{64,80},{80,96},{96,112},{112,128},... | collective-permute-start | bytes 1683464 | tf_op jit(solution)/shard_map/ppermute | solution.py:712
  29.6 18.4 %collective-permute-start.3 = (f32[1096,128]{1,0:T(8,128)S(1)}, f32[1096,128]{1,0:T(8,128)S(1)}, u32[]{:S(2)}, u32[]{:S(2)}) collective-permute-start(f32[1096,128]{1,0:T(8,128)S(1)} %get-tuple-element.26), channel_id=1, source_target_pairs={{16,0},{32,16},{48,32},{64,48},{80,64},{96,80},{112,96},{128,112},... | collective-permute-start | bytes 1683464 | tf_op jit(solution)/shard_map/ppermute | solution.py:712
  55.6 10.0 %collective-permute-start.4 = (f32[56,128]{1,0:T(8,128)S(1)}, f32[56,128]{1,0:T(8,128)S(1)}, u32[]{:S(2)}, u32[]{:S(2)}) collective-permute-start(f32[56,128]{1,0:T(8,128)S(1)} %get-tuple-element.29), channel_id=1, source_target_pairs={{0,16},{16,32},{32,48},{48,64},{64,80},{80,96},{96,112},{112,128},... | collective-permute-start | bytes 86024 | tf_op jit(solution)/shard_map/ppermute | solution.py:712
  57.5 9.0 %collective-permute-start.5 = (f32[56,128]{1,0:T(8,128)S(1)}, f32[56,128]{1,0:T(8,128)S(1)}, u32[]{:S(2)}, u32[]{:S(2)}) collective-permute-start(f32[56,128]{1,0:T(8,128)S(1)} %get-tuple-element.30), channel_id=1, source_target_pairs={{16,0},{32,16},{48,32},{64,48},{80,64},{96,80},{112,96},{128,112},... | collective-permute-start | bytes 86024 | tf_op jit(solution)/shard_map/ppermute | solution.py:712
  67.7 33.0 %all-to-all-start = ((f32[256,1,128]{2,1,0:T(1,128)}), f32[256,1,128]{2,1,0:T(1,128)S(1)}, u32[]{:S(2)}, u32[]{:S(2)}) async-start(f32[256,1,128]{2,1,0:T(1,128)} %bitcast.3), calls=%async_computation | async-start | bytes 262144 | tf_op jit(solution)/shard_map/all_to_all | solution.py:725
  86.3 9.5 %collective-permute-start.6 = (f32[3,16,128]{2,1,0:T(8,128)S(1)}, f32[3,16,128]{2,1,0:T(8,128)S(1)}, u32[]{:S(2)}, u32[]{:S(2)}) collective-permute-start(f32[3,16,128]{2,1,0:T(8,128)S(1)} %get-tuple-element.32), channel_id=1, source_target_pairs={{0,1},{1,0},{2,3},{3,2},{4,5},{5,4},{6,7},{7,6},{8,9},{9,8},{10,11... | collective-permute-start | bytes 73736 | tf_op jit(solution)/shard_map/ppermute | solution.py:719
  89.9 9.4 %collective-permute-start.7 = (f32[3,16,128]{2,1,0:T(8,128)S(1)}, f32[3,16,128]{2,1,0:T(8,128)S(1)}, u32[]{:S(2)}, u32[]{:S(2)}) collective-permute-start(f32[3,16,128]{2,1,0:T(8,128)S(1)} %get-tuple-element.33), channel_id=1, source_target_pairs={{0,15},{1,2},{2,1},{3,4},{4,3},{5,6},{6,5},{7,8},{8,7},{9,10},{10,... | collective-permute-start | bytes 73736 | tf_op jit(solution)/shard_map/ppermute | solution.py:719

commit v4 on v3

--- a/solution.py
+++ b/solution.py
@@ -295,13 +295,10 @@
     )
 
 
-CHUNKS = ((0, 5), (5, 10), (10, 15), (15, 19))
-
-
-def first_y_body(odd, fwd_any, later_any, design, node, near_out, far_out, fwd, later, up_out, down_out, sems):
+def first_y_body(fwd_any, later_any, design, node, far_out, near_out, fwd, later, up_out, down_out, sems):
     copies = [
-        pltpu.make_async_copy(source.at[lo:hi], target.at[lo:hi], sems.at[k, c])
-        for c, (lo, hi) in enumerate(CHUNKS)
+        pltpu.make_async_copy(source.at[:, :, at : at + 2, :], target.at[:, :, to : to + 2, :], sems.at[k, e])
+        for e, (at, to) in enumerate(((0, 0), (BY - 2, 2)))
         for k, (source, target) in enumerate(((fwd_any, fwd), (later_any, later)))
     ]
     for copy in copies:
@@ -319,28 +316,28 @@
                 1,
                 sign,
                 ring,
-                [fwd[i, :, y, :] for i in range(Q)],
+                [fwd[i, :, y % 12, :] for i in range(Q)],
                 node[:, y, :].astype(F32),
-                lambda i, y=y: later[i, :, y, :],
+                lambda i, y=y: later[i, :, y % 12, :],
             )
             for k, value in enumerate(fields):
                 out[BASES[ring] + k] = value
-    by_parity(odd, up_out, down_out, near_out, far_out)
-
-
-def first_y(odd, fwd, later, design, node):
-    block = pltpu.VMEM(fwd.shape, F32)
+    by_parity("gy", up_out, down_out, far_out, near_out)
+
+
+def first_y(fwd, later, design, node):
+    block = pltpu.VMEM((Q, BX, 4, NZ), F32)
     return call(
         first_y_body,
         [(MSG, BX, NZ)] * 2,
-        (odd, fwd, later, design, node),
-        [scalar(), anywhere(), anywhere(), whole(design.shape), whole(node.shape)],
+        (fwd, later, design, node),
+        [anywhere(), anywhere(), whole(design.shape), whole(node.shape)],
         scratch=(
             block,
             block,
             pltpu.VMEM((MSG, BX, NZ), F32),
             pltpu.VMEM((MSG, BX, NZ), F32),
-            pltpu.SemaphoreType.DMA((2, len(CHUNKS))),
+            pltpu.SemaphoreType.DMA((2, 2)),
         ),
         flops=800000,
         name="first_y",
@@ -348,32 +345,36 @@
     )
 
 
-def by_parity(odd, up, down, near_out, far_out):
-    @pl.when(odd[0] == 0)
+def odd(axis):
+    return lax.rem(lax.axis_index(axis), 2)
+
+
+def by_parity(axis, up, down, far_out, near_out):
+    @pl.when(odd(axis) == 0)
     def _():
         near_out[...] = up[...]
         far_out[...] = down[...]
 
-    @pl.when(odd[0] == 1)
+    @pl.when(odd(axis) == 1)
     def _():
         near_out[...] = down[...]
         far_out[...] = up[...]
 
 
-def to_sides(odd, near, far, low, high):
-    @pl.when(odd[0] == 0)
+def to_sides(axis, far, near, low, high):
+    @pl.when(odd(axis) == 0)
     def _():
         high[...] = near[...]
         low[...] = far[...]
 
-    @pl.when(odd[0] == 1)
+    @pl.when(odd(axis) == 1)
     def _():
         low[...] = near[...]
         high[...] = far[...]
 
 
-def join_x_body(odd, own_up, own_down, near, far, up_out, down_out, low, high):
-    to_sides(odd, near, far, low, high)
+def join_x_body(own_up, own_down, far, near, up_out, down_out, low, high):
+    to_sides("gy", far, near, low, high)
     for out, own, sign, planes, deep in (
         (up_out, own_up, 1, (BX - 1, BX - 2), range(BX - DEEP, BX)),
         (down_out, own_down, -1, (0, 1), range(DEEP)),
@@ -400,13 +401,13 @@
                             out[at : at + 1, :] = source[found, x : x + 1, :]
 
 
-def join_x(odd, own_up, own_down, near, far):
-    ins = (odd, own_up, own_down, near, far)
+def join_x(own_up, own_down, far, near):
+    ins = (own_up, own_down, far, near)
     return call(
         join_x_body,
         [(FLAT, NZ)] * 2,
         ins,
-        [scalar()] + [whole(x.shape) for x in ins[1:]],
+        [whole(x.shape) for x in ins],
         scratch=(pltpu.VMEM((MSG, BX, NZ), F32),) * 2,
         flops=80000,
         name="join_x",
@@ -419,13 +420,13 @@
 
 
 def main_body(
-    odd, fwd, later_any, design, node, region, xlow, xhigh, near, far,
+    fwd, later_any, design, node, region, xlow, xhigh, far, near,
     adjoint_any, raw, part, up_out, down_out,
     ylow, yhigh, wide, kinds, fine, post, later, mid, flow, flux, first, adjoint, sem, sems,
 ):
     copy = pltpu.make_async_copy(later_any, later.at[:, 2 : 2 + BX, ROW : ROW + BY, :], sem)
     copy.start()
-    to_sides(odd, near, far, ylow, yhigh)
+    to_sides("gy", far, near, ylow, yhigh)
     wide[...] = jnp.zeros_like(wide)
     wide[DEEP : DEEP + BX, ROW : ROW + BY, :] = design[...]
     for j in range(DEEP):
@@ -602,10 +603,10 @@
         send(x).wait()
 
 
-def main(odd, fwd, later, design, node, region, xlow, xhigh, near, far):
-    ins = (odd, fwd, later, design, node, region, xlow, xhigh, near, far)
-    specs = [scalar()] + [whole(x.shape) for x in ins[1:]]
-    specs[2] = anywhere()
+def main(fwd, later, design, node, region, xlow, xhigh, far, near):
+    ins = (fwd, later, design, node, region, xlow, xhigh, far, near)
+    specs = [whole(x.shape) for x in ins]
+    specs[1] = anywhere()
     outs = [(Q, BX, BY, NZ), (BX, BY, NZ), (8, NZ), (RAW_ROWS + 8, NZ), (RAW_ROWS + 8, NZ)]
     return call(
         main_body,
@@ -634,7 +635,7 @@
     )
 
 
-def raw_y_body(odd, raw, part, low, high, near_out, far_out, rows_out, up_out, down_out):
+def raw_y_body(raw, part, low, high, far_out, near_out, rows_out, up_out, down_out):
     for out, begin in ((up_out, BY - RAD), (down_out, 0)):
         out[...] = jnp.zeros_like(out)
         for j in range(RAD):
@@ -643,28 +644,28 @@
             for x in range(RAD):
                 out[j, x : x + 1, :] = low[x * BY + y : x * BY + y + 1, :]
                 out[j, RAD + BX + x : RAD + BX + x + 1, :] = high[x * BY + y : x * BY + y + 1, :]
-    by_parity(odd, up_out, down_out, near_out, far_out)
-    other = jnp.where(odd[1] == 1, low[RAW_ROWS : RAW_ROWS + 8, :], high[RAW_ROWS : RAW_ROWS + 8, :])
+    by_parity("gy", up_out, down_out, far_out, near_out)
+    other = jnp.where(odd("gx") == 1, low[RAW_ROWS : RAW_ROWS + 8, :], high[RAW_ROWS : RAW_ROWS + 8, :])
     row = part[...] + other
     for k in range(0, rows_out.shape[0], 8):
         rows_out[k : k + 8, :] = row
 
 
-def raw_y(odd, raw, part, low, high, count):
-    ins = (odd, raw, part, low, high)
+def raw_y(raw, part, low, high, count):
+    ins = (raw, part, low, high)
     return call(
         raw_y_body,
         [(RAD, BY, NZ), (RAD, BY, NZ), (count, NZ)],
         ins,
-        [scalar()] + [whole(x.shape) for x in ins[1:]],
+        [whole(x.shape) for x in ins],
         scratch=(pltpu.VMEM((RAD, BY, NZ), F32),) * 2,
         flops=20000,
         name="raw_y",
     )
 
 
-def spread_body(odd, raw, xlow, xhigh, near, far, rows, out, objective, volumes, ylow, yhigh, wide):
-    to_sides(odd, near, far, ylow, yhigh)
+def spread_body(raw, xlow, xhigh, far, near, rows, out, objective, volumes, ylow, yhigh, wide):
+    to_sides("gy", far, near, ylow, yhigh)
     wide[RAD : RAD + BX, ROW : ROW + BY, :] = raw[...]
     for j in range(RAD):
         wide[j, ROW : ROW + BY, :] = xlow[j * BY : (j + 1) * BY, :]
@@ -691,13 +692,13 @@
             objective[0] = value
 
 
-def spread(odd, raw, xlow, xhigh, near, far, rows):
-    ins = (odd, raw, xlow, xhigh, near, far, rows)
+def spread(raw, xlow, xhigh, far, near, rows):
+    ins = (raw, xlow, xhigh, far, near, rows)
     return call(
         spread_body,
         [(BX, BY, NZ), (1,), (REG,)],
         ins,
-        [scalar()] + [whole(x.shape) for x in ins[1:]],
+        [whole(x.shape) for x in ins],
         scratch=(pltpu.VMEM((RAD, BY, NZ), F32),) * 2 + (pltpu.VMEM((BX + 2 * RAD, PADY, NZ), F32),),
         flops=2000000,
         name="spread",
@@ -712,11 +713,11 @@
     return lax.ppermute(up, axis, forward), lax.ppermute(down, axis, backward)
 
 
-def swap(near, far, axis):
+def swap(far, near, axis):
     count = lax.axis_size(axis)
     inner = [(i, i ^ 1) for i in range(count)]
     outer = [(i, (i + 1 if i % 2 else i - 1) % count) for i in range(count)]
-    return lax.ppermute(near, axis, inner), lax.ppermute(far, axis, outer)
+    return lax.ppermute(far, axis, outer), lax.ppermute(near, axis, inner)
 
 
 def share(rows):
@@ -726,19 +727,18 @@
 
 
 def per_device(forward_pops, later_adjoint, design, node_type, region):
-    odd = jnp.stack([lax.axis_index("gy") % 2, lax.axis_index("gx") % 2]).astype(jnp.int32)
-    near, far = swap(*first_y(odd, forward_pops, later_adjoint, design, node_type), "gy")
+    far, near = swap(*first_y(forward_pops, later_adjoint, design, node_type), "gy")
     own_up, own_down = first_x(forward_pops, later_adjoint, design, node_type)
-    xlow, xhigh = exchange(*join_x(odd, own_up, own_down, near, far), "gx")
+    xlow, xhigh = exchange(*join_x(own_up, own_down, far, near), "gx")
     adjoint, raw, part, up, down = main(
-        odd, forward_pops, later_adjoint, design, node_type, region, xlow, xhigh, near, far
+        forward_pops, later_adjoint, design, node_type, region, xlow, xhigh, far, near
     )
     xlow, xhigh = exchange(up, down, "gx")
     pairs = lax.axis_size("gx") * lax.axis_size("gy") // 2
-    near, far, rows = raw_y(odd, raw, part, xlow, xhigh, pairs)
+    far, near, rows = raw_y(raw, part, xlow, xhigh, pairs)
     rows = share(rows)
-    near, far = swap(near, far, "gy")
-    sensitivity, objective, volumes = spread(odd, raw, xlow, xhigh, near, far, rows)
+    far, near = swap(far, near, "gy")
+    sensitivity, objective, volumes = spread(raw, xlow, xhigh, far, near, rows)
     return adjoint, sensitivity, objective[0], volumes
 
 

time: 103 us -> 98.3 us (0.954); the launches traced: 103 us -> 97.2 us
  waiting for transfers between devices: 22 us -> 14.6 us
  starting transfers between devices: 63.6 us -> 68.6 us
  Pallas kernels: 16 us -> 13.2 us
    ppermute x4, waiting for transfers between devices: 9.83 us -> 2.07 us  [swap(): return (lax.ppermute(far, axis, outer), lax.ppermute(near, axis, inner))]
    ppermute x4, starting transfers between devices: 23.5 us -> 27.6 us  [swap(): return (lax.ppermute(far, axis, outer), lax.ppermute(near, axis, inner))]
    pallas_call x6, Pallas kernels: 16 us -> 13.2 us  [call(): pl.pallas_call(body, out_shape=[jax.ShapeDtypeStruct(o, F32) for o in out...]
where the time goes in v4:
time: 98.3 us; the launch traced here: 97.2 us
  starting transfers between devices  68.6 us (70%)
  waiting for transfers between devices  14.6 us (15%)
  Pallas kernels  13.2 us (13%)
    ppermute x4, starting transfers between devices, swap(): return (lax.ppermute(far, axis, outer), lax.ppermute(near, axis, inner))  27.6 us
    ppermute x4, starting transfers between devices, exchange(): return (lax.ppermute(up, axis, forward), lax.ppermute(down, axis, backward))  22.4 us
    all_to_all x1, starting transfers between devices, share(): lax.all_to_all(rows, ('gx', 'gy'), 0, 0, tiled=True, axis_index_groups=gr...  18.6 us
    pallas_call x6, Pallas kernels, call(): pl.pallas_call(body, out_shape=[jax.ShapeDtypeStruct(o, F32) for o in out...  13.2 us
    ppermute x4, waiting for transfers between devices, exchange(): return (lax.ppermute(up, axis, forward), lax.ppermute(down, axis, backward))  10.9 us
    ppermute x4, waiting for transfers between devices, swap(): return (lax.ppermute(far, axis, outer), lax.ppermute(near, axis, inner))  2.07 us
  transfers between devices with their start and end apart: 9, of which 6 were waited for; matrix products, arithmetic and copies ran while one was open for 0% of the time, Pallas kernels for 0%

profile of v4, /device:TPU:1, one launch (start us, length us, event | category | flops | bytes accessed | tf_op | source)
XLA Modules:
  0.0 97.2 jit_solution(6600476332332628259)
XLA Ops:
  0.7 3.5 %first_y.1 = (f32[53,8,128]{2,1,0:T(8,128)}, f32[53,8,128]{2,1,0:T(8,128)}) custom-call(f32[19,8,16,128]{3,2,1,0:T(8,128)} %fwd.3, f32[19,8,16,128]{3,2,1,0:T(8,128)} %later_any.3, f32[8,16,128]{2,1,0:T(8,128)} %design.3, s32[8,16,128]{2,1,0:T(8,128)} %node.5), custom_call_target="tpu_custom_call" | custom-call | flops 800000 | bytes 3055616 | tf_op jit(solution)/shard_map/first_y/pallas_call | solution.py:248
  4.2 12.0 %collective-permute-start = (f32[53,8,128]{2,1,0:T(8,128)}, f32[53,8,128]{2,1,0:T(8,128)S(1)}, u32[]{:S(2)}, u32[]{:S(2)}) collective-permute-start(f32[53,8,128]{2,1,0:T(8,128)} %get-tuple-element.23), channel_id=1, source_target_pairs={{0,15},{1,2},{2,1},{3,4},{4,3},{5,6},{6,5},{7,8},{8,7},{9,10},{10,... | collective-permute-start | bytes 651272 | tf_op jit(solution)/shard_map/ppermute | solution.py:720
  16.2 3.9 %collective-permute-start.1 = (f32[53,8,128]{2,1,0:T(8,128)}, f32[53,8,128]{2,1,0:T(8,128)S(1)}, u32[]{:S(2)}, u32[]{:S(2)}) collective-permute-start(f32[53,8,128]{2,1,0:T(8,128)} %get-tuple-element.24), channel_id=1, source_target_pairs={{0,1},{1,0},{2,3},{3,2},{4,5},{5,4},{6,7},{7,6},{8,9},{9,8},{10,11... | collective-permute-start | bytes 651272 | tf_op jit(solution)/shard_map/ppermute | solution.py:720
  20.2 0.1 first_x.1
  20.3 0.0 copy-start.4
  20.3 1.2 %collective-permute-done.far = f32[53,8,128]{2,1,0:T(8,128)S(1)} collective-permute-done((f32[53,8,128]{2,1,0:T(8,128)}, f32[53,8,128]{2,1,0:T(8,128)S(1)}, u32[]{:S(2)}, u32[]{:S(2)}) %collective-permute-start) | collective-permute-done | bytes 217120 | tf_op jit(solution)/shard_map/ppermute | solution.py:720
  21.6 0.0 collective-permute-done.1.near
  21.6 0.3 join_x.1
  21.9 3.4 %collective-permute-start.2 = (f32[1096,128]{1,0:T(8,128)S(1)}, f32[1096,128]{1,0:T(8,128)S(1)}, u32[]{:S(2)}, u32[]{:S(2)}) collective-permute-start(f32[1096,128]{1,0:T(8,128)S(1)} %get-tuple-element.25), channel_id=1, source_target_pairs={{0,16},{16,32},{32,48},{48,64},{64,80},{80,96},{96,112},{112,128},... | collective-permute-start | bytes 1683464 | tf_op jit(solution)/shard_map/ppermute | solution.py:713
  25.3 9.1 %collective-permute-start.3 = (f32[1096,128]{1,0:T(8,128)S(1)}, f32[1096,128]{1,0:T(8,128)S(1)}, u32[]{:S(2)}, u32[]{:S(2)}) collective-permute-start(f32[1096,128]{1,0:T(8,128)S(1)} %get-tuple-element.26), channel_id=1, source_target_pairs={{16,0},{32,16},{48,32},{64,48},{80,64},{96,80},{112,96},{128,112},... | collective-permute-start | bytes 1683464 | tf_op jit(solution)/shard_map/ppermute | solution.py:713
  34.3 9.0 %collective-permute-done.2.xlow = f32[1096,128]{1,0:T(8,128)S(1)} collective-permute-done((f32[1096,128]{1,0:T(8,128)S(1)}, f32[1096,128]{1,0:T(8,128)S(1)}, u32[]{:S(2)}, u32[]{:S(2)}) %collective-permute-start.2) | collective-permute-done | bytes 561184 | tf_op jit(solution)/shard_map/ppermute | solution.py:713
  43.4 0.9 collective-permute-done.3.xhigh
  44.3 7.0 %main.1 = (f32[19,8,16,128]{3,2,1,0:T(8,128)}, f32[8,16,128]{2,1,0:T(8,128)S(1)}, f32[8,128]{1,0:T(8,128)S(1)}, f32[56,128]{1,0:T(8,128)S(1)}, f32[56,128]{1,0:T(8,128)S(1)}) custom-call(f32[19,8,16,128]{3,2,1,0:T(8,128)S(1)} %copy-done, f32[19,8,16,128]{3,2,1,0:T(8,128)S(1)} %copy-done.1, f32[8,16,128]{2,1,0:T(8,128)S(1)} %copy-done.2, ...), custom_call_target="tpu_custom_call" | custom-call | flops 30000000 | bytes 5615616 | tf_op jit(solution)/shard_map/main/pallas_call | solution.py:248
  51.3 1.9 %collective-permute-start.4 = (f32[56,128]{1,0:T(8,128)S(1)}, f32[56,128]{1,0:T(8,128)S(1)}, u32[]{:S(2)}, u32[]{:S(2)}) collective-permute-start(f32[56,128]{1,0:T(8,128)S(1)} %get-tuple-element.29), channel_id=1, source_target_pairs={{0,16},{16,32},{32,48},{48,64},{64,80},{80,96},{96,112},{112,128},... | collective-permute-start | bytes 86024 | tf_op jit(solution)/shard_map/ppermute | solution.py:713
  53.2 8.0 %collective-permute-start.5 = (f32[56,128]{1,0:T(8,128)S(1)}, f32[56,128]{1,0:T(8,128)S(1)}, u32[]{:S(2)}, u32[]{:S(2)}) collective-permute-start(f32[56,128]{1,0:T(8,128)S(1)} %get-tuple-element.30), channel_id=1, source_target_pairs={{16,0},{32,16},{48,32},{64,48},{80,64},{96,80},{112,96},{128,112},... | collective-permute-start | bytes 86024 | tf_op jit(solution)/shard_map/ppermute | solution.py:713
  61.2 0.0 collective-permute-done.4.low.xlow
  61.2 1.0 collective-permute-done.5.high.xhigh
  62.2 0.7 raw_y.1
  62.9 18.6 %all-to-all-start = ((f32[256,1,128]{2,1,0:T(1,128)}), f32[256,1,128]{2,1,0:T(1,128)S(1)}, u32[]{:S(2)}, u32[]{:S(2)}) async-start(f32[256,1,128]{2,1,0:T(1,128)} %bitcast.1), calls=%async_computation | async-start | bytes 262144 | tf_op jit(solution)/shard_map/all_to_all | solution.py:726
  81.5 7.4 %collective-permute-start.6 = (f32[3,16,128]{2,1,0:T(8,128)S(1)}, f32[3,16,128]{2,1,0:T(8,128)S(1)}, u32[]{:S(2)}, u32[]{:S(2)}) collective-permute-start(f32[3,16,128]{2,1,0:T(8,128)S(1)} %get-tuple-element.32), channel_id=1, source_target_pairs={{0,15},{1,2},{2,1},{3,4},{4,3},{5,6},{6,5},{7,8},{8,7},{9,10},{10,... | collective-permute-start | bytes 73736 | tf_op jit(solution)/shard_map/ppermute | solution.py:720
  88.9 4.2 %collective-permute-start.7 = (f32[3,16,128]{2,1,0:T(8,128)S(1)}, f32[3,16,128]{2,1,0:T(8,128)S(1)}, u32[]{:S(2)}, u32[]{:S(2)}) collective-permute-start(f32[3,16,128]{2,1,0:T(8,128)S(1)} %get-tuple-element.33), channel_id=1, source_target_pairs={{0,1},{1,0},{2,3},{3,2},{4,5},{5,4},{6,7},{7,6},{8,9},{9,8},{10,11... | collective-permute-start | bytes 73736 | tf_op jit(solution)/shard_map/ppermute | solution.py:720
  93.1 0.8 collective-permute-done.7.near
  94.0 1.6 %all-to-all-done = f32[256,1,128]{2,1,0:T(1,128)S(1)} async-done(((f32[256,1,128]{2,1,0:T(1,128)}), f32[256,1,128]{2,1,0:T(1,128)S(1)}, u32[]{:S(2)}, u32[]{:S(2)}) %all-to-all-start) | async-done | bytes 131104 | tf_op jit(solution)/shard_map/all_to_all | solution.py:726
  95.6 1.6 %spread.1 = (f32[8,16,128]{2,1,0:T(8,128)}, f32[1]{0:T(128)}, f32[8]{0:T(128)}) custom-call(f32[8,16,128]{2,1,0:T(8,128)S(1)} %get-tuple-element.28.raw, f32[56,128]{1,0:T(8,128)S(1)} %collective-permute-done.4.low.xlow, f32[56,128]{1,0:T(8,128)S(1)} %collective-permute-done.5.high.xhigh, f32[3,16,128]{2,1,0:T(8,128)S(1)} %collective-permute-done.6.far, ...), custom_call_target="tpu_custom_call" | custom-call | flops 2000000 | bytes 368676 | tf_op jit(solution)/shard_map/spread/pallas_call | solution.py:248
  (10 shorter events, 0.0 us)
Async XLA Ops:
  0.6 19.6 %copy-start.3 = (s32[8,16,128]{2,1,0:T(8,128)S(1)}, s32[8,16,128]{2,1,0:T(8,128)}, u32[]{:S(2)}) copy-start(s32[8,16,128]{2,1,0:T(8,128)} %node.5) | copy-start | bytes 196612
  0.6 19.6 %copy-start.2 = (f32[8,16,128]{2,1,0:T(8,128)S(1)}, f32[8,16,128]{2,1,0:T(8,128)}, u32[]{:S(2)}) copy-start(f32[8,16,128]{2,1,0:T(8,128)} %design.3) | copy-start | bytes 196612
  0.7 19.6 %copy-start.1 = (f32[19,8,16,128]{3,2,1,0:T(8,128)S(1)}, f32[19,8,16,128]{3,2,1,0:T(8,128)}, u32[]{:S(2)}) copy-start(f32[19,8,16,128]{3,2,1,0:T(8,128)} %later_any.3) | copy-start | bytes 3735556
  0.7 19.6 %copy-start = (f32[19,8,16,128]{3,2,1,0:T(8,128)S(1)}, f32[19,8,16,128]{3,2,1,0:T(8,128)}, u32[]{:S(2)}) copy-start(f32[19,8,16,128]{3,2,1,0:T(8,128)} %fwd.3) | copy-start | bytes 3735556
  4.2 17.4 %collective-permute-start = (f32[53,8,128]{2,1,0:T(8,128)}, f32[53,8,128]{2,1,0:T(8,128)S(1)}, u32[]{:S(2)}, u32[]{:S(2)}) collective-permute-start(f32[53,8,128]{2,1,0:T(8,128)} %get-tuple-element.23), channel_id=1, source_target_pairs={{0,15},{1,2},{2,1},{3,4},{4,3},{5,6},{6,5},{7,8},{8,7},{9,10},{10,... | collective-permute-start | bytes 651272 | tf_op jit(solution)/shard_map/ppermute | solution.py:720
  16.2 5.3 %collective-permute-start.1 = (f32[53,8,128]{2,1,0:T(8,128)}, f32[53,8,128]{2,1,0:T(8,128)S(1)}, u32[]{:S(2)}, u32[]{:S(2)}) collective-permute-start(f32[53,8,128]{2,1,0:T(8,128)} %get-tuple-element.24), channel_id=1, source_target_pairs={{0,1},{1,0},{2,3},{3,2},{4,5},{5,4},{6,7},{7,6},{8,9},{9,8},{10,11... | collective-permute-start | bytes 651272 | tf_op jit(solution)/shard_map/ppermute | solution.py:720
  20.3 23.9 %copy-start.4 = (s32[8,16,128]{2,1,0:T(8,128)S(1)}, s32[8,16,128]{2,1,0:T(8,128)}, u32[]{:S(2)}) copy-start(s32[8,16,128]{2,1,0:T(8,128)} %region.1) | copy-start | bytes 196612
  21.9 21.5 %collective-permute-start.2 = (f32[1096,128]{1,0:T(8,128)S(1)}, f32[1096,128]{1,0:T(8,128)S(1)}, u32[]{:S(2)}, u32[]{:S(2)}) collective-permute-start(f32[1096,128]{1,0:T(8,128)S(1)} %get-tuple-element.25), channel_id=1, source_target_pairs={{0,16},{16,32},{32,48},{48,64},{64,80},{80,96},{96,112},{112,128},... | collective-permute-start | bytes 1683464 | tf_op jit(solution)/shard_map/ppermute | solution.py:713
  25.3 19.0 %collective-permute-start.3 = (f32[1096,128]{1,0:T(8,128)S(1)}, f32[1096,128]{1,0:T(8,128)S(1)}, u32[]{:S(2)}, u32[]{:S(2)}) collective-permute-start(f32[1096,128]{1,0:T(8,128)S(1)} %get-tuple-element.26), channel_id=1, source_target_pairs={{16,0},{32,16},{48,32},{64,48},{80,64},{96,80},{112,96},{128,112},... | collective-permute-start | bytes 1683464 | tf_op jit(solution)/shard_map/ppermute | solution.py:713
  51.3 10.0 %collective-permute-start.4 = (f32[56,128]{1,0:T(8,128)S(1)}, f32[56,128]{1,0:T(8,128)S(1)}, u32[]{:S(2)}, u32[]{:S(2)}) collective-permute-start(f32[56,128]{1,0:T(8,128)S(1)} %get-tuple-element.29), channel_id=1, source_target_pairs={{0,16},{16,32},{32,48},{48,64},{64,80},{80,96},{96,112},{112,128},... | collective-permute-start | bytes 86024 | tf_op jit(solution)/shard_map/ppermute | solution.py:713
  53.2 9.0 %collective-permute-start.5 = (f32[56,128]{1,0:T(8,128)S(1)}, f32[56,128]{1,0:T(8,128)S(1)}, u32[]{:S(2)}, u32[]{:S(2)}) collective-permute-start(f32[56,128]{1,0:T(8,128)S(1)} %get-tuple-element.30), channel_id=1, source_target_pairs={{16,0},{32,16},{48,32},{64,48},{80,64},{96,80},{112,96},{128,112},... | collective-permute-start | bytes 86024 | tf_op jit(solution)/shard_map/ppermute | solution.py:713
  62.9 32.7 %all-to-all-start = ((f32[256,1,128]{2,1,0:T(1,128)}), f32[256,1,128]{2,1,0:T(1,128)S(1)}, u32[]{:S(2)}, u32[]{:S(2)}) async-start(f32[256,1,128]{2,1,0:T(1,128)} %bitcast.1), calls=%async_computation | async-start | bytes 262144 | tf_op jit(solution)/shard_map/all_to_all | solution.py:726
  81.5 11.6 %collective-permute-start.6 = (f32[3,16,128]{2,1,0:T(8,128)S(1)}, f32[3,16,128]{2,1,0:T(8,128)S(1)}, u32[]{:S(2)}, u32[]{:S(2)}) collective-permute-start(f32[3,16,128]{2,1,0:T(8,128)S(1)} %get-tuple-element.32), channel_id=1, source_target_pairs={{0,15},{1,2},{2,1},{3,4},{4,3},{5,6},{6,5},{7,8},{8,7},{9,10},{10,... | collective-permute-start | bytes 73736 | tf_op jit(solution)/shard_map/ppermute | solution.py:720
  88.9 5.0 %collective-permute-start.7 = (f32[3,16,128]{2,1,0:T(8,128)S(1)}, f32[3,16,128]{2,1,0:T(8,128)S(1)}, u32[]{:S(2)}, u32[]{:S(2)}) collective-permute-start(f32[3,16,128]{2,1,0:T(8,128)S(1)} %get-tuple-element.33), channel_id=1, source_target_pairs={{0,1},{1,0},{2,3},{3,2},{4,5},{5,4},{6,7},{7,6},{8,9},{9,8},{10,11... | collective-permute-start | bytes 73736 | tf_op jit(solution)/shard_map/ppermute | solution.py:720

commit v5 on v4

--- a/solution.py
+++ b/solution.py
@@ -104,7 +104,7 @@
         return value
     z = lanes(value.shape)
     moved = pltpu.roll(value, (-c) % NZ, value.ndim - 1)
-    return jnp.where((z + c >= 0) & (z + c < NZ), moved, 0.0)
+    return jnp.where(z < NZ - c if c > 0 else z >= -c, moved, 0.0)
 
 
 def norm_row(shape):
@@ -119,14 +119,25 @@
     return result
 
 
+def fold_rows(wide, folded, starts):
+    def plane(x, carry):
+        for k, r in enumerate(starts):
+            tile = slice(8 * k, 8 * k + 8)
+            folded[0, x, tile, :] = wide[x, r : r + 8, :]
+            for b in range(1, RAD + 1):
+                folded[b, x, tile, :] = wide[x, r + b : r + b + 8, :] + wide[x, r - b : r - b + 8, :]
+        return carry
+
+    lax.fori_loop(0, folded.shape[1], plane, 0)
+
+
 def filter_rows(load):
-    sums = []
-    for s in CLASSES:
-        running = None
-        for a, b in TAPS[s]:
-            tile = load(a, b)
-            running = tile if running is None else running + tile
-        sums.append(running)
+    sums = [
+        add_all(
+            load(a, b) for a in range(-RAD, RAD + 1) for b in range(RAD + 1) if a * a + b * b == s
+        )
+        for s in CLASSES
+    ]
     result = None
     for c in range(RAD + 1):
         mixed = None
@@ -181,11 +192,12 @@
     keep = 1.0 - rate
     wall = node == 2.0
     scale = rate * density
+    scales = {w: w * scale for w in sorted({WEIGHTS[i] for i in which})}
     result = {}
     for i in which:
         a = along(i, u)
         form = rest if a is None else rest + a * (3.0 + 4.5 * a)
-        relaxed = keep * straight[i] + (WEIGHTS[i] * scale) * form
+        relaxed = keep * straight[i] + scales[WEIGHTS[i]] * form
         result[i] = jnp.where(wall, bounced[i], relaxed)
     return result
 
@@ -196,37 +208,38 @@
     keep = 1.0 - rate
     wall = node == 2.0
 
-    def weighted(select):
-        total = None
-        for w, group in ((1.0 / 18.0, range(1, 7)), (1.0 / 36.0, range(7, Q))):
-            up = [m[i] for i in group if select(VELOCITY[i]) > 0]
-            down = [m[i] for i in group if select(VELOCITY[i]) < 0]
-            if not up and not down:
-                continue
-            value = add_all(up)
-            if down:
-                value = value - add_all(down)
-            value = w * value
-            total = value if total is None else total + value
-        return total
-
-    zero = (1.0 / 3.0) * m[0] + weighted(lambda c: 1)
-    one = [weighted(lambda c, a=a: c[a]) for a in range(3)]
-    two = {}
-    for a in range(3):
-        for b in range(a, 3):
-            two[a, b] = two[b, a] = weighted(lambda c, a=a, b=b: c[a] * c[b])
+    both = {i: m[i] + m[i + 1] for i in range(1, Q, 2)}
+    odds = {i: m[i] - m[i + 1] for i in range(1, Q, 2)}
+    axis, edge = 1.0 / 18.0, 1.0 / 36.0
+    planes = [both[7] + both[9], both[11] + both[13], both[15] + both[17]]
+    zero = (1.0 / 3.0) * m[0] + axis * (both[1] + both[3] + both[5])
+    zero = zero + edge * (planes[0] + planes[1] + planes[2])
+    one = [
+        axis * odds[1] + edge * ((odds[7] + odds[9]) + (odds[11] + odds[13])),
+        axis * odds[3] + edge * ((odds[7] - odds[9]) + (odds[15] + odds[17])),
+        axis * odds[5] + edge * ((odds[11] - odds[13]) + (odds[15] - odds[17])),
+    ]
+    two = {
+        (0, 0): axis * both[1] + edge * (planes[0] + planes[1]),
+        (1, 1): axis * both[3] + edge * (planes[0] + planes[2]),
+        (2, 2): axis * both[5] + edge * (planes[1] + planes[2]),
+        (0, 1): edge * (both[7] - both[9]),
+        (0, 2): edge * (both[11] - both[13]),
+        (1, 2): edge * (both[15] - both[17]),
+    }
+    for a, b in ((0, 1), (0, 2), (1, 2)):
+        two[b, a] = two[a, b]
     bent = [two[a, 0] * u[0] + two[a, 1] * u[1] + two[a, 2] * u[2] for a in range(3)]
     dot = lambda p, q: p[0] * q[0] + p[1] * q[1] + p[2] * q[2]
     scalar = zero * (1.0 - 1.5 * dot(u, u)) + 3.0 * dot(one, u) + 4.5 * dot(bent, u)
     vector = [3.0 * (one[a] + 3.0 * bent[a] - zero * u[a]) for a in range(3)]
     start = rate * (scalar - dot(vector, u))
     slope = [(rate * factor) * v for v in vector]
-    result = []
-    for i in range(Q):
+    couplings = [start]
+    for i in range(1, Q, 2):
         lean = along(i, slope)
-        relaxed = keep * m[i] + (start if lean is None else start + lean)
-        result.append(jnp.where(wall, m[OPPOSITE[i]], relaxed))
+        couplings += [start + lean, start - lean]
+    result = [jnp.where(wall, m[OPPOSITE[i]], keep * m[i] + couplings[i]) for i in range(Q)]
     gradient = jnp.where(wall, 0.0, rate * density * dot(vector, plain))
     return result, gradient
 
@@ -422,7 +435,7 @@
 def main_body(
     fwd, later_any, design, node, region, xlow, xhigh, far, near,
     adjoint_any, raw, part, up_out, down_out,
-    ylow, yhigh, wide, kinds, fine, post, later, mid, flow, flux, first, adjoint, sem, sems,
+    ylow, yhigh, wide, folded, kinds, fine, post, later, mid, flow, flux, first, adjoint, sem, sems,
 ):
     copy = pltpu.make_async_copy(later_any, later.at[:, 2 : 2 + BX, ROW : ROW + BY, :], sem)
     copy.start()
@@ -452,9 +465,12 @@
             kinds[2 + x, row : row + 1, :] = message[slot(1, sign, ring, KIND), x : x + 1, :]
     inverse_norm = 1.0 / norm_row((8, NZ))
 
+    fold_rows(wide, folded, (4, 12, 20))
+
     def filter_plane(x, carry):
-        for r in (4, 12, 20):
-            value = filter_rows(lambda a, b: wide[x + RAD + a, r + b : r + b + 8, :]) * inverse_norm
+        for k, r in enumerate((4, 12, 20)):
+            tile = slice(8 * k, 8 * k + 8)
+            value = filter_rows(lambda a, b: folded[b, x + RAD + a, tile, :]) * inverse_norm
             fine[x, r : r + 8, :] = value
         return carry
 
@@ -617,6 +633,7 @@
             pltpu.VMEM((MSG, BX, NZ), F32),
             pltpu.VMEM((MSG, BX, NZ), F32),
             pltpu.VMEM((BX + 2 * DEEP, PADY, NZ), F32),
+            pltpu.VMEM((RAD + 1, BX + 2 * DEEP, 24, NZ), F32),
             pltpu.VMEM((EX, PADY, NZ), F32),
             pltpu.VMEM((EX, PADY, NZ), F32),
             pltpu.VMEM((Q, EX, PADY, NZ), F32),
@@ -664,7 +681,7 @@
     )
 
 
-def spread_body(raw, xlow, xhigh, far, near, rows, out, objective, volumes, ylow, yhigh, wide):
+def spread_body(raw, xlow, xhigh, far, near, rows, out, objective, volumes, ylow, yhigh, wide, folded):
     to_sides("gy", far, near, ylow, yhigh)
     wide[RAD : RAD + BX, ROW : ROW + BY, :] = raw[...]
     for j in range(RAD):
@@ -675,10 +692,11 @@
             wide[x, ROW - RAD + j : ROW - RAD + j + 1, :] = ylow[j, x : x + 1, :]
             wide[x, ROW + BY + j : ROW + BY + j + 1, :] = yhigh[j, x : x + 1, :]
 
+    fold_rows(wide, folded, (ROW, ROW + 8))
+
     def plane(x, carry):
         for h in (0, 8):
-            at = ROW + h
-            out[x, h : h + 8, :] = filter_rows(lambda a, b: wide[x + RAD + a, at + b : at + b + 8, :])
+            out[x, h : h + 8, :] = filter_rows(lambda a, b: folded[b, x + RAD + a, h : h + 8, :])
         return carry
 
     lax.fori_loop(0, BX, plane, 0)
@@ -699,7 +717,8 @@
         [(BX, BY, NZ), (1,), (REG,)],
         ins,
         [whole(x.shape) for x in ins],
-        scratch=(pltpu.VMEM((RAD, BY, NZ), F32),) * 2 + (pltpu.VMEM((BX + 2 * RAD, PADY, NZ), F32),),
+        scratch=(pltpu.VMEM((RAD, BY, NZ), F32),) * 2
+        + (pltpu.VMEM((BX + 2 * RAD, PADY, NZ), F32), pltpu.VMEM((RAD + 1, BX + 2 * RAD, BY, NZ), F32)),
         flops=2000000,
         name="spread",
         out_specs=[whole((BX, BY, NZ)), scalar(), scalar()],

time: 98.3 us -> 98.2 us (level)
  no operation moved by 1% of the time
where the time goes in v5:
time: 98.2 us; the launch traced here: 97 us
  starting transfers between devices  68.6 us (70%)
  waiting for transfers between devices  14.6 us (15%)
  Pallas kernels  13 us (13%)
    ppermute x4, starting transfers between devices, swap(): return (lax.ppermute(far, axis, outer), lax.ppermute(near, axis, inner))  27.6 us
    ppermute x4, starting transfers between devices, exchange(): return (lax.ppermute(up, axis, forward), lax.ppermute(down, axis, backward))  22.4 us
    all_to_all x1, starting transfers between devices, share(): lax.all_to_all(rows, ('gx', 'gy'), 0, 0, tiled=True, axis_index_groups=gr...  18.6 us
    pallas_call x6, Pallas kernels, call(): pl.pallas_call(body, out_shape=[jax.ShapeDtypeStruct(o, F32) for o in out...  13 us
    ppermute x4, waiting for transfers between devices, exchange(): return (lax.ppermute(up, axis, forward), lax.ppermute(down, axis, backward))  10.9 us
    ppermute x4, waiting for transfers between devices, swap(): return (lax.ppermute(far, axis, outer), lax.ppermute(near, axis, inner))  2.07 us
  transfers between devices with their start and end apart: 9, of which 6 were waited for; matrix products, arithmetic and copies ran while one was open for 0% of the time, Pallas kernels for 0%

profile of v5, /device:TPU:1, one launch (start us, length us, event | category | flops | bytes accessed | tf_op | source)
XLA Modules:
  0.0 97.0 jit_solution(10034943556072074824)
XLA Ops:
  0.7 3.5 %first_y.1 = (f32[53,8,128]{2,1,0:T(8,128)}, f32[53,8,128]{2,1,0:T(8,128)}) custom-call(f32[19,8,16,128]{3,2,1,0:T(8,128)} %fwd.3, f32[19,8,16,128]{3,2,1,0:T(8,128)} %later_any.3, f32[8,16,128]{2,1,0:T(8,128)} %design.3, s32[8,16,128]{2,1,0:T(8,128)} %node.5), custom_call_target="tpu_custom_call" | custom-call | flops 800000 | bytes 3055616 | tf_op jit(solution)/shard_map/first_y/pallas_call | solution.py:261
  4.2 12.0 %collective-permute-start = (f32[53,8,128]{2,1,0:T(8,128)}, f32[53,8,128]{2,1,0:T(8,128)S(1)}, u32[]{:S(2)}, u32[]{:S(2)}) collective-permute-start(f32[53,8,128]{2,1,0:T(8,128)} %get-tuple-element.23), channel_id=1, source_target_pairs={{0,15},{1,2},{2,1},{3,4},{4,3},{5,6},{6,5},{7,8},{8,7},{9,10},{10,... | collective-permute-start | bytes 651272 | tf_op jit(solution)/shard_map/ppermute | solution.py:739
  16.2 3.9 %collective-permute-start.1 = (f32[53,8,128]{2,1,0:T(8,128)}, f32[53,8,128]{2,1,0:T(8,128)S(1)}, u32[]{:S(2)}, u32[]{:S(2)}) collective-permute-start(f32[53,8,128]{2,1,0:T(8,128)} %get-tuple-element.24), channel_id=1, source_target_pairs={{0,1},{1,0},{2,3},{3,2},{4,5},{5,4},{6,7},{7,6},{8,9},{9,8},{10,11... | collective-permute-start | bytes 651272 | tf_op jit(solution)/shard_map/ppermute | solution.py:739
  20.2 0.1 first_x.1
  20.3 0.0 copy-start.4
  20.3 1.2 %collective-permute-done.far = f32[53,8,128]{2,1,0:T(8,128)S(1)} collective-permute-done((f32[53,8,128]{2,1,0:T(8,128)}, f32[53,8,128]{2,1,0:T(8,128)S(1)}, u32[]{:S(2)}, u32[]{:S(2)}) %collective-permute-start) | collective-permute-done | bytes 217120 | tf_op jit(solution)/shard_map/ppermute | solution.py:739
  21.6 0.0 collective-permute-done.1.near
  21.6 0.3 join_x.1
  21.9 3.4 %collective-permute-start.2 = (f32[1096,128]{1,0:T(8,128)S(1)}, f32[1096,128]{1,0:T(8,128)S(1)}, u32[]{:S(2)}, u32[]{:S(2)}) collective-permute-start(f32[1096,128]{1,0:T(8,128)S(1)} %get-tuple-element.25), channel_id=1, source_target_pairs={{0,16},{16,32},{32,48},{48,64},{64,80},{80,96},{96,112},{112,128},... | collective-permute-start | bytes 1683464 | tf_op jit(solution)/shard_map/ppermute | solution.py:732
  25.3 9.1 %collective-permute-start.3 = (f32[1096,128]{1,0:T(8,128)S(1)}, f32[1096,128]{1,0:T(8,128)S(1)}, u32[]{:S(2)}, u32[]{:S(2)}) collective-permute-start(f32[1096,128]{1,0:T(8,128)S(1)} %get-tuple-element.26), channel_id=1, source_target_pairs={{16,0},{32,16},{48,32},{64,48},{80,64},{96,80},{112,96},{128,112},... | collective-permute-start | bytes 1683464 | tf_op jit(solution)/shard_map/ppermute | solution.py:732
  34.3 9.0 %collective-permute-done.2.xlow = f32[1096,128]{1,0:T(8,128)S(1)} collective-permute-done((f32[1096,128]{1,0:T(8,128)S(1)}, f32[1096,128]{1,0:T(8,128)S(1)}, u32[]{:S(2)}, u32[]{:S(2)}) %collective-permute-start.2) | collective-permute-done | bytes 561184 | tf_op jit(solution)/shard_map/ppermute | solution.py:732
  43.4 0.9 collective-permute-done.3.xhigh
  44.3 6.9 %main.1 = (f32[19,8,16,128]{3,2,1,0:T(8,128)}, f32[8,16,128]{2,1,0:T(8,128)S(1)}, f32[8,128]{1,0:T(8,128)S(1)}, f32[56,128]{1,0:T(8,128)S(1)}, f32[56,128]{1,0:T(8,128)S(1)}) custom-call(f32[19,8,16,128]{3,2,1,0:T(8,128)S(1)} %copy-done, f32[19,8,16,128]{3,2,1,0:T(8,128)S(1)} %copy-done.1, f32[8,16,128]{2,1,0:T(8,128)S(1)} %copy-done.2, ...), custom_call_target="tpu_custom_call" | custom-call | flops 30000000 | bytes 5615616 | tf_op jit(solution)/shard_map/main/pallas_call | solution.py:261
  51.2 1.9 %collective-permute-start.4 = (f32[56,128]{1,0:T(8,128)S(1)}, f32[56,128]{1,0:T(8,128)S(1)}, u32[]{:S(2)}, u32[]{:S(2)}) collective-permute-start(f32[56,128]{1,0:T(8,128)S(1)} %get-tuple-element.29), channel_id=1, source_target_pairs={{0,16},{16,32},{32,48},{48,64},{64,80},{80,96},{96,112},{112,128},... | collective-permute-start | bytes 86024 | tf_op jit(solution)/shard_map/ppermute | solution.py:732
  53.1 8.0 %collective-permute-start.5 = (f32[56,128]{1,0:T(8,128)S(1)}, f32[56,128]{1,0:T(8,128)S(1)}, u32[]{:S(2)}, u32[]{:S(2)}) collective-permute-start(f32[56,128]{1,0:T(8,128)S(1)} %get-tuple-element.30), channel_id=1, source_target_pairs={{16,0},{32,16},{48,32},{64,48},{80,64},{96,80},{112,96},{128,112},... | collective-permute-start | bytes 86024 | tf_op jit(solution)/shard_map/ppermute | solution.py:732
  61.1 1.0 collective-permute-done.5.high.xhigh
  62.1 0.7 raw_y.1
  62.8 18.6 %all-to-all-start = ((f32[256,1,128]{2,1,0:T(1,128)}), f32[256,1,128]{2,1,0:T(1,128)S(1)}, u32[]{:S(2)}, u32[]{:S(2)}) async-start(f32[256,1,128]{2,1,0:T(1,128)} %bitcast.1), calls=%async_computation | async-start | bytes 262144 | tf_op jit(solution)/shard_map/all_to_all | solution.py:745
  81.4 7.4 %collective-permute-start.6 = (f32[3,16,128]{2,1,0:T(8,128)S(1)}, f32[3,16,128]{2,1,0:T(8,128)S(1)}, u32[]{:S(2)}, u32[]{:S(2)}) collective-permute-start(f32[3,16,128]{2,1,0:T(8,128)S(1)} %get-tuple-element.32), channel_id=1, source_target_pairs={{0,15},{1,2},{2,1},{3,4},{4,3},{5,6},{6,5},{7,8},{8,7},{9,10},{10,... | collective-permute-start | bytes 73736 | tf_op jit(solution)/shard_map/ppermute | solution.py:739
  88.8 4.2 %collective-permute-start.7 = (f32[3,16,128]{2,1,0:T(8,128)S(1)}, f32[3,16,128]{2,1,0:T(8,128)S(1)}, u32[]{:S(2)}, u32[]{:S(2)}) collective-permute-start(f32[3,16,128]{2,1,0:T(8,128)S(1)} %get-tuple-element.33), channel_id=1, source_target_pairs={{0,1},{1,0},{2,3},{3,2},{4,5},{5,4},{6,7},{7,6},{8,9},{9,8},{10,11... | collective-permute-start | bytes 73736 | tf_op jit(solution)/shard_map/ppermute | solution.py:739
  93.0 0.0 collective-permute-done.6.far
  93.0 0.8 collective-permute-done.7.near
  93.8 1.6 %all-to-all-done = f32[256,1,128]{2,1,0:T(1,128)S(1)} async-done(((f32[256,1,128]{2,1,0:T(1,128)}), f32[256,1,128]{2,1,0:T(1,128)S(1)}, u32[]{:S(2)}, u32[]{:S(2)}) %all-to-all-start) | async-done | bytes 131104 | tf_op jit(solution)/shard_map/all_to_all | solution.py:745
  95.5 1.6 %spread.1 = (f32[8,16,128]{2,1,0:T(8,128)}, f32[1]{0:T(128)}, f32[8]{0:T(128)}) custom-call(f32[8,16,128]{2,1,0:T(8,128)S(1)} %get-tuple-element.28.raw, f32[56,128]{1,0:T(8,128)S(1)} %collective-permute-done.4.low.xlow, f32[56,128]{1,0:T(8,128)S(1)} %collective-permute-done.5.high.xhigh, f32[3,16,128]{2,1,0:T(8,128)S(1)} %collective-permute-done.6.far, ...), custom_call_target="tpu_custom_call" | custom-call | flops 2000000 | bytes 368676 | tf_op jit(solution)/shard_map/spread/pallas_call | solution.py:261
  (10 shorter events, 0.0 us)
Async XLA Ops:
  0.6 19.6 %copy-start.3 = (s32[8,16,128]{2,1,0:T(8,128)S(1)}, s32[8,16,128]{2,1,0:T(8,128)}, u32[]{:S(2)}) copy-start(s32[8,16,128]{2,1,0:T(8,128)} %node.5) | copy-start | bytes 196612
  0.6 19.6 %copy-start.2 = (f32[8,16,128]{2,1,0:T(8,128)S(1)}, f32[8,16,128]{2,1,0:T(8,128)}, u32[]{:S(2)}) copy-start(f32[8,16,128]{2,1,0:T(8,128)} %design.3) | copy-start | bytes 196612
  0.7 19.6 %copy-start.1 = (f32[19,8,16,128]{3,2,1,0:T(8,128)S(1)}, f32[19,8,16,128]{3,2,1,0:T(8,128)}, u32[]{:S(2)}) copy-start(f32[19,8,16,128]{3,2,1,0:T(8,128)} %later_any.3) | copy-start | bytes 3735556
  0.7 19.6 %copy-start = (f32[19,8,16,128]{3,2,1,0:T(8,128)S(1)}, f32[19,8,16,128]{3,2,1,0:T(8,128)}, u32[]{:S(2)}) copy-start(f32[19,8,16,128]{3,2,1,0:T(8,128)} %fwd.3) | copy-start | bytes 3735556
  4.2 17.4 %collective-permute-start = (f32[53,8,128]{2,1,0:T(8,128)}, f32[53,8,128]{2,1,0:T(8,128)S(1)}, u32[]{:S(2)}, u32[]{:S(2)}) collective-permute-start(f32[53,8,128]{2,1,0:T(8,128)} %get-tuple-element.23), channel_id=1, source_target_pairs={{0,15},{1,2},{2,1},{3,4},{4,3},{5,6},{6,5},{7,8},{8,7},{9,10},{10,... | collective-permute-start | bytes 651272 | tf_op jit(solution)/shard_map/ppermute | solution.py:739
  16.2 5.3 %collective-permute-start.1 = (f32[53,8,128]{2,1,0:T(8,128)}, f32[53,8,128]{2,1,0:T(8,128)S(1)}, u32[]{:S(2)}, u32[]{:S(2)}) collective-permute-start(f32[53,8,128]{2,1,0:T(8,128)} %get-tuple-element.24), channel_id=1, source_target_pairs={{0,1},{1,0},{2,3},{3,2},{4,5},{5,4},{6,7},{7,6},{8,9},{9,8},{10,11... | collective-permute-start | bytes 651272 | tf_op jit(solution)/shard_map/ppermute | solution.py:739
  20.3 23.9 %copy-start.4 = (s32[8,16,128]{2,1,0:T(8,128)S(1)}, s32[8,16,128]{2,1,0:T(8,128)}, u32[]{:S(2)}) copy-start(s32[8,16,128]{2,1,0:T(8,128)} %region.1) | copy-start | bytes 196612
  21.9 21.5 %collective-permute-start.2 = (f32[1096,128]{1,0:T(8,128)S(1)}, f32[1096,128]{1,0:T(8,128)S(1)}, u32[]{:S(2)}, u32[]{:S(2)}) collective-permute-start(f32[1096,128]{1,0:T(8,128)S(1)} %get-tuple-element.25), channel_id=1, source_target_pairs={{0,16},{16,32},{32,48},{48,64},{64,80},{80,96},{96,112},{112,128},... | collective-permute-start | bytes 1683464 | tf_op jit(solution)/shard_map/ppermute | solution.py:732
  25.3 19.0 %collective-permute-start.3 = (f32[1096,128]{1,0:T(8,128)S(1)}, f32[1096,128]{1,0:T(8,128)S(1)}, u32[]{:S(2)}, u32[]{:S(2)}) collective-permute-start(f32[1096,128]{1,0:T(8,128)S(1)} %get-tuple-element.26), channel_id=1, source_target_pairs={{16,0},{32,16},{48,32},{64,48},{80,64},{96,80},{112,96},{128,112},... | collective-permute-start | bytes 1683464 | tf_op jit(solution)/shard_map/ppermute | solution.py:732
  51.2 10.0 %collective-permute-start.4 = (f32[56,128]{1,0:T(8,128)S(1)}, f32[56,128]{1,0:T(8,128)S(1)}, u32[]{:S(2)}, u32[]{:S(2)}) collective-permute-start(f32[56,128]{1,0:T(8,128)S(1)} %get-tuple-element.29), channel_id=1, source_target_pairs={{0,16},{16,32},{32,48},{48,64},{64,80},{80,96},{96,112},{112,128},... | collective-permute-start | bytes 86024 | tf_op jit(solution)/shard_map/ppermute | solution.py:732
  53.1 9.0 %collective-permute-start.5 = (f32[56,128]{1,0:T(8,128)S(1)}, f32[56,128]{1,0:T(8,128)S(1)}, u32[]{:S(2)}, u32[]{:S(2)}) collective-permute-start(f32[56,128]{1,0:T(8,128)S(1)} %get-tuple-element.30), channel_id=1, source_target_pairs={{16,0},{32,16},{48,32},{64,48},{80,64},{96,80},{112,96},{128,112},... | collective-permute-start | bytes 86024 | tf_op jit(solution)/shard_map/ppermute | solution.py:732
  62.8 32.7 %all-to-all-start = ((f32[256,1,128]{2,1,0:T(1,128)}), f32[256,1,128]{2,1,0:T(1,128)S(1)}, u32[]{:S(2)}, u32[]{:S(2)}) async-start(f32[256,1,128]{2,1,0:T(1,128)} %bitcast.1), calls=%async_computation | async-start | bytes 262144 | tf_op jit(solution)/shard_map/all_to_all | solution.py:745
  81.4 11.6 %collective-permute-start.6 = (f32[3,16,128]{2,1,0:T(8,128)S(1)}, f32[3,16,128]{2,1,0:T(8,128)S(1)}, u32[]{:S(2)}, u32[]{:S(2)}) collective-permute-start(f32[3,16,128]{2,1,0:T(8,128)S(1)} %get-tuple-element.32), channel_id=1, source_target_pairs={{0,15},{1,2},{2,1},{3,4},{4,3},{5,6},{6,5},{7,8},{8,7},{9,10},{10,... | collective-permute-start | bytes 73736 | tf_op jit(solution)/shard_map/ppermute | solution.py:739
  88.8 5.0 %collective-permute-start.7 = (f32[3,16,128]{2,1,0:T(8,128)S(1)}, f32[3,16,128]{2,1,0:T(8,128)S(1)}, u32[]{:S(2)}, u32[]{:S(2)}) collective-permute-start(f32[3,16,128]{2,1,0:T(8,128)S(1)} %get-tuple-element.33), channel_id=1, source_target_pairs={{0,1},{1,0},{2,3},{3,2},{4,5},{5,4},{6,7},{7,6},{8,9},{9,8},{10,11... | collective-permute-start | bytes 73736 | tf_op jit(solution)/shard_map/ppermute | solution.py:739

commit v6 on v5

--- a/solution.py
+++ b/solution.py
@@ -681,7 +681,7 @@
     )
 
 
-def spread_body(raw, xlow, xhigh, far, near, rows, out, objective, volumes, ylow, yhigh, wide, folded):
+def spread_body(raw, xlow, xhigh, far, near, out, ylow, yhigh, wide, folded):
     to_sides("gy", far, near, ylow, yhigh)
     wide[RAD : RAD + BX, ROW : ROW + BY, :] = raw[...]
     for j in range(RAD):
@@ -700,6 +700,9 @@
         return carry
 
     lax.fori_loop(0, BX, plane, 0)
+
+
+def finish_body(rows, objective, volumes):
     total = add_all(rows[k : k + 8, :] for k in range(0, rows.shape[0], 8))
     lane = lanes((8, NZ))
     for r in range(REG + 1):
@@ -710,19 +713,30 @@
             objective[0] = value
 
 
-def spread(raw, xlow, xhigh, far, near, rows):
-    ins = (raw, xlow, xhigh, far, near, rows)
+def finish(rows):
+    return call(
+        finish_body,
+        [(1,), (REG,)],
+        (rows,),
+        [whole(rows.shape)],
+        flops=100000,
+        name="finish",
+        out_specs=[scalar(), scalar()],
+    )
+
+
+def spread(raw, xlow, xhigh, far, near):
+    ins = (raw, xlow, xhigh, far, near)
     return call(
         spread_body,
-        [(BX, BY, NZ), (1,), (REG,)],
+        [(BX, BY, NZ)],
         ins,
         [whole(x.shape) for x in ins],
         scratch=(pltpu.VMEM((RAD, BY, NZ), F32),) * 2
         + (pltpu.VMEM((BX + 2 * RAD, PADY, NZ), F32), pltpu.VMEM((RAD + 1, BX + 2 * RAD, BY, NZ), F32)),
         flops=2000000,
         name="spread",
-        out_specs=[whole((BX, BY, NZ)), scalar(), scalar()],
-    )
+    )[0]
 
 
 def exchange(up, down, axis):
@@ -757,7 +771,8 @@
     far, near, rows = raw_y(raw, part, xlow, xhigh, pairs)
     rows = share(rows)
     far, near = swap(far, near, "gy")
-    sensitivity, objective, volumes = spread(raw, xlow, xhigh, far, near, rows)
+    sensitivity = spread(raw, xlow, xhigh, far, near)
+    objective, volumes = finish(rows)
     return adjoint, sensitivity, objective[0], volumes
 
 

time: 98.2 us -> 97.8 us (level)
  waiting for transfers between devices: 14.6 us -> 13 us
    all_to_all x1, waiting for transfers between devices: 1.65 us -> 0.09 us  [share(): lax.all_to_all(rows, ('gx', 'gy'), 0, 0, tiled=True, axis_index_groups=gr...]
    pallas_call x6 -> x7, Pallas kernels: 13 us -> 13.7 us  [call(): pl.pallas_call(body, out_shape=[jax.ShapeDtypeStruct(o, F32) for o in out...]
  transfers between devices with their start and end apart: 9 -> 9, of which waited for: 6 -> 6; matrix products, arithmetic and copies ran while one was open for 0% -> 0% of each run, Pallas kernels for 0% -> 2%
where the time goes in v6:
time: 97.8 us; the launch traced here: 96.1 us
  starting transfers between devices  68.6 us (70%)
  Pallas kernels  13.7 us (14%)
  waiting for transfers between devices  13 us (13%)
    ppermute x4, starting transfers between devices, swap(): return (lax.ppermute(far, axis, outer), lax.ppermute(near, axis, inner))  27.6 us
    ppermute x4, starting transfers between devices, exchange(): return (lax.ppermute(up, axis, forward), lax.ppermute(down, axis, backward))  22.4 us
    all_to_all x1, starting transfers between devices, share(): lax.all_to_all(rows, ('gx', 'gy'), 0, 0, tiled=True, axis_index_groups=gr...  18.6 us
    pallas_call x7, Pallas kernels, call(): pl.pallas_call(body, out_shape=[jax.ShapeDtypeStruct(o, F32) for o in out...  13.7 us
    ppermute x4, waiting for transfers between devices, exchange(): return (lax.ppermute(up, axis, forward), lax.ppermute(down, axis, backward))  10.9 us
    ppermute x4, waiting for transfers between devices, swap(): return (lax.ppermute(far, axis, outer), lax.ppermute(near, axis, inner))  2.07 us
  transfers between devices with their start and end apart: 9, of which 6 were waited for; matrix products, arithmetic and copies ran while one was open for 0% of the time, Pallas kernels for 2%

profile of v6, /device:TPU:1, one launch (start us, length us, event | category | flops | bytes accessed | tf_op | source)
XLA Modules:
  0.0 96.1 jit_solution(5499788090269994798)
XLA Ops:
  0.7 3.5 %first_y.1 = (f32[53,8,128]{2,1,0:T(8,128)}, f32[53,8,128]{2,1,0:T(8,128)}) custom-call(f32[19,8,16,128]{3,2,1,0:T(8,128)} %fwd.3, f32[19,8,16,128]{3,2,1,0:T(8,128)} %later_any.3, f32[8,16,128]{2,1,0:T(8,128)} %design.3, s32[8,16,128]{2,1,0:T(8,128)} %node.5), custom_call_target="tpu_custom_call" | custom-call | flops 800000 | bytes 3055616 | tf_op jit(solution)/shard_map/first_y/pallas_call | solution.py:261
  4.2 12.0 %collective-permute-start = (f32[53,8,128]{2,1,0:T(8,128)}, f32[53,8,128]{2,1,0:T(8,128)S(1)}, u32[]{:S(2)}, u32[]{:S(2)}) collective-permute-start(f32[53,8,128]{2,1,0:T(8,128)} %get-tuple-element.22), channel_id=1, source_target_pairs={{0,15},{1,2},{2,1},{3,4},{4,3},{5,6},{6,5},{7,8},{8,7},{9,10},{10,... | collective-permute-start | bytes 651272 | tf_op jit(solution)/shard_map/ppermute | solution.py:753
  16.2 3.9 %collective-permute-start.1 = (f32[53,8,128]{2,1,0:T(8,128)}, f32[53,8,128]{2,1,0:T(8,128)S(1)}, u32[]{:S(2)}, u32[]{:S(2)}) collective-permute-start(f32[53,8,128]{2,1,0:T(8,128)} %get-tuple-element.23), channel_id=1, source_target_pairs={{0,1},{1,0},{2,3},{3,2},{4,5},{5,4},{6,7},{7,6},{8,9},{9,8},{10,11... | collective-permute-start | bytes 651272 | tf_op jit(solution)/shard_map/ppermute | solution.py:753
  20.2 0.1 first_x.1
  20.3 0.0 copy-start.4
  20.3 1.2 %collective-permute-done.far = f32[53,8,128]{2,1,0:T(8,128)S(1)} collective-permute-done((f32[53,8,128]{2,1,0:T(8,128)}, f32[53,8,128]{2,1,0:T(8,128)S(1)}, u32[]{:S(2)}, u32[]{:S(2)}) %collective-permute-start) | collective-permute-done | bytes 217120 | tf_op jit(solution)/shard_map/ppermute | solution.py:753
  21.6 0.0 collective-permute-done.1.near
  21.6 0.3 join_x.1
  21.9 3.4 %collective-permute-start.2 = (f32[1096,128]{1,0:T(8,128)S(1)}, f32[1096,128]{1,0:T(8,128)S(1)}, u32[]{:S(2)}, u32[]{:S(2)}) collective-permute-start(f32[1096,128]{1,0:T(8,128)S(1)} %get-tuple-element.24), channel_id=1, source_target_pairs={{0,16},{16,32},{32,48},{48,64},{64,80},{80,96},{96,112},{112,128},... | collective-permute-start | bytes 1683464 | tf_op jit(solution)/shard_map/ppermute | solution.py:746
  25.3 9.1 %collective-permute-start.3 = (f32[1096,128]{1,0:T(8,128)S(1)}, f32[1096,128]{1,0:T(8,128)S(1)}, u32[]{:S(2)}, u32[]{:S(2)}) collective-permute-start(f32[1096,128]{1,0:T(8,128)S(1)} %get-tuple-element.25), channel_id=1, source_target_pairs={{16,0},{32,16},{48,32},{64,48},{80,64},{96,80},{112,96},{128,112},... | collective-permute-start | bytes 1683464 | tf_op jit(solution)/shard_map/ppermute | solution.py:746
  34.3 9.0 %collective-permute-done.2.xlow = f32[1096,128]{1,0:T(8,128)S(1)} collective-permute-done((f32[1096,128]{1,0:T(8,128)S(1)}, f32[1096,128]{1,0:T(8,128)S(1)}, u32[]{:S(2)}, u32[]{:S(2)}) %collective-permute-start.2) | collective-permute-done | bytes 561184 | tf_op jit(solution)/shard_map/ppermute | solution.py:746
  43.4 0.9 collective-permute-done.3.xhigh
  44.3 6.9 %main.1 = (f32[19,8,16,128]{3,2,1,0:T(8,128)}, f32[8,16,128]{2,1,0:T(8,128)S(1)}, f32[8,128]{1,0:T(8,128)S(1)}, f32[56,128]{1,0:T(8,128)S(1)}, f32[56,128]{1,0:T(8,128)S(1)}) custom-call(f32[19,8,16,128]{3,2,1,0:T(8,128)S(1)} %copy-done, f32[19,8,16,128]{3,2,1,0:T(8,128)S(1)} %copy-done.1, f32[8,16,128]{2,1,0:T(8,128)S(1)} %copy-done.2, ...), custom_call_target="tpu_custom_call" | custom-call | flops 30000000 | bytes 5615616 | tf_op jit(solution)/shard_map/main/pallas_call | solution.py:261
  51.2 1.9 %collective-permute-start.4 = (f32[56,128]{1,0:T(8,128)S(1)}, f32[56,128]{1,0:T(8,128)S(1)}, u32[]{:S(2)}, u32[]{:S(2)}) collective-permute-start(f32[56,128]{1,0:T(8,128)S(1)} %get-tuple-element.28), channel_id=1, source_target_pairs={{0,16},{16,32},{32,48},{48,64},{64,80},{80,96},{96,112},{112,128},... | collective-permute-start | bytes 86024 | tf_op jit(solution)/shard_map/ppermute | solution.py:746
  53.1 8.0 %collective-permute-start.5 = (f32[56,128]{1,0:T(8,128)S(1)}, f32[56,128]{1,0:T(8,128)S(1)}, u32[]{:S(2)}, u32[]{:S(2)}) collective-permute-start(f32[56,128]{1,0:T(8,128)S(1)} %get-tuple-element.29), channel_id=1, source_target_pairs={{16,0},{32,16},{48,32},{64,48},{80,64},{96,80},{112,96},{128,112},... | collective-permute-start | bytes 86024 | tf_op jit(solution)/shard_map/ppermute | solution.py:746
  61.1 1.0 collective-permute-done.5.high.xhigh
  62.1 0.7 raw_y.1
  62.8 18.6 %all-to-all-start = ((f32[256,1,128]{2,1,0:T(1,128)}), f32[256,1,128]{2,1,0:T(1,128)S(1)}, u32[]{:S(2)}, u32[]{:S(2)}) async-start(f32[256,1,128]{2,1,0:T(1,128)} %bitcast.1), calls=%async_computation | async-start | bytes 262144 | tf_op jit(solution)/shard_map/all_to_all | solution.py:759
  81.4 7.4 %collective-permute-start.6 = (f32[3,16,128]{2,1,0:T(8,128)S(1)}, f32[3,16,128]{2,1,0:T(8,128)S(1)}, u32[]{:S(2)}, u32[]{:S(2)}) collective-permute-start(f32[3,16,128]{2,1,0:T(8,128)S(1)} %get-tuple-element.31), channel_id=1, source_target_pairs={{0,15},{1,2},{2,1},{3,4},{4,3},{5,6},{6,5},{7,8},{8,7},{9,10},{10,... | collective-permute-start | bytes 73736 | tf_op jit(solution)/shard_map/ppermute | solution.py:753
  88.8 4.2 %collective-permute-start.7 = (f32[3,16,128]{2,1,0:T(8,128)S(1)}, f32[3,16,128]{2,1,0:T(8,128)S(1)}, u32[]{:S(2)}, u32[]{:S(2)}) collective-permute-start(f32[3,16,128]{2,1,0:T(8,128)S(1)} %get-tuple-element.32), channel_id=1, source_target_pairs={{0,1},{1,0},{2,3},{3,2},{4,5},{5,4},{6,7},{7,6},{8,9},{9,8},{10,11... | collective-permute-start | bytes 73736 | tf_op jit(solution)/shard_map/ppermute | solution.py:753
  93.0 0.8 collective-permute-done.7.near
  93.8 1.6 %spread.1 = f32[8,16,128]{2,1,0:T(8,128)} custom-call(f32[8,16,128]{2,1,0:T(8,128)S(1)} %get-tuple-element.27.raw, f32[56,128]{1,0:T(8,128)S(1)} %collective-permute-done.4.low.xlow, f32[56,128]{1,0:T(8,128)S(1)} %collective-permute-done.5.high.xhigh, f32[3,16,128]{2,1,0:T(8,128)S(1)} %collective-permute-done.6.far, ...), custom_call_target="tpu_custom_call" | custom-call | flops 2000000 | bytes 237568 | tf_op jit(solution)/shard_map/spread/pallas_call | solution.py:261
  95.4 0.1 all-to-all-done
  95.5 0.7 finish.1
  (11 shorter events, 0.0 us)
Async XLA Ops:
  0.6 19.6 %copy-start.3 = (s32[8,16,128]{2,1,0:T(8,128)S(1)}, s32[8,16,128]{2,1,0:T(8,128)}, u32[]{:S(2)}) copy-start(s32[8,16,128]{2,1,0:T(8,128)} %node.5) | copy-start | bytes 196612
  0.6 19.6 %copy-start.2 = (f32[8,16,128]{2,1,0:T(8,128)S(1)}, f32[8,16,128]{2,1,0:T(8,128)}, u32[]{:S(2)}) copy-start(f32[8,16,128]{2,1,0:T(8,128)} %design.3) | copy-start | bytes 196612
  0.7 19.6 %copy-start.1 = (f32[19,8,16,128]{3,2,1,0:T(8,128)S(1)}, f32[19,8,16,128]{3,2,1,0:T(8,128)}, u32[]{:S(2)}) copy-start(f32[19,8,16,128]{3,2,1,0:T(8,128)} %later_any.3) | copy-start | bytes 3735556
  0.7 19.6 %copy-start = (f32[19,8,16,128]{3,2,1,0:T(8,128)S(1)}, f32[19,8,16,128]{3,2,1,0:T(8,128)}, u32[]{:S(2)}) copy-start(f32[19,8,16,128]{3,2,1,0:T(8,128)} %fwd.3) | copy-start | bytes 3735556
  4.2 17.4 %collective-permute-start = (f32[53,8,128]{2,1,0:T(8,128)}, f32[53,8,128]{2,1,0:T(8,128)S(1)}, u32[]{:S(2)}, u32[]{:S(2)}) collective-permute-start(f32[53,8,128]{2,1,0:T(8,128)} %get-tuple-element.22), channel_id=1, source_target_pairs={{0,15},{1,2},{2,1},{3,4},{4,3},{5,6},{6,5},{7,8},{8,7},{9,10},{10,... | collective-permute-start | bytes 651272 | tf_op jit(solution)/shard_map/ppermute | solution.py:753
  16.2 5.3 %collective-permute-start.1 = (f32[53,8,128]{2,1,0:T(8,128)}, f32[53,8,128]{2,1,0:T(8,128)S(1)}, u32[]{:S(2)}, u32[]{:S(2)}) collective-permute-start(f32[53,8,128]{2,1,0:T(8,128)} %get-tuple-element.23), channel_id=1, source_target_pairs={{0,1},{1,0},{2,3},{3,2},{4,5},{5,4},{6,7},{7,6},{8,9},{9,8},{10,11... | collective-permute-start | bytes 651272 | tf_op jit(solution)/shard_map/ppermute | solution.py:753
  20.3 23.9 %copy-start.4 = (s32[8,16,128]{2,1,0:T(8,128)S(1)}, s32[8,16,128]{2,1,0:T(8,128)}, u32[]{:S(2)}) copy-start(s32[8,16,128]{2,1,0:T(8,128)} %region.1) | copy-start | bytes 196612
  21.9 21.5 %collective-permute-start.2 = (f32[1096,128]{1,0:T(8,128)S(1)}, f32[1096,128]{1,0:T(8,128)S(1)}, u32[]{:S(2)}, u32[]{:S(2)}) collective-permute-start(f32[1096,128]{1,0:T(8,128)S(1)} %get-tuple-element.24), channel_id=1, source_target_pairs={{0,16},{16,32},{32,48},{48,64},{64,80},{80,96},{96,112},{112,128},... | collective-permute-start | bytes 1683464 | tf_op jit(solution)/shard_map/ppermute | solution.py:746
  25.3 19.0 %collective-permute-start.3 = (f32[1096,128]{1,0:T(8,128)S(1)}, f32[1096,128]{1,0:T(8,128)S(1)}, u32[]{:S(2)}, u32[]{:S(2)}) collective-permute-start(f32[1096,128]{1,0:T(8,128)S(1)} %get-tuple-element.25), channel_id=1, source_target_pairs={{16,0},{32,16},{48,32},{64,48},{80,64},{96,80},{112,96},{128,112},... | collective-permute-start | bytes 1683464 | tf_op jit(solution)/shard_map/ppermute | solution.py:746
  51.2 10.0 %collective-permute-start.4 = (f32[56,128]{1,0:T(8,128)S(1)}, f32[56,128]{1,0:T(8,128)S(1)}, u32[]{:S(2)}, u32[]{:S(2)}) collective-permute-start(f32[56,128]{1,0:T(8,128)S(1)} %get-tuple-element.28), channel_id=1, source_target_pairs={{0,16},{16,32},{32,48},{48,64},{64,80},{80,96},{96,112},{112,128},... | collective-permute-start | bytes 86024 | tf_op jit(solution)/shard_map/ppermute | solution.py:746
  53.1 9.0 %collective-permute-start.5 = (f32[56,128]{1,0:T(8,128)S(1)}, f32[56,128]{1,0:T(8,128)S(1)}, u32[]{:S(2)}, u32[]{:S(2)}) collective-permute-start(f32[56,128]{1,0:T(8,128)S(1)} %get-tuple-element.29), channel_id=1, source_target_pairs={{16,0},{32,16},{48,32},{64,48},{80,64},{96,80},{112,96},{128,112},... | collective-permute-start | bytes 86024 | tf_op jit(solution)/shard_map/ppermute | solution.py:746
  62.8 32.7 %all-to-all-start = ((f32[256,1,128]{2,1,0:T(1,128)}), f32[256,1,128]{2,1,0:T(1,128)S(1)}, u32[]{:S(2)}, u32[]{:S(2)}) async-start(f32[256,1,128]{2,1,0:T(1,128)} %bitcast.1), calls=%async_computation | async-start | bytes 262144 | tf_op jit(solution)/shard_map/all_to_all | solution.py:759
  81.4 11.6 %collective-permute-start.6 = (f32[3,16,128]{2,1,0:T(8,128)S(1)}, f32[3,16,128]{2,1,0:T(8,128)S(1)}, u32[]{:S(2)}, u32[]{:S(2)}) collective-permute-start(f32[3,16,128]{2,1,0:T(8,128)S(1)} %get-tuple-element.31), channel_id=1, source_target_pairs={{0,15},{1,2},{2,1},{3,4},{4,3},{5,6},{6,5},{7,8},{8,7},{9,10},{10,... | collective-permute-start | bytes 73736 | tf_op jit(solution)/shard_map/ppermute | solution.py:753
  88.8 5.0 %collective-permute-start.7 = (f32[3,16,128]{2,1,0:T(8,128)S(1)}, f32[3,16,128]{2,1,0:T(8,128)S(1)}, u32[]{:S(2)}, u32[]{:S(2)}) collective-permute-start(f32[3,16,128]{2,1,0:T(8,128)S(1)} %get-tuple-element.32), channel_id=1, source_target_pairs={{0,1},{1,0},{2,3},{3,2},{4,5},{5,4},{6,7},{7,6},{8,9},{9,8},{10,11... | collective-permute-start | bytes 73736 | tf_op jit(solution)/shard_map/ppermute | solution.py:753
